TPU v7x, 32 devices: a whole 2x2x4 slice. The times are simulated.
32 devices in a mesh: row: 4 (over y, x), col: 8 (over z, core).
Axes of the slice: x: 2, y: 2, z: 4, core: 2. Of those that a mesh axis runs over, the one named last changes fastest.
Arguments:
- left_blocks: float32 [4, 8, 42, 128, 128], P('row', 'col'), may hold values from -1 to 1
- right_blocks: float32 [4, 8, 42, 128, 128], P('row', 'col'), may hold values from -1 to 1
- left_send: int32 [4, 8, 8, 8], P('row', 'col'), may hold values from -1 to 41, as said below
- left_place: int32 [4, 8, 2, 32], P('row', 'col'), may hold values from -1 to 63, as said below
- right_send: int32 [4, 8, 4, 16], P('row', 'col'), may hold values from -1 to 41, as said below
- right_place: int32 [4, 8, 2, 32], P('row', 'col'), may hold values from -1 to 63, as said below
- triples: int32 [4, 8, 2, 2, 3, 384], P('row', 'col'), may hold values from -1 to 31, as said below
Outputs:
- product_blocks: float32 [4, 8, 42, 128, 128], P('row', 'col')
Inputs may be any that keep to these rules, and one draw needn't show every extreme that they name: `left_send`: each owner's 42 local blocks are each named exactly once over all peers and bucket slots; the other slots are -1. In every grid row one device receives a full bucket of 8 blocks from every owner. `left_place`: every received live position is named exactly once over a device's two panels, and no empty position is named. `right_send`: each owner's 42 local blocks are each named exactly once over all peers and bucket slots; the other slots are -1. In every grid column one device receives a full bucket of 16 blocks from every owner. `right_place`: every received live position is named exactly once over a device's two panels, and no empty position is named. For each image and stop the live triples come first and the rest are -1 in all three entries; some image and stop has 384 live triples.
All inputs are finite; a program needn't handle non-finite values.
Results may differ from a plain program's by a relative error of at most 0.0003.
Values sent between devices are 32-bit elements; how exact they have to be, the bound alone decides.
No kernel may reach another device: no remote copies, remote signals or barrier semaphores. Data moves between devices by JAX's collectives and lax.ppermute only.
A program may use at most 128 MiB of HBM per device.

v0:
```python
import jax
import jax.numpy as jnp
from jax import lax
from jax.sharding import PartitionSpec as P


def shifted(value, axis, steps):
    count = lax.axis_size(axis)
    pairs = [(source, (source + steps) % count) for source in range(count)]
    return lax.ppermute(value, axis, pairs)


def pick_rows(blocks, index):
    safe = jnp.clip(index, 0, blocks.shape[0] - 1)
    return jnp.where((index >= 0)[..., None, None], blocks[safe], jnp.zeros((), blocks.dtype))


def multiply(left_panel, right_panel, lists, running):
    pair_count = lists.shape[-1]
    group_size = 128
    shaped = jnp.transpose(lists.reshape(3, pair_count // group_size, group_size), (1, 0, 2))

    def advance(current, triple_group):
        present = triple_group[0] >= 0
        left_pick = left_panel[jnp.where(present, triple_group[0], 0)]
        right_pick = right_panel[jnp.where(present, triple_group[1], 0)]
        product = jnp.einsum("pik,pkj->pij", left_pick, right_pick, precision=lax.Precision.HIGHEST)
        product = jnp.where(present[:, None, None], product, 0.0)
        return (current.at[jnp.where(present, triple_group[2], 0)].add(product), None)

    result, _ = lax.scan(advance, running, shaped)
    return result


def local(left_blocks, right_blocks, left_send, left_place, right_send, right_place, triples):
    grid_rows = lax.axis_size("row")
    grid_cols = lax.axis_size("col")
    left_own = left_blocks[0, 0]
    own_count = left_own.shape[0]
    block_size = left_own.shape[-1]
    left_list = left_send[0, 0]
    per_peer = left_list.shape[1]
    left_positions = left_place[0, 0]
    panel_slots = left_positions.shape[1]
    right_buckets = pick_rows(right_blocks[0, 0], right_send[0, 0].reshape(-1))
    right_recv = lax.all_to_all(right_buckets, "row", split_axis=0, concat_axis=0, tiled=True)
    right_first = pick_rows(right_recv, right_place[0, 0])
    left_buckets = pick_rows(left_own, left_list.reshape(-1))
    left_recv = lax.all_to_all(left_buckets, "col", split_axis=0, concat_axis=0, tiled=True)
    left_first = pick_rows(left_recv, left_positions)
    left_second = shifted(left_first, "col", -1)
    right_moved = shifted(right_first, "row", -1)
    right_second = jnp.where(lax.axis_index("row") == grid_rows - 1, right_moved[::-1], right_moved)
    lists = triples[0, 0]
    panels = []
    for image_slot in range(2):
        running = jnp.zeros((panel_slots, block_size, block_size), jnp.float32)
        running = multiply(
            left_first[image_slot], right_first[image_slot], lists[image_slot, 0], running
        )
        running = multiply(
            left_second[image_slot], right_second[image_slot], lists[image_slot, 1], running
        )
        panels.append(running)
    product_panel = jnp.stack(panels)
    flat_positions = left_positions.reshape(-1)
    target = jnp.where(flat_positions >= 0, flat_positions, grid_cols * per_peer)
    buckets = jnp.zeros((grid_cols * per_peer, block_size, block_size), jnp.float32)
    buckets = buckets.at[target].set(product_panel.reshape(-1, block_size, block_size), mode="drop")
    returned = lax.all_to_all(buckets, "col", split_axis=0, concat_axis=0, tiled=True)
    flat_list = left_list.reshape(-1)
    own_slot = jnp.where(flat_list >= 0, flat_list, own_count)
    result = jnp.zeros((own_count, block_size, block_size), jnp.float32)
    result = result.at[own_slot].set(returned, mode="drop")
    return result[None, None]


def solution(mesh):
    placed = (
        P("row", "col", None, None, None),
        P("row", "col", None, None, None),
        P("row", "col", None, None),
        P("row", "col", None, None),
        P("row", "col", None, None),
        P("row", "col", None, None),
        P("row", "col", None, None, None, None),
    )
    return jax.shard_map(
        local,
        mesh=mesh,
        in_specs=placed,
        out_specs=P("row", "col", None, None, None),
        check_vma=False,
    )
```

profile of v0, /device:TPU:0, one launch (start us, length us, event | category | flops | bytes accessed | tf_op | source)
XLA Modules:
  0.0 907.4 jit_solution(3860516581727413831)
XLA Ops:
  22.4 40.7 %all-to-all-done.1 = f32[64,128,128]{2,1,0:T(8,128)} async-done(((f32[64,128,128]{2,1,0:T(8,128)}), f32[64,128,128]{2,1,0:T(8,128)}, u32[]{:S(2)}, u32[]{:S(2)}) %all-to-all-start.1) | async-done | bytes 4194336 | tf_op jit(solution)/shard_map/all_to_all | solution.py:46
  86.0 76.3 %all-to-all-done = f32[64,128,128]{2,1,0:T(8,128)} async-done(((f32[64,128,128]{2,1,0:T(8,128)}), f32[64,128,128]{2,1,0:T(8,128)}, u32[]{:S(2)}, u32[]{:S(2)}) %all-to-all-start) | async-done | bytes 4194336 | tf_op jit(solution)/shard_map/all_to_all | solution.py:49
  177.6 130.5 %while.40 = (s32[]{:T(128)}, f32[32,128,128]{2,1,0:T(8,128)S(1)}, s32[3,3,128]{2,0,1:T(4,128)S(1)}, f32[32,128,128]{2,1,0:T(8,128)}, f32[32,128,128]{2,1,0:T(8,128)}, /*index=5*/s32[]{:T(128)}, s32[]{:T(128)}, s32[]{}, s32[]{}) while((s32[]{:T(128)}, f32[32,128,128]{2,1,0:T(8,128)S(1)}, s32[3,3,128]{2,0,1:T(4,128)S(1)}, ...), condition=%wide.region_2.3_spmd, body=%wide.region_0.2_spmd.sunk | while | flops 3225423616 | bytes 83900800 | solution.py:31
  189.4 14.6 %broadcast_select_fusion.12 = f32[128,128,128]{2,1,0:T(8,128)} fusion(pred[128]{0:T(512)(128)(4,1)S(1)} %compare_bitcast_fusion.10, f32[128,128,128]{2,1,0:T(8,128)} %gather_fusion, f32[128,128,128]{2,1,0:T(8,128)} %gather_fusion.1), kind=kOutput, calls=%fused_computation.18.clone.1 | convolution fusion | flops 3223322624 | bytes 25165952 | tf_op jit(solution)/shard_map/while/body/eval_jaxpr/pik,pkj->pij/dot_general | solution.py:27
  204.0 17.0 %scatter_fusion = f32[32,128,128]{2,1,0:T(8,128)S(1)} fusion(f32[32,128,128]{2,1,0:T(8,128)S(1)} %get-tuple-element.439, s32[128]{0:T(128)S(1)} %get-tuple-element.340, f32[128,128,128]{2,1,0:T(8,128)} %broadcast_select_fusion.12), kind=kCustom, calls=%fused_computation.12.clone.1 | custom fusion | flops 2097152 | bytes 25166336 | tf_op jit(solution)/shard_map/while/body/eval_jaxpr/scatter-add | solution.py:29
  232.9 14.6 %broadcast_select_fusion.12 = f32[128,128,128]{2,1,0:T(8,128)} fusion(pred[128]{0:T(512)(128)(4,1)S(1)} %compare_bitcast_fusion.10, f32[128,128,128]{2,1,0:T(8,128)} %gather_fusion, f32[128,128,128]{2,1,0:T(8,128)} %gather_fusion.1), kind=kOutput, calls=%fused_computation.18.clone.1 | convolution fusion | flops 3223322624 | bytes 25165952 | tf_op jit(solution)/shard_map/while/body/eval_jaxpr/pik,pkj->pij/dot_general | solution.py:27
  247.5 17.1 %scatter_fusion = f32[32,128,128]{2,1,0:T(8,128)S(1)} fusion(f32[32,128,128]{2,1,0:T(8,128)S(1)} %get-tuple-element.439, s32[128]{0:T(128)S(1)} %get-tuple-element.340, f32[128,128,128]{2,1,0:T(8,128)} %broadcast_select_fusion.12), kind=kCustom, calls=%fused_computation.12.clone.1 | custom fusion | flops 2097152 | bytes 25166336 | tf_op jit(solution)/shard_map/while/body/eval_jaxpr/scatter-add | solution.py:29
  276.5 14.6 %broadcast_select_fusion.12 = f32[128,128,128]{2,1,0:T(8,128)} fusion(pred[128]{0:T(512)(128)(4,1)S(1)} %compare_bitcast_fusion.10, f32[128,128,128]{2,1,0:T(8,128)} %gather_fusion, f32[128,128,128]{2,1,0:T(8,128)} %gather_fusion.1), kind=kOutput, calls=%fused_computation.18.clone.1 | convolution fusion | flops 3223322624 | bytes 25165952 | tf_op jit(solution)/shard_map/while/body/eval_jaxpr/pik,pkj->pij/dot_general | solution.py:27
  291.0 17.0 %scatter_fusion = f32[32,128,128]{2,1,0:T(8,128)S(1)} fusion(f32[32,128,128]{2,1,0:T(8,128)S(1)} %get-tuple-element.439, s32[128]{0:T(128)S(1)} %get-tuple-element.340, f32[128,128,128]{2,1,0:T(8,128)} %broadcast_select_fusion.12), kind=kCustom, calls=%fused_computation.12.clone.1 | custom fusion | flops 2097152 | bytes 25166336 | tf_op jit(solution)/shard_map/while/body/eval_jaxpr/scatter-add | solution.py:29
  316.2 158.0 %while.42 = (s32[]{:T(128)}, f32[32,128,128]{2,1,0:T(8,128)}, s32[3,3,128]{2,0,1:T(4,128)S(1)}, f32[32,128,128]{2,1,0:T(8,128)}, f32[32,128,128]{2,1,0:T(8,128)}, /*index=5*/s32[]{:T(128)}, s32[]{:T(128)}, s32[]{}, s32[]{}) while((s32[]{:T(128)}, f32[32,128,128]{2,1,0:T(8,128)}, s32[3,3,128]{2,0,1:T(4,128)S(1)}, f32[32,128,128]{2,1,0:T(8,128)}, ...), condition=%wide.region_8.9_spmd, body=%wide.region_6.8_spmd.sunk | while | flops 3225423616 | bytes 83900800 | solution.py:31
  328.0 14.6 %broadcast_select_fusion.14 = f32[128,128,128]{2,1,0:T(8,128)} fusion(pred[128]{0:T(512)(128)(4,1)S(1)} %compare_bitcast_fusion.12, f32[128,128,128]{2,1,0:T(8,128)} %gather_fusion.4, f32[128,128,128]{2,1,0:T(8,128)} %gather_fusion.5), kind=kOutput, calls=%fused_computation.54.clone.1 | convolution fusion | flops 3223322624 | bytes 25165952 | tf_op jit(solution)/shard_map/while/body/eval_jaxpr/pik,pkj->pij/dot_general | solution.py:27
  342.6 26.0 %scatter_fusion.2 = f32[32,128,128]{2,1,0:T(8,128)} fusion(f32[32,128,128]{2,1,0:T(8,128)} %get-tuple-element.385, s32[128]{0:T(128)S(1)} %get-tuple-element.360, f32[128,128,128]{2,1,0:T(8,128)} %broadcast_select_fusion.14), kind=kCustom, calls=%fused_computation.14.clone.1 | custom fusion | flops 2097152 | bytes 25166336 | tf_op jit(solution)/shard_map/while/body/eval_jaxpr/scatter-add | solution.py:29
  380.5 14.6 %broadcast_select_fusion.14 = f32[128,128,128]{2,1,0:T(8,128)} fusion(pred[128]{0:T(512)(128)(4,1)S(1)} %compare_bitcast_fusion.12, f32[128,128,128]{2,1,0:T(8,128)} %gather_fusion.4, f32[128,128,128]{2,1,0:T(8,128)} %gather_fusion.5), kind=kOutput, calls=%fused_computation.54.clone.1 | convolution fusion | flops 3223322624 | bytes 25165952 | tf_op jit(solution)/shard_map/while/body/eval_jaxpr/pik,pkj->pij/dot_general | solution.py:27
  395.1 26.1 %scatter_fusion.2 = f32[32,128,128]{2,1,0:T(8,128)} fusion(f32[32,128,128]{2,1,0:T(8,128)} %get-tuple-element.385, s32[128]{0:T(128)S(1)} %get-tuple-element.360, f32[128,128,128]{2,1,0:T(8,128)} %broadcast_select_fusion.14), kind=kCustom, calls=%fused_computation.14.clone.1 | custom fusion | flops 2097152 | bytes 25166336 | tf_op jit(solution)/shard_map/while/body/eval_jaxpr/scatter-add | solution.py:29
  433.0 14.6 %broadcast_select_fusion.14 = f32[128,128,128]{2,1,0:T(8,128)} fusion(pred[128]{0:T(512)(128)(4,1)S(1)} %compare_bitcast_fusion.12, f32[128,128,128]{2,1,0:T(8,128)} %gather_fusion.4, f32[128,128,128]{2,1,0:T(8,128)} %gather_fusion.5), kind=kOutput, calls=%fused_computation.54.clone.1 | convolution fusion | flops 3223322624 | bytes 25165952 | tf_op jit(solution)/shard_map/while/body/eval_jaxpr/pik,pkj->pij/dot_general | solution.py:27
  447.6 26.6 %scatter_fusion.2 = f32[32,128,128]{2,1,0:T(8,128)} fusion(f32[32,128,128]{2,1,0:T(8,128)} %get-tuple-element.385, s32[128]{0:T(128)S(1)} %get-tuple-element.360, f32[128,128,128]{2,1,0:T(8,128)} %broadcast_select_fusion.14), kind=kCustom, calls=%fused_computation.14.clone.1 | custom fusion | flops 2097152 | bytes 25166336 | tf_op jit(solution)/shard_map/while/body/eval_jaxpr/scatter-add | solution.py:29
  478.9 134.4 %while.41 = (s32[]{:T(128)}, f32[32,128,128]{2,1,0:T(8,128)S(1)}, s32[3,3,128]{2,0,1:T(4,128)}, f32[32,128,128]{2,1,0:T(8,128)}, f32[32,128,128]{2,1,0:T(8,128)}, /*index=5*/s32[]{:T(128)}, s32[]{:T(128)}, s32[]{}, s32[]{}) while((s32[]{:T(128)}, f32[32,128,128]{2,1,0:T(8,128)S(1)}, s32[3,3,128]{2,0,1:T(4,128)}, f32[32,128,128]{2,1,0:T(8,128)}, ...), condition=%wide.region_5.6_spmd, body=%wide.region_3.5_spmd.sunk | while | flops 3225423616 | bytes 83900800 | solution.py:31
  492.1 14.6 %broadcast_select_fusion.13 = f32[128,128,128]{2,1,0:T(8,128)} fusion(pred[128]{0:T(512)(128)(4,1)S(1)} %compare_bitcast_fusion.11, f32[128,128,128]{2,1,0:T(8,128)} %gather_fusion.2, f32[128,128,128]{2,1,0:T(8,128)} %gather_fusion.3), kind=kOutput, calls=%fused_computation.36.clone.1 | convolution fusion | flops 3223322624 | bytes 25165952 | tf_op jit(solution)/shard_map/while/body/eval_jaxpr/pik,pkj->pij/dot_general | solution.py:27
  506.6 17.1 %scatter_fusion.1 = f32[32,128,128]{2,1,0:T(8,128)S(1)} fusion(f32[32,128,128]{2,1,0:T(8,128)S(1)} %get-tuple-element.466, s32[128]{0:T(128)S(1)} %get-tuple-element.350, f32[128,128,128]{2,1,0:T(8,128)} %broadcast_select_fusion.13), kind=kCustom, calls=%fused_computation.13.clone.1 | custom fusion | flops 2097152 | bytes 25166336 | tf_op jit(solution)/shard_map/while/body/eval_jaxpr/scatter-add | solution.py:29
  536.9 14.6 %broadcast_select_fusion.13 = f32[128,128,128]{2,1,0:T(8,128)} fusion(pred[128]{0:T(512)(128)(4,1)S(1)} %compare_bitcast_fusion.11, f32[128,128,128]{2,1,0:T(8,128)} %gather_fusion.2, f32[128,128,128]{2,1,0:T(8,128)} %gather_fusion.3), kind=kOutput, calls=%fused_computation.36.clone.1 | convolution fusion | flops 3223322624 | bytes 25165952 | tf_op jit(solution)/shard_map/while/body/eval_jaxpr/pik,pkj->pij/dot_general | solution.py:27
  551.5 17.0 %scatter_fusion.1 = f32[32,128,128]{2,1,0:T(8,128)S(1)} fusion(f32[32,128,128]{2,1,0:T(8,128)S(1)} %get-tuple-element.466, s32[128]{0:T(128)S(1)} %get-tuple-element.350, f32[128,128,128]{2,1,0:T(8,128)} %broadcast_select_fusion.13), kind=kCustom, calls=%fused_computation.13.clone.1 | custom fusion | flops 2097152 | bytes 25166336 | tf_op jit(solution)/shard_map/while/body/eval_jaxpr/scatter-add | solution.py:29
  581.7 14.6 %broadcast_select_fusion.13 = f32[128,128,128]{2,1,0:T(8,128)} fusion(pred[128]{0:T(512)(128)(4,1)S(1)} %compare_bitcast_fusion.11, f32[128,128,128]{2,1,0:T(8,128)} %gather_fusion.2, f32[128,128,128]{2,1,0:T(8,128)} %gather_fusion.3), kind=kOutput, calls=%fused_computation.36.clone.1 | convolution fusion | flops 3223322624 | bytes 25165952 | tf_op jit(solution)/shard_map/while/body/eval_jaxpr/pik,pkj->pij/dot_general | solution.py:27
  596.3 17.0 %scatter_fusion.1 = f32[32,128,128]{2,1,0:T(8,128)S(1)} fusion(f32[32,128,128]{2,1,0:T(8,128)S(1)} %get-tuple-element.466, s32[128]{0:T(128)S(1)} %get-tuple-element.350, f32[128,128,128]{2,1,0:T(8,128)} %broadcast_select_fusion.13), kind=kCustom, calls=%fused_computation.13.clone.1 | custom fusion | flops 2097152 | bytes 25166336 | tf_op jit(solution)/shard_map/while/body/eval_jaxpr/scatter-add | solution.py:29
  613.3 163.9 %while.43 = (s32[]{:T(128)}, f32[32,128,128]{2,1,0:T(8,128)}, s32[3,3,128]{2,0,1:T(4,128)}, f32[32,128,128]{2,1,0:T(8,128)}, f32[32,128,128]{2,1,0:T(8,128)}, /*index=5*/s32[]{:T(128)}, s32[]{:T(128)}, s32[]{}, s32[]{}) while((s32[]{:T(128)}, f32[32,128,128]{2,1,0:T(8,128)}, s32[3,3,128]{2,0,1:T(4,128)}, f32[32,128,128]{2,1,0:T(8,128)}, ...), condition=%wide.region_11.12_spmd, body=%wide.region_9.11_spmd.sunk | while | flops 3225423616 | bytes 83900800 | solution.py:31
  626.7 14.6 %broadcast_select_fusion.15 = f32[128,128,128]{2,1,0:T(8,128)} fusion(pred[128]{0:T(512)(128)(4,1)S(1)} %compare_bitcast_fusion.13, f32[128,128,128]{2,1,0:T(8,128)} %gather_fusion.6, f32[128,128,128]{2,1,0:T(8,128)} %gather_fusion.7), kind=kOutput, calls=%fused_computation.72.clone.1 | convolution fusion | flops 3223322624 | bytes 25165952 | tf_op jit(solution)/shard_map/while/body/eval_jaxpr/pik,pkj->pij/dot_general | solution.py:27
  641.3 26.0 %scatter_fusion.3 = f32[32,128,128]{2,1,0:T(8,128)} fusion(f32[32,128,128]{2,1,0:T(8,128)} %get-tuple-element.412, s32[128]{0:T(128)S(1)} %get-tuple-element.370, f32[128,128,128]{2,1,0:T(8,128)} %broadcast_select_fusion.15), kind=kCustom, calls=%fused_computation.15.clone.1 | custom fusion | flops 2097152 | bytes 25166336 | tf_op jit(solution)/shard_map/while/body/eval_jaxpr/scatter-add | solution.py:29
  680.5 14.6 %broadcast_select_fusion.15 = f32[128,128,128]{2,1,0:T(8,128)} fusion(pred[128]{0:T(512)(128)(4,1)S(1)} %compare_bitcast_fusion.13, f32[128,128,128]{2,1,0:T(8,128)} %gather_fusion.6, f32[128,128,128]{2,1,0:T(8,128)} %gather_fusion.7), kind=kOutput, calls=%fused_computation.72.clone.1 | convolution fusion | flops 3223322624 | bytes 25165952 | tf_op jit(solution)/shard_map/while/body/eval_jaxpr/pik,pkj->pij/dot_general | solution.py:27
  695.1 25.9 %scatter_fusion.3 = f32[32,128,128]{2,1,0:T(8,128)} fusion(f32[32,128,128]{2,1,0:T(8,128)} %get-tuple-element.412, s32[128]{0:T(128)S(1)} %get-tuple-element.370, f32[128,128,128]{2,1,0:T(8,128)} %broadcast_select_fusion.15), kind=kCustom, calls=%fused_computation.15.clone.1 | custom fusion | flops 2097152 | bytes 25166336 | tf_op jit(solution)/shard_map/while/body/eval_jaxpr/scatter-add | solution.py:29
  734.1 14.6 %broadcast_select_fusion.15 = f32[128,128,128]{2,1,0:T(8,128)} fusion(pred[128]{0:T(512)(128)(4,1)S(1)} %compare_bitcast_fusion.13, f32[128,128,128]{2,1,0:T(8,128)} %gather_fusion.6, f32[128,128,128]{2,1,0:T(8,128)} %gather_fusion.7), kind=kOutput, calls=%fused_computation.72.clone.1 | convolution fusion | flops 3223322624 | bytes 25165952 | tf_op jit(solution)/shard_map/while/body/eval_jaxpr/pik,pkj->pij/dot_general | solution.py:27
  748.7 28.4 %scatter_fusion.3 = f32[32,128,128]{2,1,0:T(8,128)} fusion(f32[32,128,128]{2,1,0:T(8,128)} %get-tuple-element.412, s32[128]{0:T(128)S(1)} %get-tuple-element.370, f32[128,128,128]{2,1,0:T(8,128)} %broadcast_select_fusion.15), kind=kCustom, calls=%fused_computation.15.clone.1 | custom fusion | flops 2097152 | bytes 25166336 | tf_op jit(solution)/shard_map/while/body/eval_jaxpr/scatter-add | solution.py:29
  783.6 12.0 %scatter_fusion.4 = f32[64,128,128]{2,1,0:T(8,128)} fusion(f32[64,128,128]{2,1,0:T(8,128)} %broadcast_in_dim.127, s32[64]{0:T(128)S(1)} %copy-done.8, f32[64,128,128]{2,1,0:T(8,128)} %bitcast.260), kind=kCustom, calls=%fused_computation.16 | custom fusion | bytes 12583168 | tf_op jit(solution)/shard_map/scatter | solution.py:69
  795.6 98.6 %all_to_all.15 = f32[64,128,128]{2,1,0:T(8,128)} all-to-all(f32[64,128,128]{2,1,0:T(8,128)} %scatter_fusion.4), channel_id=1, replica_groups=mesh['row'=4,'col'=8] {'col'}, dimensions={0} | all-to-all | bytes 8388608 | tf_op jit(solution)/shard_map/all_to_all | solution.py:70
  (129 shorter events, 243.0 us)
Async XLA Ops:
  0.0 1.8 copy-start
  9.0 5.5 copy-start.4
  9.0 6.1 copy-start.2
  9.0 54.1 %all-to-all-start.1 = ((f32[64,128,128]{2,1,0:T(8,128)}), f32[64,128,128]{2,1,0:T(8,128)}, u32[]{:S(2)}, u32[]{:S(2)}) async-start(f32[64,128,128]{2,1,0:T(8,128)} %broadcast_select_fusion.6), calls=%async_computation.1 | async-start | bytes 8388608 | tf_op jit(solution)/shard_map/all_to_all | solution.py:46
  22.4 45.8 %copy-start.5 = (s32[1,1,2,32]{3,2,1,0:T(2,128)S(1)}, s32[1,1,2,32]{3,2,1,0:T(2,128)}, u32[]{:S(2)}) copy-start(s32[1,1,2,32]{3,2,1,0:T(2,128)} %param.18) | copy-start | bytes 772
  22.4 46.0 %copy-start.3 = (s32[1,1,2,2,3,384]{5,3,4,2,1,0:T(2,128)S(1)}, s32[1,1,2,2,3,384]{5,3,4,2,1,0:T(2,128)}, u32[]{:S(2)}) copy-start(s32[1,1,2,2,3,384]{5,3,4,2,1,0:T(2,128)} %param.21) | copy-start | bytes 55300
  22.4 46.0 %copy-start.6 = (s32[1,1,2,32]{3,2,1,0:T(2,128)S(1)}, s32[1,1,2,32]{3,2,1,0:T(2,128)}, u32[]{:S(2)}) copy-start(s32[1,1,2,32]{3,2,1,0:T(2,128)} %param.20) | copy-start | bytes 772
  63.1 99.2 %all-to-all-start = ((f32[64,128,128]{2,1,0:T(8,128)}), f32[64,128,128]{2,1,0:T(8,128)}, u32[]{:S(2)}, u32[]{:S(2)}) async-start(f32[64,128,128]{2,1,0:T(8,128)} %broadcast_select_fusion.7), calls=%async_computation | async-start | bytes 8388608 | tf_op jit(solution)/shard_map/all_to_all | solution.py:49
  79.9 228.2 %collective-permute-start.1 = (f32[2,32,128,128]{3,2,1,0:T(8,128)}, f32[2,32,128,128]{3,2,1,0:T(8,128)}, u32[]{:S(2)}, u32[]{:S(2)}) collective-permute-start(f32[2,32,128,128]{3,2,1,0:T(8,128)} %broadcast_select_fusion.4), channel_id=1, source_target_pairs={{0,24},{8,0},{16,8},{24,16},{1,25},{9,1},{17,9},{25,17},{2,26},{10... | collective-permute-start | bytes 12582920 | tf_op jit(solution)/shard_map/ppermute | solution.py:10
  171.7 302.5 %collective-permute-start = (f32[2,32,128,128]{3,2,1,0:T(8,128)}, f32[2,32,128,128]{3,2,1,0:T(8,128)}, u32[]{:S(2)}, u32[]{:S(2)}) collective-permute-start(f32[2,32,128,128]{3,2,1,0:T(8,128)} %broadcast_select_fusion.5), channel_id=1, source_target_pairs={{0,7},{1,0},{2,1},{3,2},{4,3},{5,4},{6,5},{7,6},{8,15},{9,8},{10,9... | collective-permute-start | bytes 12582920 | tf_op jit(solution)/shard_map/ppermute | solution.py:10
  781.2 2.5 copy-start.8
  795.6 100.5 %copy-start.7 = (s32[64]{0:T(128)S(1)}, s32[64]{0:T(128)}, u32[]{:S(2)}) copy-start(s32[64]{0:T(128)} %get-tuple-element.210) | copy-start | bytes 772
  894.2 13.2 %copy-start.1 = (f32[1,1,42,128,128]{4,3,2,1,0:T(8,128)S(1)}, f32[1,1,42,128,128]{4,3,2,1,0:T(8,128)}, u32[]{:S(2)}) copy-start(f32[1,1,42,128,128]{4,3,2,1,0:T(8,128)} %param.16) | copy-start | bytes 8257540
where the time goes:
time: 913 us; the launch traced here: 907 us
  other arithmetic  298 us (33%)
  local copies, waits for them, and re-layouts  205 us (22%)
  matrix products  175 us (19%)
  waiting for transfers between devices  117 us (13%)
  blocking collectives  98.6 us (11%)
  starting transfers between devices  12.9 us (1%)
    scatter-add x12, other arithmetic, advance(): current.at[jnp.where(present, triple_group[2], 0)].add(product)  261 us
    dot_general x12, matrix products, advance(): jnp.einsum('pik,pkj->pij', left_pick, right_pick, precision=lax.Precision...  175 us
    all_to_all x1, blocking collectives, local(): lax.all_to_all(buckets, 'col', split_axis=0, concat_axis=0, tiled=True)  98.6 us
    all_to_all x1, waiting for transfers between devices, local(): lax.all_to_all(left_buckets, 'col', split_axis=0, concat_axis=0, tiled=True)  76.3 us
    gather x12, local copies, waits for them, and re-layouts, advance(): left_pick = left_panel[jnp.where(present, triple_group[0], 0)]  70.9 us
    gather x12, local copies, waits for them, and re-layouts, advance(): right_pick = right_panel[jnp.where(present, triple_group[1], 0)]  70.6 us
    all_to_all x1, waiting for transfers between devices, local(): lax.all_to_all(right_buckets, 'row', split_axis=0, concat_axis=0, tiled=T...  40.7 us
  transfers between devices with their start and end apart: 4, of which 2 were waited for; matrix products, arithmetic and copies ran while one was open for 37% of the time, Pallas kernels for 0%

commit v1 on v0

v1 whole, which is shorter than its diff:
```python
import functools

import jax
import jax.numpy as jnp
from jax import lax
from jax.experimental import pallas as pl
from jax.experimental.pallas import tpu as pltpu
from jax.sharding import PartitionSpec as P


GROUP = 4
UNROLL = 4
SHIFT = 1024
ABSENT = -(1 << 24)
LATE = 1 << 10
SMEM = pl.BlockSpec(memory_space=pltpu.SMEM)
HBM = pl.BlockSpec(memory_space=pl.ANY)


def moved(value, axis, target, among=None):
    places = range(lax.axis_size(axis)) if among is None else among
    return lax.ppermute(value, axis, [(source, target(source)) for source in places])


def spread(piece, axis, masks):
    held = {0: piece}
    for mask in masks:
        for key, value in list(held.items()):
            held[mask ^ key] = moved(value, axis, lambda source: source ^ mask)
    return held


def plan_body(sizes, place_ref, triple_ref, left_ref, left_next_ref, table_ref, code_ref, slot_ref, bound_ref,
              block_ref, left_at, right_at, out_at, raw_code, raw_key, count_ref):
    rows, cols, own, per_left, per_right, panel, pairs = sizes
    row, col = place_ref[0], place_ref[1]
    half = per_left // 2
    middle, quarter = cols // 2, cols // 4
    slots = cols * per_left
    stride = panel + 1

    for stop in range(2):
        for image in range(2):
            left_at[(stop * 2 + image) * stride] = ABSENT
            right_at[(stop * 2 + image) * stride] = ABSENT
            out_at[image * stride] = 2 * slots

    def tables(index, _):
        image = index // panel
        slot = lax.rem(index, panel)
        for stop in range(2):
            entry = (stop * 2 + image) * stride + 1 + slot
            left = (left_ref if stop == 0 else left_next_ref)[image, slot]
            safe = jnp.maximum(left, 0)
            owner, within = safe // per_left, lax.rem(safe, per_left)
            if stop == 0:
                bucket = owner ^ col
                spot = (within // half) * (cols * half) + bucket * half + lax.rem(within, half)
                out_at[image * stride + 1 + slot] = jnp.where(left >= 0, spot, 2 * slots)
            else:
                after = lax.rem(col + 1, cols)
                bucket = owner ^ after
                crossing = lax.rem(after, middle) == 0
                turned = jnp.where(bucket < quarter, bucket, bucket + middle)
                turned = jnp.where(bucket < middle, turned, quarter + (owner ^ col))
                bucket = jnp.where(crossing, turned, bucket)
            late = bucket >= 3 * quarter
            early_at = 1 + (stop * 3 * quarter + bucket) * per_left + within
            late_at = 1 + (stop * quarter + bucket - 3 * quarter) * per_left + within + LATE
            left_at[entry] = jnp.where(left >= 0, jnp.where(late, late_at, early_at) * SHIFT, ABSENT)
            target = lax.rem(row + stop, rows)
            turned = jnp.where(row == rows - 1, 1 - image, image) if stop == 1 else image
            place = table_ref[target ^ row, rows * per_right + turned * panel + slot]
            safe = jnp.maximum(place, 0)
            source = (safe // per_right) ^ row
            block = table_ref[source, target * per_right + lax.rem(safe, per_right)]
            there = (place >= 0) & (block >= 0)
            right_at[entry] = jnp.where(there, stop * 2 * panel + index, ABSENT)
            block_ref[stop * 2 * panel + index] = jnp.where(there, source * own + block, 0)
        return 0

    lax.fori_loop(0, 2 * panel, tables, 0)

    def clear(index, _):
        count_ref[index] = 0
        return 0

    lax.fori_loop(0, 2 * slots + 1, clear, 0)
    total = jnp.int32(0)
    for stop in range(2):
        for image in range(2):
            base = (stop * 2 + image) * stride + 1

            def read(index, found):
                a = triple_ref[image, stop, 0, index]
                b = triple_ref[image, stop, 1, index]
                t = triple_ref[image, stop, 2, index]
                code = left_at[base + a] + right_at[base + b]
                spot = out_at[image * stride + 1 + t]
                live = (code >= 0) & (spot < slots)
                late = (code >= LATE * SHIFT).astype(jnp.int32)
                key = jnp.where(live, spot + late * slots, 2 * slots)
                raw_code[found] = code - late * (LATE * SHIFT)
                raw_key[found] = key
                count_ref[key] = count_ref[key] + 1
                return found + live.astype(jnp.int32)

            total = lax.fori_loop(0, pairs, read, total, unroll=4)

    def fill(index, _):
        code_ref[index] = 0
        return 0

    lax.fori_loop(0, code_ref.shape[0], fill, 0, unroll=16)

    def idle(index, _):
        slot_ref[index] = slots
        return 0

    lax.fori_loop(0, slot_ref.shape[0], idle, 0, unroll=16)

    def prefix(key, group):
        groups = (count_ref[key] + GROUP - 1) // GROUP

        def label(index, _):
            slot_ref[index] = lax.rem(key, slots)
            return 0

        lax.fori_loop(group, group + groups, label, 0)
        count_ref[key] = group * GROUP
        return group + groups

    done = jnp.int32(0)
    bound_ref[0] = 0
    for part, (low, high) in enumerate([(0, slots), (slots, slots + slots // 2), (slots + slots // 2, 2 * slots)]):
        done = lax.fori_loop(low, high, prefix, done)
        done = (done + UNROLL - 1) // UNROLL * UNROLL
        bound_ref[part + 1] = done // UNROLL

    def place(index, _):
        key = raw_key[index]
        spot = count_ref[key]
        code_ref[spot] = raw_code[index]
        count_ref[key] = spot + 1
        return 0

    lax.fori_loop(0, total, place, 0)


def make_plan(place, triples, left_place, left_next, table, sizes):
    _, cols, _, per_left, _, panel, pairs = sizes
    slots = cols * per_left
    groups = 4 * pairs // GROUP + 2 * slots + 3 * UNROLL
    groups = (groups + 31) // 32 * 32
    return pl.pallas_call(
        functools.partial(plan_body, sizes),
        out_shape=(
            jax.ShapeDtypeStruct((groups * GROUP,), jnp.int32),
            jax.ShapeDtypeStruct((groups,), jnp.int32),
            jax.ShapeDtypeStruct((4,), jnp.int32),
            jax.ShapeDtypeStruct((4 * panel,), jnp.int32),
        ),
        in_specs=[SMEM] * 5,
        out_specs=(SMEM,) * 4,
        scratch_shapes=[
            pltpu.SMEM((4 * (panel + 1),), jnp.int32),
            pltpu.SMEM((4 * (panel + 1),), jnp.int32),
            pltpu.SMEM((2 * (panel + 1),), jnp.int32),
            pltpu.SMEM((4 * pairs + 8,), jnp.int32),
            pltpu.SMEM((4 * pairs + 8,), jnp.int32),
            pltpu.SMEM((2 * slots + 8,), jnp.int32),
        ],
        cost_estimate=pl.CostEstimate(flops=40_000_000, bytes_accessed=60_000_000, transcendentals=0),
        name="plan",
    )(place, triples, left_place, left_next, table)


def halves(value):
    high = value.astype(jnp.bfloat16)
    return high, (value - high.astype(jnp.float32)).astype(jnp.bfloat16)


DEPTH = 8
CHUNK = 8


def split_body(bases, *refs):
    sources, (out_ref, raw, cut, in_sems, out_sems) = refs[: len(bases)], refs[-5:]
    size = raw.shape[-1]
    steps = []
    for source, base in zip(sources, bases):
        for start in range(0, source.shape[0], CHUNK):
            steps.append((source, start, min(CHUNK, source.shape[0] - start), base + start))

    def fetch(step):
        source, start, count, _ = steps[step]
        slot = step % DEPTH
        return pltpu.make_async_copy(source.at[pl.ds(start, count)], raw.at[slot, pl.ds(0, count)], in_sems.at[slot])

    def store(step):
        _, _, count, base = steps[step]
        slot = step % DEPTH
        return pltpu.make_async_copy(cut.at[slot, pl.ds(0, count)], out_ref.at[pl.ds(base, count)], out_sems.at[slot])

    for step in range(min(DEPTH, len(steps))):
        fetch(step).start()
    for step in range(len(steps)):
        slot = step % DEPTH
        fetch(step).wait()
        if step >= DEPTH:
            store(step - DEPTH).wait()

        def convert(index, _):
            high, low = halves(raw[slot, index])
            cut[slot, index, :, 0:size] = high
            cut[slot, index, :, size : 2 * size] = low
            return 0

        lax.fori_loop(0, steps[step][2], convert, 0)
        store(step).start()
        if step + DEPTH < len(steps):
            fetch(step + DEPTH).start()
    for step in range(max(0, len(steps) - DEPTH), len(steps)):
        store(step).wait()


def split(pieces, count, held=None):
    size = pieces[0][0].shape[-1]
    held = [] if held is None else [held]
    return pl.pallas_call(
        functools.partial(split_body, [base for _, base in pieces]),
        out_shape=jax.ShapeDtypeStruct((count, size, 2 * size), jnp.bfloat16),
        in_specs=[HBM] * (len(pieces) + len(held)),
        out_specs=HBM,
        input_output_aliases={len(pieces): 0} if held else {},
        scratch_shapes=[
            pltpu.VMEM((DEPTH, CHUNK, size, size), jnp.float32),
            pltpu.VMEM((DEPTH, CHUNK, size, 2 * size), jnp.bfloat16),
            pltpu.SemaphoreType.DMA((DEPTH,)),
            pltpu.SemaphoreType.DMA((DEPTH,)),
        ],
        cost_estimate=pl.CostEstimate(flops=0, bytes_accessed=2 * count * size * size * 4, transcendentals=0),
        name="split",
    )(*[piece for piece, _ in pieces], *held)


def multiply_body(late, part, kinds, sizes, place_ref, code_ref, slot_ref, bound_ref, block_ref, right_ref, *refs):
    _, cols, _, per_left, _, panel, _ = sizes
    slots = cols * per_left
    half = per_left // 2
    spots = slots // 2 if late else slots
    outs = cols if late else 1
    count = len(kinds) + sum(kinds)
    sources, before_ref, rest = refs[:count], refs[count] if late else None, refs[count + late :]
    out_refs, (lefts, rights, total, raw, left_sems, right_sem, total_sem, out_sem) = rest[:outs], rest[outs:]
    size = raw.shape[-1]
    first = part * spots
    crossing = lax.rem(place_ref[1] + 1, cols // 2) == 0

    def fetch(source, bucket):
        return pltpu.make_async_copy(source, raw.at[pl.ds(bucket * per_left, per_left)], left_sems.at[bucket])

    def gather(index, _):
        block = block_ref[index]
        pltpu.make_async_copy(right_ref.at[block], rights.at[index], right_sem).start()
        return 0

    offset = 0
    for bucket, two in enumerate(kinds):
        if two:

            @pl.when(jnp.logical_not(crossing))
            def _():
                fetch(sources[offset], bucket).start()

            @pl.when(crossing)
            def _():
                fetch(sources[offset + 1], bucket).start()

        else:
            fetch(sources[offset], bucket).start()
        offset += 1 + two
    lax.fori_loop(0, 4 * panel, gather, 0, unroll=4)
    if late:
        carried = pltpu.make_async_copy(before_ref.at[pl.ds(first, spots)], total.at[pl.ds(0, spots)], total_sem)
        carried.start()
        total[spots] = jnp.zeros(total.shape[1:], total.dtype)
    else:
        total[...] = jnp.zeros_like(total)
    lefts[0] = jnp.zeros(lefts.shape[1:], lefts.dtype)
    for bucket in range(len(kinds)):
        fetch(sources[0], bucket).wait()

        def convert(index, _):
            high, low = halves(raw[index])
            lefts[1 + index, :, 0:size] = high
            lefts[1 + index, :, size : 2 * size] = low
            return 0

        lax.fori_loop(bucket * per_left, (bucket + 1) * per_left, convert, 0, unroll=2)
    pltpu.make_async_copy(right_ref.at[pl.ds(0, 4 * panel)], rights, right_sem).wait()
    if late:
        carried.wait()

    def multiply(step, _):
        for lane in range(UNROLL):
            group = step * UNROLL + lane
            spot = jnp.minimum(slot_ref[group] - first, spots)
            parts_left, parts_right = [], []
            for index in range(GROUP):
                code = code_ref[group * GROUP + index]
                parts_left.append(lefts[code // SHIFT])
                block = rights[lax.rem(code, SHIFT)]
                parts_right += [block, block]
            product = jnp.dot(
                jnp.concatenate(parts_left, axis=1),
                jnp.concatenate(parts_right, axis=0),
                preferred_element_type=jnp.float32,
            )
            total[spot] += product[:, 0:size] + product[:, size : 2 * size]
        return 0

    chapter = 1 + part if late else 0
    lax.fori_loop(bound_ref[chapter], bound_ref[chapter + 1], multiply, 0)
    copies = []
    if late:
        for bucket in range(cols):
            copies.append(
                pltpu.make_async_copy(total.at[pl.ds(bucket * half, half)], out_refs[bucket], out_sem.at[bucket])
            )
    else:
        copies.append(pltpu.make_async_copy(total.at[pl.ds(0, slots)], out_refs[0], out_sem.at[0]))
    for entry in copies:
        entry.start()
    for entry in copies:
        entry.wait()


def multiplied(late, part, sizes, place, plan, rights, lefts, before=None):
    _, cols, _, per_left, _, panel, _ = sizes
    slots = cols * per_left
    spots = slots // 2 if late else slots
    size = rights.shape[1]
    if late:
        out_shape = [jax.ShapeDtypeStruct((per_left // 2, size, size), jnp.float32)] * cols
        out_specs = [HBM] * cols
    else:
        out_shape, out_specs = jax.ShapeDtypeStruct((slots, size, size), jnp.float32), HBM
    arrays = [array for entry in lefts for array in entry] + ([before] if late else [])
    return pl.pallas_call(
        functools.partial(multiply_body, late, part, [len(entry) - 1 for entry in lefts], sizes),
        out_shape=out_shape,
        in_specs=[SMEM] * 5 + [HBM] * (1 + len(arrays)),
        out_specs=out_specs,
        scratch_shapes=[
            pltpu.VMEM((len(lefts) * per_left + 1, size, 2 * size), jnp.bfloat16),
            pltpu.VMEM((4 * panel, size, 2 * size), jnp.bfloat16),
            pltpu.VMEM((spots + 1, size, size), jnp.float32),
            pltpu.VMEM((len(lefts) * per_left, size, size), jnp.float32),
            pltpu.SemaphoreType.DMA((len(lefts),)),
            pltpu.SemaphoreType.DMA,
            pltpu.SemaphoreType.DMA,
            pltpu.SemaphoreType.DMA((cols,)),
        ],
        cost_estimate=pl.CostEstimate(flops=0, bytes_accessed=4 * slots * size * size * 4, transcendentals=0),
        compiler_params=pltpu.CompilerParams(vmem_limit_bytes=40 * 1024 * 1024),
    )(place, *plan, rights, *arrays)


def collect_body(sizes, place_ref, list_ref, *refs):
    _, cols, _, per_left, _, _, _ = sizes
    half = per_left // 2
    sources, out_ref, whole, sem, out_sem = refs[: 2 * cols], *refs[2 * cols :]
    for part in range(2):
        for bucket in range(cols):
            for within in range(half):
                block = list_ref[place_ref[1] ^ bucket, part * half + within]

                @pl.when(block >= 0)
                def _():
                    pltpu.make_async_copy(sources[part * cols + bucket].at[within], whole.at[block], sem).start()

    pltpu.make_async_copy(out_ref, whole, sem).wait()
    result = pltpu.make_async_copy(whole, out_ref, out_sem)
    result.start()
    result.wait()


def collected(sizes, place, left_list, backs):
    own, size = sizes[2], backs[0].shape[-1]
    return pl.pallas_call(
        functools.partial(collect_body, sizes),
        out_shape=jax.ShapeDtypeStruct((own, size, size), jnp.float32),
        in_specs=[SMEM] * 2 + [HBM] * len(backs),
        out_specs=HBM,
        scratch_shapes=[
            pltpu.VMEM((own, size, size), jnp.float32),
            pltpu.SemaphoreType.DMA,
            pltpu.SemaphoreType.DMA,
        ],
        name="collect",
    )(place, left_list, *backs)


def local(left_blocks, right_blocks, left_send, left_place, right_send, right_place, triples):
    rows, cols = lax.axis_size("row"), lax.axis_size("col")
    row, col = lax.axis_index("row").astype(jnp.int32), lax.axis_index("col").astype(jnp.int32)
    place = jnp.stack([row, col])
    left_own, right_own = left_blocks[0, 0], right_blocks[0, 0]
    own = left_own.shape[0]
    left_list, right_list = left_send[0, 0], right_send[0, 0]
    positions = left_place[0, 0]
    per_left, per_right = left_list.shape[1], right_list.shape[1]
    panel, pairs = positions.shape[1], triples.shape[-1]
    sizes = (rows, cols, own, per_left, per_right, panel, pairs)
    middle, quarter = cols // 2, cols // 4
    back_one = lambda source: (source - 1) % cols

    masks = [1 << bit for bit in range((rows - 1).bit_length())]
    table_own = jnp.concatenate([right_list.reshape(-1), right_place[0, 0].reshape(-1)])
    tables = spread(table_own, "row", masks)
    table = jnp.stack([tables[mask] for mask in range(rows)])
    left_next = moved(positions, "col", back_one)

    cut = own // 2
    whole, low, high = {0: right_own}, {}, {}
    for mask in masks:
        whole[mask] = moved(right_own, "row", lambda source: source ^ mask)
        low[mask], high[mask] = whole[mask][:cut], whole[mask][cut:]
    for key in range(rows):
        if key not in whole:
            top, bottom = 1 << (key.bit_length() - 1), key & -key
            low[key] = moved(low[key ^ top], "row", lambda source: source ^ top)
            high[key] = moved(high[key ^ bottom], "row", lambda source: source ^ bottom)

    def bucket_for(peer):
        return left_own[jnp.clip(left_list[peer], 0, own - 1)]

    here = {0: bucket_for(col)}
    for mask in range(1, cols):
        here[mask] = moved(bucket_for(col ^ mask), "col", lambda source: source ^ mask)
    extra = {0: bucket_for(jnp.where(col < middle, middle, 0))}
    for mask in range(1, middle):
        extra[mask] = moved(
            extra[0], "col", lambda source: source ^ mask, [(middle - 1) ^ mask, (cols - 1) ^ mask]
        )
    there = {}
    for mask in range(cols):
        among = None if mask < middle else [source for source in range(cols) if source % middle != 0]
        there[mask] = moved(here[mask], "col", back_one, among)

    plan = make_plan(place, triples[0, 0], positions, left_next, table, sizes)
    rights = split([(whole[mask], mask * own) for mask in whole], rows * own)
    pieces = []
    for mask in range(rows):
        if mask not in whole:
            pieces += [(low[mask], mask * own), (high[mask], mask * own + cut)]
    rights = split(pieces, rows * own, rights)
    early = [(here[mask],) for mask in range(3 * quarter)]
    early += [(there[mask],) for mask in range(quarter)]
    early += [(there[mask], extra[mask - quarter]) for mask in range(quarter, 3 * quarter)]
    late = [(here[mask],) for mask in range(3 * quarter, cols)]
    late += [(there[mask], there[mask - middle]) for mask in range(3 * quarter, cols)]
    before = multiplied(0, 0, sizes, place, plan, rights, early)
    backs = []
    for part in range(2):
        product = multiplied(1, part, sizes, place, plan, rights, late, before)
        returned = {0: product[0]}
        for mask in list(range(middle, cols)) + list(range(1, middle)):
            returned[mask] = moved(product[mask], "col", lambda source: source ^ mask)
        backs += [returned[mask] for mask in range(cols)]
    return collected(sizes, place, left_list, backs)[None, None]


def solution(mesh):
    placed = (
        P("row", "col", None, None, None),
        P("row", "col", None, None, None),
        P("row", "col", None, None),
        P("row", "col", None, None),
        P("row", "col", None, None),
        P("row", "col", None, None),
        P("row", "col", None, None, None, None),
    )

    return jax.shard_map(
        local,
        mesh=mesh,
        in_specs=placed,
        out_specs=P("row", "col", None, None, None),
        check_vma=False,
    )
```

time: 913 us -> 380 us (0.42)
  the two profiles are of different devices: /device:TPU:0 before, /device:TPU:11 now
where the time goes in v1:
time: 380 us; the launch traced here: 379 us
  waiting for transfers between devices  170 us (45%)
  starting transfers between devices  91.9 us (24%)
  Pallas kernels  82.1 us (22%)
  local copies, waits for them, and re-layouts  32.4 us (9%)
    ppermute x40, waiting for transfers between devices, moved(): lax.ppermute(value, axis, [(source, target(source)) for source in places])  170 us
    ppermute x40, starting transfers between devices, moved(): lax.ppermute(value, axis, [(source, target(source)) for source in places])  91.9 us
    pallas_call x1, Pallas kernels, make_plan(): pl.pallas_call(functools.partial(plan_body, sizes), out_shape=(jax.ShapeD...  34.4 us
    pallas_call x3, Pallas kernels, multiplied(): pl.pallas_call(functools.partial(multiply_body, late, part, [len(entry) -...  34.3 us
    unnamed x79, local copies, waits for them, and re-layouts  14 us
    gather x9, local copies, waits for them, and re-layouts, bucket_for(): return left_own[jnp.clip(left_list[peer], 0, own - 1)]  11.7 us
    pallas_call x2, Pallas kernels, split(): pl.pallas_call(functools.partial(split_body, [base for _, base in pieces]...  9.32 us
  transfers between devices with their start and end apart: 40, of which 15 were waited for; matrix products, arithmetic and copies ran while one was open for 6% of the time, Pallas kernels for 18%

profile of v1, /device:TPU:11, one launch (start us, length us, event | category | flops | bytes accessed | tf_op | source)
XLA Modules:
  0.0 379.3 jit_solution(10336859946099676813)
XLA Ops:
  10.9 18.5 %collective-permute-done.left_next_ref = s32[2,32]{1,0:T(2,128)S(1)} collective-permute-done((s32[2,32]{1,0:T(2,128)}, s32[2,32]{1,0:T(2,128)S(1)}, u32[]{:S(2)}, u32[]{:S(2)}) %collective-permute-start) | collective-permute-done | bytes 288 | tf_op jit(solution)/shard_map/ppermute | solution.py:22
  30.0 30.9 %collective-permute-done.1 = s32[128]{0:T(128)S(1)} collective-permute-done((s32[128]{0:T(128)S(1)}, s32[128]{0:T(128)S(1)}, u32[]{:S(2)}, u32[]{:S(2)}) %collective-permute-start.1) | collective-permute-done | bytes 544 | tf_op jit(solution)/shard_map/ppermute | solution.py:22
  60.9 2.7 collective-permute-start.9
  74.1 13.7 %collective-permute-done.9.refs_1_ = f32[8,128,128]{2,1,0:T(8,128)} collective-permute-done((f32[8,128,128]{2,1,0:T(8,128)}, f32[8,128,128]{2,1,0:T(8,128)}, u32[]{:S(2)}, u32[]{:S(2)}) %collective-permute-start.9) | collective-permute-done | bytes 524320 | tf_op jit(solution)/shard_map/ppermute | solution.py:22
  88.1 2.8 collective-permute-start.18
  90.8 2.6 slice.26
  93.4 2.6 slice.27
  97.3 11.4 %collective-permute-done.14.refs_3_ = f32[8,128,128]{2,1,0:T(8,128)} collective-permute-done((f32[8,128,128]{2,1,0:T(8,128)}, f32[8,128,128]{2,1,0:T(8,128)}, u32[]{:S(2)}, u32[]{:S(2)}) %collective-permute-start.14) | collective-permute-done | bytes 524320 | tf_op jit(solution)/shard_map/ppermute | solution.py:22
  112.4 26.7 %collective-permute-done.18.refs_5_ = f32[8,128,128]{2,1,0:T(8,128)} collective-permute-done((f32[8,128,128]{2,1,0:T(8,128)}, f32[8,128,128]{2,1,0:T(8,128)}, u32[]{:S(2)}, u32[]{:S(2)}) %collective-permute-start.18) | collective-permute-done | bytes 524320 | tf_op jit(solution)/shard_map/ppermute | solution.py:22
  143.7 8.0 %collective-permute-done.23.refs_13_ = f32[8,128,128]{2,1,0:T(8,128)S(1)} collective-permute-done((f32[8,128,128]{2,1,0:T(8,128)}, f32[8,128,128]{2,1,0:T(8,128)S(1)}, u32[]{:S(2)}, u32[]{:S(2)}) %collective-permute-start.23) | collective-permute-done | bytes 524320 | tf_op jit(solution)/shard_map/ppermute | solution.py:22
  152.5 2.3 collective-permute-done.25.refs_15_
  157.8 3.5 collective-permute-done.15.refs_10_.refs_5_
  162.1 2.3 collective-permute-start.24
  164.4 15.0 %collective-permute-start.10 = (f32[8,128,128]{2,1,0:T(8,128)}, f32[8,128,128]{2,1,0:T(8,128)}, u32[]{:S(2)}, u32[]{:S(2)}) collective-permute-start(f32[8,128,128]{2,1,0:T(8,128)} %copy-done.3), channel_id=1, source_target_pairs={{1,0},{2,1},{3,2},{5,4},{6,5},{7,6},{9,8},{10,9},{11,10},{13,12},{... | collective-permute-start | bytes 1572872 | tf_op jit(solution)/shard_map/ppermute | solution.py:22
  183.5 34.4 %plan.1 = (s32[2176]{0:T(1024)}, s32[544]{0:T(1024)}, s32[4]{0:T(128)}, s32[128]{0:T(128)}) custom-call(s32[2]{0:T(128)} %pad_add_fusion.1.place_ref, s32[2,2,3,384]{3,2,1,0:T(4,128)} %bitcast.99, s32[2,32]{1,0:T(2,128)} %bitcast.105, s32[2,32]{1,0:T(2,128)} %copy-done.38, s32[4,128]{1,0:T(4,128)} %pad_add_fusion.table_ref), custom_call_target="tpu_custom_call" | custom-call | flops 40000000 | bytes 60000000 | tf_op jit(solution)/shard_map/plan/pallas_call | solution.py:155
  217.9 6.5 %split.2.refs_2_ = bf16[168,128,256]{2,1,0:T(8,128)(2,1)} custom-call(f32[42,128,128]{2,1,0:T(8,128)} %bitcast.98, f32[42,128,128]{2,1,0:T(8,128)} %collective-permute-done.4.refs_1_, f32[42,128,128]{2,1,0:T(8,128)} %collective-permute-done.6.refs_2_), custom_call_target="tpu_custom_call" | custom-call | bytes 22020096 | tf_op jit(solution)/shard_map/split/pallas_call | solution.py:230
  224.5 2.8 split.3.right_ref
  234.7 16.3 %shard_map.73.refs_6_ = f32[64,128,128]{2,1,0:T(8,128)S(1)} custom-call(s32[2]{0:T(128)S(1)} %copy-done.20, s32[2176]{0:T(1024)S(1)} %copy-done.18, s32[544]{0:T(1024)S(1)} %copy-done.19, s32[4]{0:T(128)S(1)} %copy-done.21, s32[128]{0:T(128)S(1)} %copy-done.22, bf16[168,128,256]{2,1,0:T(8,128)(2,1)} %split.3.right_ref, f32[8,128,128]{2,1,0:T(8,128)S(1)} %copy-done.6, ...), custom_call_target="tpu_custom_call" | custom-call | bytes 16777216 | tf_op jit(solution)/shard_map/pallas_call | solution.py:350
  251.0 9.0 %shard_map.74 = (f32[4,128,128]{2,1,0:T(8,128)S(1)}, f32[4,128,128]{2,1,0:T(8,128)S(1)}, f32[4,128,128]{2,1,0:T(8,128)S(1)}, f32[4,128,128]{2,1,0:T(8,128)S(1)},...) custom-call(s32[2]{0:T(128)S(1)} %copy-done.20, ...), custom_call_target="tpu_custom_call" | custom-call | bytes 16777216 | tf_op jit(solution)/shard_map/pallas_call | solution.py:350
  260.7 20.3 %collective-permute-start.26 = (f32[4,128,128]{2,1,0:T(8,128)S(1)}, f32[4,128,128]{2,1,0:T(8,128)S(1)}, u32[]{:S(2)}, u32[]{:S(2)}) collective-permute-start(f32[4,128,128]{2,1,0:T(8,128)S(1)} %get-tuple-element.30), channel_id=1, source_target_pairs={{0,1},{1,0},{2,3},{3,2},{4,5},{5,4},{6,7},{7,6},{8,9},{9,8},{10,11... | collective-permute-start | bytes 786440 | tf_op jit(solution)/shard_map/ppermute | solution.py:22
  282.6 2.8 collective-permute-start.30
  285.4 9.0 %shard_map.75 = (f32[4,128,128]{2,1,0:T(8,128)S(1)}, f32[4,128,128]{2,1,0:T(8,128)S(1)}, f32[4,128,128]{2,1,0:T(8,128)S(1)}, f32[4,128,128]{2,1,0:T(8,128)S(1)},...) custom-call(s32[2]{0:T(128)S(1)} %copy-done.20, ...), custom_call_target="tpu_custom_call" | custom-call | bytes 16777216 | tf_op jit(solution)/shard_map/pallas_call | solution.py:350
  295.1 3.5 collective-permute-start.32
  298.7 3.4 collective-permute-start.34
  302.1 17.2 %collective-permute-start.35 = (f32[4,128,128]{2,1,0:T(8,128)S(1)}, f32[4,128,128]{2,1,0:T(8,128)S(1)}, u32[]{:S(2)}, u32[]{:S(2)}) collective-permute-start(f32[4,128,128]{2,1,0:T(8,128)S(1)} %get-tuple-element.40), channel_id=1, source_target_pairs={{0,3},{1,2},{2,1},{3,0},{4,7},{5,6},{6,5},{7,4},{8,11},{9,10},{10,... | collective-permute-start | bytes 786440 | tf_op jit(solution)/shard_map/ppermute | solution.py:22
  319.3 4.1 %collective-permute-done.31.refs_6_ = f32[4,128,128]{2,1,0:T(8,128)S(1)} collective-permute-done((f32[4,128,128]{2,1,0:T(8,128)S(1)}, f32[4,128,128]{2,1,0:T(8,128)S(1)}, u32[]{:S(2)}, u32[]{:S(2)}) %collective-permute-start.31) | collective-permute-done | bytes 262176 | tf_op jit(solution)/shard_map/ppermute | solution.py:22
  323.4 12.6 %collective-permute-done.32.refs_7_ = f32[4,128,128]{2,1,0:T(8,128)S(1)} collective-permute-done((f32[4,128,128]{2,1,0:T(8,128)S(1)}, f32[4,128,128]{2,1,0:T(8,128)S(1)}, u32[]{:S(2)}, u32[]{:S(2)}) %collective-permute-start.32) | collective-permute-done | bytes 262176 | tf_op jit(solution)/shard_map/ppermute | solution.py:22
  336.8 19.0 %collective-permute-done.36.refs_12_ = f32[4,128,128]{2,1,0:T(8,128)S(1)} collective-permute-done((f32[4,128,128]{2,1,0:T(8,128)S(1)}, f32[4,128,128]{2,1,0:T(8,128)S(1)}, u32[]{:S(2)}, u32[]{:S(2)}) %collective-permute-start.36) | collective-permute-done | bytes 262176 | tf_op jit(solution)/shard_map/ppermute | solution.py:22
  355.8 5.6 %collective-permute-done.37.refs_13_ = f32[4,128,128]{2,1,0:T(8,128)S(1)} collective-permute-done((f32[4,128,128]{2,1,0:T(8,128)S(1)}, f32[4,128,128]{2,1,0:T(8,128)S(1)}, u32[]{:S(2)}, u32[]{:S(2)}) %collective-permute-start.37) | collective-permute-done | bytes 262176 | tf_op jit(solution)/shard_map/ppermute | solution.py:22
  361.5 6.9 %collective-permute-done.38.refs_14_ = f32[4,128,128]{2,1,0:T(8,128)S(1)} collective-permute-done((f32[4,128,128]{2,1,0:T(8,128)S(1)}, f32[4,128,128]{2,1,0:T(8,128)S(1)}, u32[]{:S(2)}, u32[]{:S(2)}) %collective-permute-start.38) | collective-permute-done | bytes 262176 | tf_op jit(solution)/shard_map/ppermute | solution.py:22
  368.4 6.2 %collective-permute-done.39.refs_15_ = f32[4,128,128]{2,1,0:T(8,128)S(1)} collective-permute-done((f32[4,128,128]{2,1,0:T(8,128)S(1)}, f32[4,128,128]{2,1,0:T(8,128)S(1)}, u32[]{:S(2)}, u32[]{:S(2)}) %collective-permute-start.39) | collective-permute-done | bytes 262176 | tf_op jit(solution)/shard_map/ppermute | solution.py:22
  375.3 4.1 %collect.1 = f32[42,128,128]{2,1,0:T(8,128)} custom-call(s32[2]{0:T(128)} %pad_add_fusion.1.place_ref, s32[8,8]{1,0:T(8,128)} %bitcast.100, f32[4,128,128]{2,1,0:T(8,128)} %copy-done.16, f32[4,128,128]{2,1,0:T(8,128)} %copy-done.23, f32[4,128,128]{2,1,0:T(8,128)} %copy-done.24, f32[4,128,128]{2,1,0:T(8,128)} %copy-done.25, f32[4,128,128]{2,1,0:T(8,128)} %copy-done.26, ...), custom_call_target="tpu_custom_call" | custom-call | tf_op jit(solution)/shard_map/collect/pallas_call | solution.py:391
  (161 shorter events, 52.1 us)
Async XLA Ops:
  0.0 88.1 %collective-permute-start.4 = (f32[42,128,128]{2,1,0:T(8,128)}, f32[42,128,128]{2,1,0:T(8,128)}, u32[]{:S(2)}, u32[]{:S(2)}) collective-permute-start(f32[42,128,128]{2,1,0:T(8,128)} %bitcast.96), channel_id=1, source_target_pairs={{0,8},{8,0},{16,24},{24,16},{1,9},{9,1},{17,25},{25,17},{2,10},{10... | collective-permute-start | bytes 8257544 | tf_op jit(solution)/shard_map/ppermute | solution.py:22
  0.3 87.8 %collective-permute-start.6 = (f32[42,128,128]{2,1,0:T(8,128)}, f32[42,128,128]{2,1,0:T(8,128)}, u32[]{:S(2)}, u32[]{:S(2)}) collective-permute-start(f32[42,128,128]{2,1,0:T(8,128)} %bitcast.97), channel_id=1, source_target_pairs={{0,16},{8,24},{16,0},{24,8},{1,17},{9,25},{17,1},{25,9},{2,18},{10... | collective-permute-start | bytes 8257544 | tf_op jit(solution)/shard_map/ppermute | solution.py:22
  3.9 65.9 %collective-permute-start.8 = (f32[8,128,128]{2,1,0:T(8,128)}, f32[8,128,128]{2,1,0:T(8,128)S(1)}, u32[]{:S(2)}, u32[]{:S(2)}) collective-permute-start(f32[8,128,128]{2,1,0:T(8,128)} %gather_fusion), channel_id=1, source_target_pairs={{0,6},{1,7},{2,4},{3,5},{4,2},{5,3},{6,0},{7,1},{8,14},{9,15},{10,... | collective-permute-start | bytes 1572872 | tf_op jit(solution)/shard_map/ppermute | solution.py:22
  5.2 24.2 %collective-permute-start = (s32[2,32]{1,0:T(2,128)}, s32[2,32]{1,0:T(2,128)S(1)}, u32[]{:S(2)}, u32[]{:S(2)}) collective-permute-start(s32[2,32]{1,0:T(2,128)} %bitcast.104), channel_id=1, source_target_pairs={{0,7},{1,0},{2,1},{3,2},{4,3},{5,4},{6,5},{7,6},{8,15},{9,8},{10,9... | collective-permute-start | bytes 776 | tf_op jit(solution)/shard_map/ppermute | solution.py:22
  8.3 52.5 %collective-permute-start.1 = (s32[128]{0:T(128)S(1)}, s32[128]{0:T(128)S(1)}, u32[]{:S(2)}, u32[]{:S(2)}) collective-permute-start(s32[128]{0:T(128)S(1)} %pad_add_fusion.2), channel_id=1, source_target_pairs={{0,8},{8,0},{16,24},{24,16},{1,9},{9,1},{17,25},{25,17},{2,10},{10... | collective-permute-start | bytes 1544 | tf_op jit(solution)/shard_map/ppermute | solution.py:22
  29.4 34.2 %collective-permute-start.2 = (s32[128]{0:T(128)S(1)}, s32[128]{0:T(128)S(1)}, u32[]{:S(2)}, u32[]{:S(2)}) collective-permute-start(s32[128]{0:T(128)S(1)} %pad_add_fusion.2), channel_id=1, source_target_pairs={{0,16},{8,24},{16,0},{24,8},{1,17},{9,25},{17,1},{25,9},{2,18},{10... | collective-permute-start | bytes 1544 | tf_op jit(solution)/shard_map/ppermute | solution.py:22
  60.9 26.9 %collective-permute-start.9 = (f32[8,128,128]{2,1,0:T(8,128)}, f32[8,128,128]{2,1,0:T(8,128)}, u32[]{:S(2)}, u32[]{:S(2)}) collective-permute-start(f32[8,128,128]{2,1,0:T(8,128)} %gather_fusion.1), channel_id=1, source_target_pairs={{0,7},{1,6},{2,5},{3,4},{4,3},{5,2},{6,1},{7,0},{8,15},{9,14},{10,... | collective-permute-start | bytes 1572872 | tf_op jit(solution)/shard_map/ppermute | solution.py:22
  67.7 28.4 %collective-permute-start.11 = (f32[8,128,128]{2,1,0:T(8,128)}, f32[8,128,128]{2,1,0:T(8,128)}, u32[]{:S(2)}, u32[]{:S(2)}) collective-permute-start(f32[8,128,128]{2,1,0:T(8,128)} %gather_fusion.2), channel_id=1, source_target_pairs={{0,2},{1,3},{2,0},{3,1},{4,6},{5,7},{6,4},{7,5},{8,10},{9,11},{10,... | collective-permute-start | bytes 1572872 | tf_op jit(solution)/shard_map/ppermute | solution.py:22
  69.9 38.8 %collective-permute-start.14 = (f32[8,128,128]{2,1,0:T(8,128)}, f32[8,128,128]{2,1,0:T(8,128)}, u32[]{:S(2)}, u32[]{:S(2)}) collective-permute-start(f32[8,128,128]{2,1,0:T(8,128)} %gather_fusion.3), channel_id=1, source_target_pairs={{0,3},{1,2},{2,1},{3,0},{4,7},{5,6},{6,5},{7,4},{8,11},{9,10},{10,... | collective-permute-start | bytes 1572872 | tf_op jit(solution)/shard_map/ppermute | solution.py:22
  87.8 22.9 %collective-permute-start.16 = (f32[8,128,128]{2,1,0:T(8,128)}, f32[8,128,128]{2,1,0:T(8,128)}, u32[]{:S(2)}, u32[]{:S(2)}) collective-permute-start(f32[8,128,128]{2,1,0:T(8,128)} %gather_fusion.5), channel_id=1, source_target_pairs={{0,1},{1,0},{2,3},{3,2},{4,5},{5,4},{6,7},{7,6},{8,9},{9,8},{10,11... | collective-permute-start | bytes 1572872 | tf_op jit(solution)/shard_map/ppermute | solution.py:22
  88.1 23.0 %collective-permute-start.17 = (f32[8,128,128]{2,1,0:T(8,128)}, f32[8,128,128]{2,1,0:T(8,128)}, u32[]{:S(2)}, u32[]{:S(2)}) collective-permute-start(f32[8,128,128]{2,1,0:T(8,128)} %gather_fusion.6), channel_id=1, source_target_pairs={{0,4},{1,5},{2,6},{3,7},{4,0},{5,1},{6,2},{7,3},{8,12},{9,13},{10,... | collective-permute-start | bytes 1572872 | tf_op jit(solution)/shard_map/ppermute | solution.py:22
  88.1 51.0 %collective-permute-start.18 = (f32[8,128,128]{2,1,0:T(8,128)}, f32[8,128,128]{2,1,0:T(8,128)}, u32[]{:S(2)}, u32[]{:S(2)}) collective-permute-start(f32[8,128,128]{2,1,0:T(8,128)} %gather_fusion.7), channel_id=1, source_target_pairs={{0,5},{1,4},{2,7},{3,6},{4,1},{5,0},{6,3},{7,2},{8,13},{9,12},{10,... | collective-permute-start | bytes 1572872 | tf_op jit(solution)/shard_map/ppermute | solution.py:22
  96.0 68.4 %collective-permute-start.5 = (f32[21,128,128]{2,1,0:T(8,128)}, f32[21,128,128]{2,1,0:T(8,128)}, u32[]{:S(2)}, u32[]{:S(2)}) collective-permute-start(f32[21,128,128]{2,1,0:T(8,128)} %slice.26), channel_id=1, source_target_pairs={{0,16},{8,24},{16,0},{24,8},{1,17},{9,25},{17,1},{25,9},{2,18},{10... | collective-permute-start | bytes 4128776 | tf_op jit(solution)/shard_map/ppermute | solution.py:22
  108.7 70.8 %collective-permute-start.7 = (f32[21,128,128]{2,1,0:T(8,128)}, f32[21,128,128]{2,1,0:T(8,128)}, u32[]{:S(2)}, u32[]{:S(2)}) collective-permute-start(f32[21,128,128]{2,1,0:T(8,128)} %slice.27), channel_id=1, source_target_pairs={{0,8},{8,0},{16,24},{24,16},{1,9},{9,1},{17,25},{25,17},{2,10},{10... | collective-permute-start | bytes 4128776 | tf_op jit(solution)/shard_map/ppermute | solution.py:22
  110.7 30.1 %collective-permute-start.19 = (f32[8,128,128]{2,1,0:T(8,128)S(1)}, f32[8,128,128]{2,1,0:T(8,128)S(1)}, u32[]{:S(2)}, u32[]{:S(2)}) collective-permute-start(f32[8,128,128]{2,1,0:T(8,128)S(1)} %gather_fusion.4), channel_id=1, source_target_pairs={{0,7},{1,0},{2,1},{3,2},{4,3},{5,4},{6,5},{7,6},{8,15},{9,8},{10,9... | collective-permute-start | bytes 1572872 | tf_op jit(solution)/shard_map/ppermute | solution.py:22
  111.1 31.9 %collective-permute-start.21 = (f32[8,128,128]{2,1,0:T(8,128)}, f32[8,128,128]{2,1,0:T(8,128)S(1)}, u32[]{:S(2)}, u32[]{:S(2)}) collective-permute-start(f32[8,128,128]{2,1,0:T(8,128)} %gather_fusion.8), channel_id=1, source_target_pairs={{2,3},{6,7},{10,11},{14,15},{18,19},{22,23},{26,27},{30,31}} | collective-permute-start | bytes 1572872 | tf_op jit(solution)/shard_map/ppermute | solution.py:22
  155.6 71.7 %collective-permute-start.20 = (f32[8,128,128]{2,1,0:T(8,128)}, f32[8,128,128]{2,1,0:T(8,128)}, u32[]{:S(2)}, u32[]{:S(2)}) collective-permute-start(f32[8,128,128]{2,1,0:T(8,128)} %collective-permute-done.16.refs_1_), channel_id=1, source_target_pairs={{0,7},{1,0},{2,1},{3,2},{4,3},{5,4},{6,5},{7,6},{8,15},{9,8},{10,9... | collective-permute-start | bytes 1572872 | tf_op jit(solution)/shard_map/ppermute | solution.py:22
  155.6 71.7 %collective-permute-start.22 = (f32[8,128,128]{2,1,0:T(8,128)}, f32[8,128,128]{2,1,0:T(8,128)}, u32[]{:S(2)}, u32[]{:S(2)}) collective-permute-start(f32[8,128,128]{2,1,0:T(8,128)} %collective-permute-done.17.refs_4_), channel_id=1, source_target_pairs={{1,0},{2,1},{3,2},{5,4},{6,5},{7,6},{9,8},{10,9},{11,10},{13,12},{... | collective-permute-start | bytes 1572872 | tf_op jit(solution)/shard_map/ppermute | solution.py:22
  162.1 65.2 %collective-permute-start.24 = (f32[8,128,128]{2,1,0:T(8,128)}, f32[8,128,128]{2,1,0:T(8,128)}, u32[]{:S(2)}, u32[]{:S(2)}) collective-permute-start(f32[8,128,128]{2,1,0:T(8,128)} %collective-permute-done.18.refs_5_), channel_id=1, source_target_pairs={{1,0},{2,1},{3,2},{5,4},{6,5},{7,6},{9,8},{10,9},{11,10},{13,12},{... | collective-permute-start | bytes 1572872 | tf_op jit(solution)/shard_map/ppermute | solution.py:22
  164.4 86.5 %collective-permute-start.10 = (f32[8,128,128]{2,1,0:T(8,128)}, f32[8,128,128]{2,1,0:T(8,128)}, u32[]{:S(2)}, u32[]{:S(2)}) collective-permute-start(f32[8,128,128]{2,1,0:T(8,128)} %copy-done.3), channel_id=1, source_target_pairs={{1,0},{2,1},{3,2},{5,4},{6,5},{7,6},{9,8},{10,9},{11,10},{13,12},{... | collective-permute-start | bytes 1572872 | tf_op jit(solution)/shard_map/ppermute | solution.py:22
  179.4 71.5 %collective-permute-start.13 = (f32[8,128,128]{2,1,0:T(8,128)}, f32[8,128,128]{2,1,0:T(8,128)}, u32[]{:S(2)}, u32[]{:S(2)}) collective-permute-start(f32[8,128,128]{2,1,0:T(8,128)} %collective-permute-done.9.refs_1_), channel_id=1, source_target_pairs={{1,0},{2,1},{3,2},{5,4},{6,5},{7,6},{9,8},{10,9},{11,10},{13,12},{... | collective-permute-start | bytes 1572872 | tf_op jit(solution)/shard_map/ppermute | solution.py:22
  260.7 34.4 %collective-permute-start.26 = (f32[4,128,128]{2,1,0:T(8,128)S(1)}, f32[4,128,128]{2,1,0:T(8,128)S(1)}, u32[]{:S(2)}, u32[]{:S(2)}) collective-permute-start(f32[4,128,128]{2,1,0:T(8,128)S(1)} %get-tuple-element.30), channel_id=1, source_target_pairs={{0,1},{1,0},{2,3},{3,2},{4,5},{5,4},{6,7},{7,6},{8,9},{9,8},{10,11... | collective-permute-start | bytes 786440 | tf_op jit(solution)/shard_map/ppermute | solution.py:22
  282.6 19.5 %collective-permute-start.30 = (f32[4,128,128]{2,1,0:T(8,128)S(1)}, f32[4,128,128]{2,1,0:T(8,128)S(1)}, u32[]{:S(2)}, u32[]{:S(2)}) collective-permute-start(f32[4,128,128]{2,1,0:T(8,128)S(1)} %get-tuple-element.34), channel_id=1, source_target_pairs={{0,5},{1,4},{2,7},{3,6},{4,1},{5,0},{6,3},{7,2},{8,13},{9,12},{10,... | collective-permute-start | bytes 786440 | tf_op jit(solution)/shard_map/ppermute | solution.py:22
  295.1 28.3 %collective-permute-start.31 = (f32[4,128,128]{2,1,0:T(8,128)S(1)}, f32[4,128,128]{2,1,0:T(8,128)S(1)}, u32[]{:S(2)}, u32[]{:S(2)}) collective-permute-start(f32[4,128,128]{2,1,0:T(8,128)S(1)} %get-tuple-element.35), channel_id=1, source_target_pairs={{0,6},{1,7},{2,4},{3,5},{4,2},{5,3},{6,0},{7,1},{8,14},{9,15},{10,... | collective-permute-start | bytes 786440 | tf_op jit(solution)/shard_map/ppermute | solution.py:22
  295.1 41.0 %collective-permute-start.32 = (f32[4,128,128]{2,1,0:T(8,128)S(1)}, f32[4,128,128]{2,1,0:T(8,128)S(1)}, u32[]{:S(2)}, u32[]{:S(2)}) collective-permute-start(f32[4,128,128]{2,1,0:T(8,128)S(1)} %get-tuple-element.36), channel_id=1, source_target_pairs={{0,7},{1,6},{2,5},{3,4},{4,3},{5,2},{6,1},{7,0},{8,15},{9,14},{10,... | collective-permute-start | bytes 786440 | tf_op jit(solution)/shard_map/ppermute | solution.py:22
  298.7 37.4 %collective-permute-start.33 = (f32[4,128,128]{2,1,0:T(8,128)S(1)}, f32[4,128,128]{2,1,0:T(8,128)S(1)}, u32[]{:S(2)}, u32[]{:S(2)}) collective-permute-start(f32[4,128,128]{2,1,0:T(8,128)S(1)} %get-tuple-element.38), channel_id=1, source_target_pairs={{0,1},{1,0},{2,3},{3,2},{4,5},{5,4},{6,7},{7,6},{8,9},{9,8},{10,11... | collective-permute-start | bytes 786440 | tf_op jit(solution)/shard_map/ppermute | solution.py:22
  298.7 37.5 %collective-permute-start.34 = (f32[4,128,128]{2,1,0:T(8,128)S(1)}, f32[4,128,128]{2,1,0:T(8,128)S(1)}, u32[]{:S(2)}, u32[]{:S(2)}) collective-permute-start(f32[4,128,128]{2,1,0:T(8,128)S(1)} %get-tuple-element.39), channel_id=1, source_target_pairs={{0,2},{1,3},{2,0},{3,1},{4,6},{5,7},{6,4},{7,5},{8,10},{9,11},{10,... | collective-permute-start | bytes 786440 | tf_op jit(solution)/shard_map/ppermute | solution.py:22
  302.1 34.7 %collective-permute-start.35 = (f32[4,128,128]{2,1,0:T(8,128)S(1)}, f32[4,128,128]{2,1,0:T(8,128)S(1)}, u32[]{:S(2)}, u32[]{:S(2)}) collective-permute-start(f32[4,128,128]{2,1,0:T(8,128)S(1)} %get-tuple-element.40), channel_id=1, source_target_pairs={{0,3},{1,2},{2,1},{3,0},{4,7},{5,6},{6,5},{7,4},{8,11},{9,10},{10,... | collective-permute-start | bytes 786440 | tf_op jit(solution)/shard_map/ppermute | solution.py:22
  323.4 32.4 %collective-permute-start.36 = (f32[4,128,128]{2,1,0:T(8,128)S(1)}, f32[4,128,128]{2,1,0:T(8,128)S(1)}, u32[]{:S(2)}, u32[]{:S(2)}) collective-permute-start(f32[4,128,128]{2,1,0:T(8,128)S(1)} %get-tuple-element.41), channel_id=1, source_target_pairs={{0,4},{1,5},{2,6},{3,7},{4,0},{5,1},{6,2},{7,3},{8,12},{9,13},{10,... | collective-permute-start | bytes 786440 | tf_op jit(solution)/shard_map/ppermute | solution.py:22
  336.1 25.4 %collective-permute-start.37 = (f32[4,128,128]{2,1,0:T(8,128)S(1)}, f32[4,128,128]{2,1,0:T(8,128)S(1)}, u32[]{:S(2)}, u32[]{:S(2)}) collective-permute-start(f32[4,128,128]{2,1,0:T(8,128)S(1)} %get-tuple-element.42), channel_id=1, source_target_pairs={{0,5},{1,4},{2,7},{3,6},{4,1},{5,0},{6,3},{7,2},{8,13},{9,12},{10,... | collective-permute-start | bytes 786440 | tf_op jit(solution)/shard_map/ppermute | solution.py:22
  336.1 32.3 %collective-permute-start.38 = (f32[4,128,128]{2,1,0:T(8,128)S(1)}, f32[4,128,128]{2,1,0:T(8,128)S(1)}, u32[]{:S(2)}, u32[]{:S(2)}) collective-permute-start(f32[4,128,128]{2,1,0:T(8,128)S(1)} %get-tuple-element.43), channel_id=1, source_target_pairs={{0,6},{1,7},{2,4},{3,5},{4,2},{5,3},{6,0},{7,1},{8,14},{9,15},{10,... | collective-permute-start | bytes 786440 | tf_op jit(solution)/shard_map/ppermute | solution.py:22
  336.2 38.4 %collective-permute-start.39 = (f32[4,128,128]{2,1,0:T(8,128)S(1)}, f32[4,128,128]{2,1,0:T(8,128)S(1)}, u32[]{:S(2)}, u32[]{:S(2)}) collective-permute-start(f32[4,128,128]{2,1,0:T(8,128)S(1)} %get-tuple-element.44), channel_id=1, source_target_pairs={{0,7},{1,6},{2,5},{3,4},{4,3},{5,2},{6,1},{7,0},{8,15},{9,14},{10,... | collective-permute-start | bytes 786440 | tf_op jit(solution)/shard_map/ppermute | solution.py:22
  (47 other events, 982.3 us)

commit v2 on v1

--- a/solution.py
+++ b/solution.py
@@ -11,8 +11,10 @@
 GROUP = 4
 UNROLL = 4
 SHIFT = 1024
+READ = 8
 ABSENT = -(1 << 24)
-LATE = 1 << 10
+LATE = 20
+RELAY = 21
 SMEM = pl.BlockSpec(memory_space=pltpu.SMEM)
 HBM = pl.BlockSpec(memory_space=pl.ANY)
 
@@ -28,6 +30,11 @@
         for key, value in list(held.items()):
             held[mask ^ key] = moved(value, axis, lambda source: source ^ mask)
     return held
+
+
+def right_order(rows):
+    direct = [0] + [1 << bit for bit in range((rows - 1).bit_length())]
+    return direct + [mask for mask in range(rows) if mask not in direct]
 
 
 def plan_body(sizes, place_ref, triple_ref, left_ref, left_next_ref, table_ref, code_ref, slot_ref, bound_ref,
@@ -43,7 +50,7 @@
         for image in range(2):
             left_at[(stop * 2 + image) * stride] = ABSENT
             right_at[(stop * 2 + image) * stride] = ABSENT
-            out_at[image * stride] = 2 * slots
+            out_at[image * stride] = slots
 
     def tables(index, _):
         image = index // panel
@@ -56,7 +63,7 @@
             if stop == 0:
                 bucket = owner ^ col
                 spot = (within // half) * (cols * half) + bucket * half + lax.rem(within, half)
-                out_at[image * stride + 1 + slot] = jnp.where(left >= 0, spot, 2 * slots)
+                out_at[image * stride + 1 + slot] = jnp.where(left >= 0, spot, slots)
             else:
                 after = lax.rem(col + 1, cols)
                 bucket = owner ^ after
@@ -65,9 +72,9 @@
                 turned = jnp.where(bucket < middle, turned, quarter + (owner ^ col))
                 bucket = jnp.where(crossing, turned, bucket)
             late = bucket >= 3 * quarter
-            early_at = 1 + (stop * 3 * quarter + bucket) * per_left + within
-            late_at = 1 + (stop * quarter + bucket - 3 * quarter) * per_left + within + LATE
-            left_at[entry] = jnp.where(left >= 0, jnp.where(late, late_at, early_at) * SHIFT, ABSENT)
+            early_at = (1 + (stop * 3 * quarter + bucket) * per_left + within) * SHIFT
+            late_at = (1 + (stop * quarter + bucket - 3 * quarter) * per_left + within) * SHIFT + (1 << LATE)
+            left_at[entry] = jnp.where(left >= 0, jnp.where(late, late_at, early_at), ABSENT)
             target = lax.rem(row + stop, rows)
             turned = jnp.where(row == rows - 1, 1 - image, image) if stop == 1 else image
             place = table_ref[target ^ row, rows * per_right + turned * panel + slot]
@@ -75,8 +82,12 @@
             source = (safe // per_right) ^ row
             block = table_ref[source, target * per_right + lax.rem(safe, per_right)]
             there = (place >= 0) & (block >= 0)
-            right_at[entry] = jnp.where(there, stop * 2 * panel + index, ABSENT)
-            block_ref[stop * 2 * panel + index] = jnp.where(there, source * own + block, 0)
+            rank = jnp.int32(0)
+            for position, mask in enumerate(right_order(rows)):
+                rank = jnp.where(source == mask, position, rank)
+            relay = (rank >= rows.bit_length()).astype(jnp.int32) << RELAY
+            right_at[entry] = jnp.where(there, stop * 2 * panel + index + relay, ABSENT)
+            block_ref[stop * 2 * panel + index] = jnp.where(there, rank * own + block, 0)
         return 0
 
     lax.fori_loop(0, 2 * panel, tables, 0)
@@ -85,27 +96,30 @@
         count_ref[index] = 0
         return 0
 
-    lax.fori_loop(0, 2 * slots + 1, clear, 0)
+    lax.fori_loop(0, 3 * slots + 1, clear, 0)
     total = jnp.int32(0)
     for stop in range(2):
         for image in range(2):
-            base = (stop * 2 + image) * stride + 1
-
-            def read(index, found):
-                a = triple_ref[image, stop, 0, index]
-                b = triple_ref[image, stop, 1, index]
-                t = triple_ref[image, stop, 2, index]
-                code = left_at[base + a] + right_at[base + b]
-                spot = out_at[image * stride + 1 + t]
-                live = (code >= 0) & (spot < slots)
-                late = (code >= LATE * SHIFT).astype(jnp.int32)
-                key = jnp.where(live, spot + late * slots, 2 * slots)
-                raw_code[found] = code - late * (LATE * SHIFT)
-                raw_key[found] = key
-                count_ref[key] = count_ref[key] + 1
-                return found + live.astype(jnp.int32)
-
-            total = lax.fori_loop(0, pairs, read, total, unroll=4)
+            base = (stop * 2 + image) * stride
+
+            def read(step, found):
+                codes, spots = [], []
+                for lane in range(READ):
+                    packed = triple_ref[(image * 2 + stop) * pairs + step * READ + lane]
+                    codes.append(left_at[base + (packed & 255)] + right_at[base + ((packed >> 8) & 255)])
+                    spots.append(out_at[image * stride + (packed >> 16)])
+                for code, spot in zip(codes, spots):
+                    live = (code >= 0) & (spot < slots)
+                    chapter = (code >> RELAY) & 1 if stop == 0 else 1
+                    chapter = jnp.where(((code >> LATE) & 1) == 1, 2, chapter)
+                    key = jnp.where(live, spot + chapter * slots, 3 * slots)
+                    raw_code[found] = code & ((1 << LATE) - 1)
+                    raw_key[found] = key
+                    count_ref[key] = count_ref[key] + 1
+                    found = found + live.astype(jnp.int32)
+                return found
+
+            total = lax.fori_loop(0, pairs // READ, read, total)
 
     def fill(index, _):
         code_ref[index] = 0
@@ -132,7 +146,8 @@
 
     done = jnp.int32(0)
     bound_ref[0] = 0
-    for part, (low, high) in enumerate([(0, slots), (slots, slots + slots // 2), (slots + slots // 2, 2 * slots)]):
+    cuts = (0, slots, 2 * slots, 2 * slots + slots // 2, 3 * slots)
+    for part, (low, high) in enumerate(zip(cuts[:-1], cuts[1:])):
         done = lax.fori_loop(low, high, prefix, done)
         done = (done + UNROLL - 1) // UNROLL * UNROLL
         bound_ref[part + 1] = done // UNROLL
@@ -150,14 +165,14 @@
 def make_plan(place, triples, left_place, left_next, table, sizes):
     _, cols, _, per_left, _, panel, pairs = sizes
     slots = cols * per_left
-    groups = 4 * pairs // GROUP + 2 * slots + 3 * UNROLL
+    groups = 4 * pairs // GROUP + 3 * slots + 4 * UNROLL
     groups = (groups + 31) // 32 * 32
     return pl.pallas_call(
         functools.partial(plan_body, sizes),
         out_shape=(
             jax.ShapeDtypeStruct((groups * GROUP,), jnp.int32),
             jax.ShapeDtypeStruct((groups,), jnp.int32),
-            jax.ShapeDtypeStruct((4,), jnp.int32),
+            jax.ShapeDtypeStruct((5,), jnp.int32),
             jax.ShapeDtypeStruct((4 * panel,), jnp.int32),
         ),
         in_specs=[SMEM] * 5,
@@ -168,7 +183,7 @@
             pltpu.SMEM((2 * (panel + 1),), jnp.int32),
             pltpu.SMEM((4 * pairs + 8,), jnp.int32),
             pltpu.SMEM((4 * pairs + 8,), jnp.int32),
-            pltpu.SMEM((2 * slots + 8,), jnp.int32),
+            pltpu.SMEM((3 * slots + 8,), jnp.int32),
         ],
         cost_estimate=pl.CostEstimate(flops=40_000_000, bytes_accessed=60_000_000, transcendentals=0),
         name="plan",
@@ -224,15 +239,13 @@
         store(step).wait()
 
 
-def split(pieces, count, held=None):
+def split(pieces, count):
     size = pieces[0][0].shape[-1]
-    held = [] if held is None else [held]
     return pl.pallas_call(
         functools.partial(split_body, [base for _, base in pieces]),
         out_shape=jax.ShapeDtypeStruct((count, size, 2 * size), jnp.bfloat16),
-        in_specs=[HBM] * (len(pieces) + len(held)),
+        in_specs=[HBM] * len(pieces),
         out_specs=HBM,
-        input_output_aliases={len(pieces): 0} if held else {},
         scratch_shapes=[
             pltpu.VMEM((DEPTH, CHUNK, size, size), jnp.float32),
             pltpu.VMEM((DEPTH, CHUNK, size, 2 * size), jnp.bfloat16),
@@ -241,17 +254,20 @@
         ],
         cost_estimate=pl.CostEstimate(flops=0, bytes_accessed=2 * count * size * size * 4, transcendentals=0),
         name="split",
-    )(*[piece for piece, _ in pieces], *held)
-
-
-def multiply_body(late, part, kinds, sizes, place_ref, code_ref, slot_ref, bound_ref, block_ref, right_ref, *refs):
-    _, cols, _, per_left, _, panel, _ = sizes
+    )(*[piece for piece, _ in pieces])
+
+
+def multiply_body(mode, part, kinds, sizes, place_ref, code_ref, slot_ref, bound_ref, block_ref, right_ref, *refs):
+    _, cols, _, per_left, _, _, _ = sizes
     slots = cols * per_left
     half = per_left // 2
+    relay_ref, refs = (refs[0], refs[1:]) if mode > 0 else (None, refs)
+    direct = right_ref.shape[0]
+    late, added = mode == 2, mode > 0
     spots = slots // 2 if late else slots
     outs = cols if late else 1
     count = len(kinds) + sum(kinds)
-    sources, before_ref, rest = refs[:count], refs[count] if late else None, refs[count + late :]
+    sources, before_ref, rest = refs[:count], refs[count] if added else None, refs[count + added :]
     out_refs, (lefts, rights, total, raw, left_sems, right_sem, total_sem, out_sem) = rest[:outs], rest[outs:]
     size = raw.shape[-1]
     first = part * spots
@@ -262,7 +278,16 @@
 
     def gather(index, _):
         block = block_ref[index]
-        pltpu.make_async_copy(right_ref.at[block], rights.at[index], right_sem).start()
+
+        @pl.when(block < direct)
+        def _():
+            pltpu.make_async_copy(right_ref.at[block], rights.at[index], right_sem).start()
+
+        @pl.when(block >= direct)
+        def _():
+            source = right_ref.at[0] if relay_ref is None else relay_ref.at[block - direct]
+            pltpu.make_async_copy(source, rights.at[index], right_sem).start()
+
         return 0
 
     offset = 0
@@ -280,8 +305,8 @@
         else:
             fetch(sources[offset], bucket).start()
         offset += 1 + two
-    lax.fori_loop(0, 4 * panel, gather, 0, unroll=4)
-    if late:
+    lax.fori_loop(0, rights.shape[0], gather, 0, unroll=4)
+    if added:
         carried = pltpu.make_async_copy(before_ref.at[pl.ds(first, spots)], total.at[pl.ds(0, spots)], total_sem)
         carried.start()
         total[spots] = jnp.zeros(total.shape[1:], total.dtype)
@@ -298,8 +323,8 @@
             return 0
 
         lax.fori_loop(bucket * per_left, (bucket + 1) * per_left, convert, 0, unroll=2)
-    pltpu.make_async_copy(right_ref.at[pl.ds(0, 4 * panel)], rights, right_sem).wait()
-    if late:
+    pltpu.make_async_copy(rights, rights, right_sem).wait()
+    if added:
         carried.wait()
 
     def multiply(step, _):
@@ -320,7 +345,7 @@
             total[spot] += product[:, 0:size] + product[:, size : 2 * size]
         return 0
 
-    chapter = 1 + part if late else 0
+    chapter = mode + part
     lax.fori_loop(bound_ref[chapter], bound_ref[chapter + 1], multiply, 0)
     copies = []
     if late:
@@ -336,25 +361,27 @@
         entry.wait()
 
 
-def multiplied(late, part, sizes, place, plan, rights, lefts, before=None):
+def multiplied(mode, part, sizes, place, plan, rights, lefts, before=None):
     _, cols, _, per_left, _, panel, _ = sizes
     slots = cols * per_left
+    late = mode == 2
     spots = slots // 2 if late else slots
-    size = rights.shape[1]
+    size = rights[0].shape[1]
+    rights = rights[: 1 + (mode > 0)]
     if late:
         out_shape = [jax.ShapeDtypeStruct((per_left // 2, size, size), jnp.float32)] * cols
         out_specs = [HBM] * cols
     else:
         out_shape, out_specs = jax.ShapeDtypeStruct((slots, size, size), jnp.float32), HBM
-    arrays = [array for entry in lefts for array in entry] + ([before] if late else [])
+    arrays = [array for entry in lefts for array in entry] + ([before] if mode > 0 else [])
     return pl.pallas_call(
-        functools.partial(multiply_body, late, part, [len(entry) - 1 for entry in lefts], sizes),
+        functools.partial(multiply_body, mode, part, [len(entry) - 1 for entry in lefts], sizes),
         out_shape=out_shape,
-        in_specs=[SMEM] * 5 + [HBM] * (1 + len(arrays)),
+        in_specs=[SMEM] * 5 + [HBM] * (len(rights) + len(arrays)),
         out_specs=out_specs,
         scratch_shapes=[
             pltpu.VMEM((len(lefts) * per_left + 1, size, 2 * size), jnp.bfloat16),
-            pltpu.VMEM((4 * panel, size, 2 * size), jnp.bfloat16),
+            pltpu.VMEM(((4 if mode > 0 else 2) * panel, size, 2 * size), jnp.bfloat16),
             pltpu.VMEM((spots + 1, size, size), jnp.float32),
             pltpu.VMEM((len(lefts) * per_left, size, size), jnp.float32),
             pltpu.SemaphoreType.DMA((len(lefts),)),
@@ -363,8 +390,8 @@
             pltpu.SemaphoreType.DMA((cols,)),
         ],
         cost_estimate=pl.CostEstimate(flops=0, bytes_accessed=4 * slots * size * size * 4, transcendentals=0),
-        compiler_params=pltpu.CompilerParams(vmem_limit_bytes=40 * 1024 * 1024),
-    )(place, *plan, rights, *arrays)
+        compiler_params=pltpu.CompilerParams(vmem_limit_bytes=48 * 1024 * 1024),
+    )(place, *plan, *rights, *arrays)
 
 
 def collect_body(sizes, place_ref, list_ref, *refs):
@@ -402,6 +429,15 @@
     )(place, left_list, *backs)
 
 
+def send_order(cols):
+    middle = cols // 2
+    order = []
+    for index in range(max(middle - 2, cols // 4)):
+        order += [mask for mask in (2 + index, middle + index) if mask < (middle if mask < middle else 3 * cols // 4)]
+    order = list(dict.fromkeys(order))
+    return order + [mask for mask in range(1, cols) if mask not in order and mask > 1] + [1]
+
+
 def local(left_blocks, right_blocks, left_send, left_place, right_send, right_place, triples):
     rows, cols = lax.axis_size("row"), lax.axis_size("col")
     row, col = lax.axis_index("row").astype(jnp.int32), lax.axis_index("col").astype(jnp.int32)
@@ -436,9 +472,11 @@
     def bucket_for(peer):
         return left_own[jnp.clip(left_list[peer], 0, own - 1)]
 
-    here = {0: bucket_for(col)}
-    for mask in range(1, cols):
-        here[mask] = moved(bucket_for(col ^ mask), "col", lambda source: source ^ mask)
+    here = {}
+    for mask in send_order(cols):
+        bucket = bucket_for(col ^ mask)
+        here[mask] = moved(bucket, "col", lambda source: source ^ mask)
+    here[0] = bucket_for(col)
     extra = {0: bucket_for(jnp.where(col < middle, middle, 0))}
     for mask in range(1, middle):
         extra[mask] = moved(
@@ -449,22 +487,25 @@
         among = None if mask < middle else [source for source in range(cols) if source % middle != 0]
         there[mask] = moved(here[mask], "col", back_one, among)
 
-    plan = make_plan(place, triples[0, 0], positions, left_next, table, sizes)
-    rights = split([(whole[mask], mask * own) for mask in whole], rows * own)
+    shifted = triples[0, 0] + 1
+    packed = (shifted[:, :, 0] + shifted[:, :, 1] * 256 + shifted[:, :, 2] * 65536).reshape(-1)
+    plan = make_plan(place, packed, positions, left_next, table, sizes)
+    direct = split([(whole[mask], index * own) for index, mask in enumerate(whole)], len(whole) * own)
     pieces = []
-    for mask in range(rows):
-        if mask not in whole:
-            pieces += [(low[mask], mask * own), (high[mask], mask * own + cut)]
-    rights = split(pieces, rows * own, rights)
-    early = [(here[mask],) for mask in range(3 * quarter)]
-    early += [(there[mask],) for mask in range(quarter)]
-    early += [(there[mask], extra[mask - quarter]) for mask in range(quarter, 3 * quarter)]
+    for index, mask in enumerate(right_order(rows)[len(whole) :]):
+        pieces += [(low[mask], index * own), (high[mask], index * own + cut)]
+    relayed = split(pieces, (rows - len(whole)) * own)
+    rights = (direct, relayed)
+    first = [(here[mask],) for mask in range(3 * quarter)]
+    second = first + [(there[mask],) for mask in range(quarter)]
+    second += [(there[mask], extra[mask - quarter]) for mask in range(quarter, 3 * quarter)]
     late = [(here[mask],) for mask in range(3 * quarter, cols)]
     late += [(there[mask], there[mask - middle]) for mask in range(3 * quarter, cols)]
-    before = multiplied(0, 0, sizes, place, plan, rights, early)
+    before = multiplied(0, 0, sizes, place, plan, rights, first)
+    before = multiplied(1, 0, sizes, place, plan, rights, second, before)
     backs = []
     for part in range(2):
-        product = multiplied(1, part, sizes, place, plan, rights, late, before)
+        product = multiplied(2, part, sizes, place, plan, rights, late, before)
         returned = {0: product[0]}
         for mask in list(range(middle, cols)) + list(range(1, middle)):
             returned[mask] = moved(product[mask], "col", lambda source: source ^ mask)

time: 380 us -> 409 us (1.076)
  waiting for transfers between devices: 170 us -> 200 us
  Pallas kernels: 82.1 us -> 96.7 us
  starting transfers between devices: 91.9 us -> 82.5 us
  local copies, waits for them, and re-layouts: 32.4 us -> 26.4 us
    ppermute x40, waiting for transfers between devices: 170 us -> 200 us  [moved(): lax.ppermute(value, axis, [(source, target(source)) for source in places])]
    pallas_call x3 -> x4, Pallas kernels: 34.3 us -> 50 us  [multiplied(): pl.pallas_call(functools.partial(multiply_body, mode, part, [len(entry) -...]
    ppermute x40, starting transfers between devices: 91.9 us -> 82.5 us  [moved(): lax.ppermute(value, axis, [(source, target(source)) for source in places])]
    unnamed x79 -> x62, local copies, waits for them, and re-layouts: 14 us -> 7.34 us
  transfers between devices with their start and end apart: 40 -> 40, of which waited for: 15 -> 15; matrix products, arithmetic and copies ran while one was open for 6% -> 5% of each run, Pallas kernels for 18% -> 20%
where the time goes in v2:
time: 409 us; the launch traced here: 408 us
  waiting for transfers between devices  200 us (49%)
  Pallas kernels  96.7 us (24%)
  starting transfers between devices  82.5 us (20%)
  local copies, waits for them, and re-layouts  26.4 us (6%)
    ppermute x40, waiting for transfers between devices, moved(): lax.ppermute(value, axis, [(source, target(source)) for source in places])  200 us
    ppermute x40, starting transfers between devices, moved(): lax.ppermute(value, axis, [(source, target(source)) for source in places])  82.5 us
    pallas_call x4, Pallas kernels, multiplied(): pl.pallas_call(functools.partial(multiply_body, mode, part, [len(entry) -...  50 us
    pallas_call x1, Pallas kernels, make_plan(): pl.pallas_call(functools.partial(plan_body, sizes), out_shape=(jax.ShapeD...  33.4 us
    gather x9, local copies, waits for them, and re-layouts, bucket_for(): return left_own[jnp.clip(left_list[peer], 0, own - 1)]  11.8 us
    pallas_call x2, Pallas kernels, split(): pl.pallas_call(functools.partial(split_body, [base for _, base in pieces]...  9.35 us
  transfers between devices with their start and end apart: 40, of which 15 were waited for; matrix products, arithmetic and copies ran while one was open for 5% of the time, Pallas kernels for 20%

profile of v2, /device:TPU:11, one launch (start us, length us, event | category | flops | bytes accessed | tf_op | source)
XLA Modules:
  0.0 408.4 jit_solution(11719234939992658561)
XLA Ops:
  10.1 2.8 collective-permute-done.left_next_ref
  13.1 47.8 %collective-permute-done.1 = s32[128]{0:T(128)S(1)} collective-permute-done((s32[128]{0:T(128)S(1)}, s32[128]{0:T(128)S(1)}, u32[]{:S(2)}, u32[]{:S(2)}) %collective-permute-start.1) | collective-permute-done | bytes 544 | tf_op jit(solution)/shard_map/ppermute | solution.py:24
  67.0 2.3 collective-permute-start.17
  72.8 8.5 %collective-permute-done.14.refs_3_.refs_4_ = f32[8,128,128]{2,1,0:T(8,128)} collective-permute-done((f32[8,128,128]{2,1,0:T(8,128)}, f32[8,128,128]{2,1,0:T(8,128)}, u32[]{:S(2)}, u32[]{:S(2)}) %collective-permute-start.14) | collective-permute-done | bytes 524320 | tf_op jit(solution)/shard_map/ppermute | solution.py:24
  84.3 2.6 slice.41
  86.8 2.6 slice.42
  91.4 17.5 %collective-permute-done.17.refs_4_.refs_5_ = f32[8,128,128]{2,1,0:T(8,128)} collective-permute-done((f32[8,128,128]{2,1,0:T(8,128)}, f32[8,128,128]{2,1,0:T(8,128)}, u32[]{:S(2)}, u32[]{:S(2)}) %collective-permute-start.17) | collective-permute-done | bytes 524320 | tf_op jit(solution)/shard_map/ppermute | solution.py:24
  111.6 8.6 %collective-permute-done.18.refs_5_.refs_6_ = f32[8,128,128]{2,1,0:T(8,128)} collective-permute-done((f32[8,128,128]{2,1,0:T(8,128)}, f32[8,128,128]{2,1,0:T(8,128)}, u32[]{:S(2)}, u32[]{:S(2)}) %collective-permute-start.18) | collective-permute-done | bytes 524320 | tf_op jit(solution)/shard_map/ppermute | solution.py:24
  122.8 5.2 %collective-permute-start.8 = (f32[8,128,128]{2,1,0:T(8,128)}, f32[8,128,128]{2,1,0:T(8,128)}, u32[]{:S(2)}, u32[]{:S(2)}) collective-permute-start(f32[8,128,128]{2,1,0:T(8,128)} %gather_fusion), channel_id=1, source_target_pairs={{0,6},{1,7},{2,4},{3,5},{4,2},{5,3},{6,0},{7,1},{8,14},{9,15},{10,... | collective-permute-start | bytes 1572872 | tf_op jit(solution)/shard_map/ppermute | solution.py:24
  129.4 5.0 %collective-permute-done.23.refs_14_ = f32[8,128,128]{2,1,0:T(8,128)} collective-permute-done((f32[8,128,128]{2,1,0:T(8,128)}, f32[8,128,128]{2,1,0:T(8,128)}, u32[]{:S(2)}, u32[]{:S(2)}) %collective-permute-start.23) | collective-permute-done | bytes 524320 | tf_op jit(solution)/shard_map/ppermute | solution.py:24
  134.4 3.8 collective-permute-done.25.refs_16_
  138.2 24.9 %collective-permute-done.8.refs_1_ = f32[8,128,128]{2,1,0:T(8,128)} collective-permute-done((f32[8,128,128]{2,1,0:T(8,128)}, f32[8,128,128]{2,1,0:T(8,128)}, u32[]{:S(2)}, u32[]{:S(2)}) %collective-permute-start.8) | collective-permute-done | bytes 524320 | tf_op jit(solution)/shard_map/ppermute | solution.py:24
  163.7 26.3 %collective-permute-done.9.refs_2_ = f32[8,128,128]{2,1,0:T(8,128)} collective-permute-done((f32[8,128,128]{2,1,0:T(8,128)}, f32[8,128,128]{2,1,0:T(8,128)}, u32[]{:S(2)}, u32[]{:S(2)}) %collective-permute-start.9) | collective-permute-done | bytes 524320 | tf_op jit(solution)/shard_map/ppermute | solution.py:24
  191.0 2.7 collective-permute-start.22
  202.0 33.4 %plan.1 = (s32[2432]{0:T(1024)}, s32[608]{0:T(1024)}, s32[5]{0:T(128)}, s32[128]{0:T(128)}) custom-call(s32[2]{0:T(128)} %pad_add_fusion.1.place_ref, s32[1536]{0:T(1024)} %add.141.triple_ref, s32[2,32]{1,0:T(2,128)} %bitcast.105, s32[2,32]{1,0:T(2,128)} %copy-done.30, s32[4,128]{1,0:T(4,128)} %pad_add_fusion.table_ref), custom_call_target="tpu_custom_call" | custom-call | flops 40000000 | bytes 60000000 | tf_op jit(solution)/shard_map/plan/pallas_call | solution.py:170
  235.4 6.5 %split.2.right_ref = bf16[126,128,256]{2,1,0:T(8,128)(2,1)} custom-call(f32[42,128,128]{2,1,0:T(8,128)} %bitcast.99, f32[42,128,128]{2,1,0:T(8,128)} %collective-permute-done.4.refs_1_, f32[42,128,128]{2,1,0:T(8,128)} %collective-permute-done.5.refs_2_), custom_call_target="tpu_custom_call" | custom-call | bytes 16515072 | tf_op jit(solution)/shard_map/split/pallas_call | solution.py:244
  244.1 12.0 %shard_map.73.refs_17_ = f32[64,128,128]{2,1,0:T(8,128)} custom-call(s32[2]{0:T(128)S(1)} %copy-done.12, s32[2432]{0:T(1024)S(1)} %copy-done.10, s32[608]{0:T(1024)S(1)} %copy-done.11, s32[5]{0:T(128)S(1)} %copy-done.13, s32[128]{0:T(128)S(1)} %copy-done.14, bf16[126,128,256]{2,1,0:T(8,128)(2,1)} %split.2.right_ref, f32[8,128,128]{2,1,0:T(8,128)S(1)} %copy-done.2, ...), custom_call_target="tpu_custom_call" | custom-call | bytes 16777216 | tf_op jit(solution)/shard_map/pallas_call | solution.py:377
  256.1 2.8 split.3.refs_0_
  262.0 18.2 %shard_map.74.refs_7_ = f32[64,128,128]{2,1,0:T(8,128)} custom-call(s32[2]{0:T(128)S(1)} %copy-done.12, s32[2432]{0:T(1024)S(1)} %copy-done.10, s32[608]{0:T(1024)S(1)} %copy-done.11, s32[5]{0:T(128)S(1)} %copy-done.13, s32[128]{0:T(128)S(1)} %copy-done.14, bf16[126,128,256]{2,1,0:T(8,128)(2,1)} %split.2.right_ref, bf16[42,128,256]{2,1,0:T(8,128)(2,1)} %split.3.refs_0_, ...), custom_call_target="tpu_custom_call" | custom-call | bytes 16777216 | tf_op jit(solution)/shard_map/pallas_call | solution.py:377
  280.3 9.9 %shard_map.76 = (f32[4,128,128]{2,1,0:T(8,128)S(1)}, f32[4,128,128]{2,1,0:T(8,128)S(1)}, f32[4,128,128]{2,1,0:T(8,128)S(1)}, f32[4,128,128]{2,1,0:T(8,128)S(1)},...) custom-call(s32[2]{0:T(128)S(1)} %copy-done.12, ...), custom_call_target="tpu_custom_call" | custom-call | bytes 16777216 | tf_op jit(solution)/shard_map/pallas_call | solution.py:377
  290.9 19.1 %collective-permute-start.33 = (f32[4,128,128]{2,1,0:T(8,128)S(1)}, f32[4,128,128]{2,1,0:T(8,128)S(1)}, u32[]{:S(2)}, u32[]{:S(2)}) collective-permute-start(f32[4,128,128]{2,1,0:T(8,128)S(1)} %get-tuple-element.38), channel_id=1, source_target_pairs={{0,1},{1,0},{2,3},{3,2},{4,5},{5,4},{6,7},{7,6},{8,9},{9,8},{10,11... | collective-permute-start | bytes 786440 | tf_op jit(solution)/shard_map/ppermute | solution.py:24
  311.6 2.8 collective-permute-start.37
  314.4 9.9 %shard_map.75 = (f32[4,128,128]{2,1,0:T(8,128)S(1)}, f32[4,128,128]{2,1,0:T(8,128)S(1)}, f32[4,128,128]{2,1,0:T(8,128)S(1)}, f32[4,128,128]{2,1,0:T(8,128)S(1)},...) custom-call(s32[2]{0:T(128)S(1)} %copy-done.12, ...), custom_call_target="tpu_custom_call" | custom-call | bytes 16777216 | tf_op jit(solution)/shard_map/pallas_call | solution.py:377
  325.0 4.3 %collective-permute-start.39 = (f32[4,128,128]{2,1,0:T(8,128)S(1)}, f32[4,128,128]{2,1,0:T(8,128)S(1)}, u32[]{:S(2)}, u32[]{:S(2)}) collective-permute-start(f32[4,128,128]{2,1,0:T(8,128)S(1)} %get-tuple-element.44), channel_id=1, source_target_pairs={{0,7},{1,6},{2,5},{3,4},{4,3},{5,2},{6,1},{7,0},{8,15},{9,14},{10,... | collective-permute-start | bytes 786440 | tf_op jit(solution)/shard_map/ppermute | solution.py:24
  331.4 17.0 %collective-permute-start.28 = (f32[4,128,128]{2,1,0:T(8,128)S(1)}, f32[4,128,128]{2,1,0:T(8,128)S(1)}, u32[]{:S(2)}, u32[]{:S(2)}) collective-permute-start(f32[4,128,128]{2,1,0:T(8,128)S(1)} %get-tuple-element.32), channel_id=1, source_target_pairs={{0,3},{1,2},{2,1},{3,0},{4,7},{5,6},{6,5},{7,4},{8,11},{9,10},{10,... | collective-permute-start | bytes 786440 | tf_op jit(solution)/shard_map/ppermute | solution.py:24
  348.4 4.1 %collective-permute-done.38.refs_14_ = f32[4,128,128]{2,1,0:T(8,128)S(1)} collective-permute-done((f32[4,128,128]{2,1,0:T(8,128)S(1)}, f32[4,128,128]{2,1,0:T(8,128)S(1)}, u32[]{:S(2)}, u32[]{:S(2)}) %collective-permute-start.38) | collective-permute-done | bytes 262176 | tf_op jit(solution)/shard_map/ppermute | solution.py:24
  352.5 12.6 %collective-permute-done.39.refs_15_ = f32[4,128,128]{2,1,0:T(8,128)S(1)} collective-permute-done((f32[4,128,128]{2,1,0:T(8,128)S(1)}, f32[4,128,128]{2,1,0:T(8,128)S(1)}, u32[]{:S(2)}, u32[]{:S(2)}) %collective-permute-start.39) | collective-permute-done | bytes 262176 | tf_op jit(solution)/shard_map/ppermute | solution.py:24
  365.8 19.0 %collective-permute-done.29.refs_4_ = f32[4,128,128]{2,1,0:T(8,128)S(1)} collective-permute-done((f32[4,128,128]{2,1,0:T(8,128)S(1)}, f32[4,128,128]{2,1,0:T(8,128)S(1)}, u32[]{:S(2)}, u32[]{:S(2)}) %collective-permute-start.29) | collective-permute-done | bytes 262176 | tf_op jit(solution)/shard_map/ppermute | solution.py:24
  384.9 5.6 %collective-permute-done.30.refs_5_ = f32[4,128,128]{2,1,0:T(8,128)S(1)} collective-permute-done((f32[4,128,128]{2,1,0:T(8,128)S(1)}, f32[4,128,128]{2,1,0:T(8,128)S(1)}, u32[]{:S(2)}, u32[]{:S(2)}) %collective-permute-start.30) | collective-permute-done | bytes 262176 | tf_op jit(solution)/shard_map/ppermute | solution.py:24
  390.5 6.9 %collective-permute-done.31.refs_6_ = f32[4,128,128]{2,1,0:T(8,128)S(1)} collective-permute-done((f32[4,128,128]{2,1,0:T(8,128)S(1)}, f32[4,128,128]{2,1,0:T(8,128)S(1)}, u32[]{:S(2)}, u32[]{:S(2)}) %collective-permute-start.31) | collective-permute-done | bytes 262176 | tf_op jit(solution)/shard_map/ppermute | solution.py:24
  397.4 6.2 %collective-permute-done.32.refs_7_ = f32[4,128,128]{2,1,0:T(8,128)S(1)} collective-permute-done((f32[4,128,128]{2,1,0:T(8,128)S(1)}, f32[4,128,128]{2,1,0:T(8,128)S(1)}, u32[]{:S(2)}, u32[]{:S(2)}) %collective-permute-start.32) | collective-permute-done | bytes 262176 | tf_op jit(solution)/shard_map/ppermute | solution.py:24
  404.3 4.1 collect.1
  (148 shorter events, 53.0 us)
Async XLA Ops:
  0.0 82.9 %collective-permute-start.4 = (f32[42,128,128]{2,1,0:T(8,128)}, f32[42,128,128]{2,1,0:T(8,128)}, u32[]{:S(2)}, u32[]{:S(2)}) collective-permute-start(f32[42,128,128]{2,1,0:T(8,128)} %bitcast.97), channel_id=1, source_target_pairs={{0,8},{8,0},{16,24},{24,16},{1,9},{9,1},{17,25},{25,17},{2,10},{10... | collective-permute-start | bytes 8257544 | tf_op jit(solution)/shard_map/ppermute | solution.py:24
  0.3 82.7 %collective-permute-start.5 = (f32[42,128,128]{2,1,0:T(8,128)}, f32[42,128,128]{2,1,0:T(8,128)}, u32[]{:S(2)}, u32[]{:S(2)}) collective-permute-start(f32[42,128,128]{2,1,0:T(8,128)} %bitcast.98), channel_id=1, source_target_pairs={{0,16},{8,24},{16,0},{24,8},{1,17},{9,25},{17,1},{25,9},{2,18},{10... | collective-permute-start | bytes 8257544 | tf_op jit(solution)/shard_map/ppermute | solution.py:24
  3.9 63.1 %collective-permute-start.11 = (f32[8,128,128]{2,1,0:T(8,128)}, f32[8,128,128]{2,1,0:T(8,128)S(1)}, u32[]{:S(2)}, u32[]{:S(2)}) collective-permute-start(f32[8,128,128]{2,1,0:T(8,128)} %gather_fusion.2), channel_id=1, source_target_pairs={{0,2},{1,3},{2,0},{3,1},{4,6},{5,7},{6,4},{7,5},{8,10},{9,11},{10,... | collective-permute-start | bytes 1572872 | tf_op jit(solution)/shard_map/ppermute | solution.py:24
  5.7 55.2 %collective-permute-start.1 = (s32[128]{0:T(128)S(1)}, s32[128]{0:T(128)S(1)}, u32[]{:S(2)}, u32[]{:S(2)}) collective-permute-start(s32[128]{0:T(128)S(1)} %pad_add_fusion.2), channel_id=1, source_target_pairs={{0,8},{8,0},{16,24},{24,16},{1,9},{9,1},{17,25},{25,17},{2,10},{10... | collective-permute-start | bytes 1544 | tf_op jit(solution)/shard_map/ppermute | solution.py:24
  12.9 49.6 %collective-permute-start.2 = (s32[128]{0:T(128)S(1)}, s32[128]{0:T(128)S(1)}, u32[]{:S(2)}, u32[]{:S(2)}) collective-permute-start(s32[128]{0:T(128)S(1)} %pad_add_fusion.2), channel_id=1, source_target_pairs={{0,16},{8,24},{16,0},{24,8},{1,17},{9,25},{17,1},{25,9},{2,18},{10... | collective-permute-start | bytes 1544 | tf_op jit(solution)/shard_map/ppermute | solution.py:24
  60.9 20.4 %collective-permute-start.14 = (f32[8,128,128]{2,1,0:T(8,128)}, f32[8,128,128]{2,1,0:T(8,128)}, u32[]{:S(2)}, u32[]{:S(2)}) collective-permute-start(f32[8,128,128]{2,1,0:T(8,128)} %gather_fusion.3), channel_id=1, source_target_pairs={{0,3},{1,2},{2,1},{3,0},{4,7},{5,6},{6,5},{7,4},{8,11},{9,10},{10,... | collective-permute-start | bytes 1572872 | tf_op jit(solution)/shard_map/ppermute | solution.py:24
  66.6 22.8 %collective-permute-start.16 = (f32[8,128,128]{2,1,0:T(8,128)}, f32[8,128,128]{2,1,0:T(8,128)}, u32[]{:S(2)}, u32[]{:S(2)}) collective-permute-start(f32[8,128,128]{2,1,0:T(8,128)} %gather_fusion.5), channel_id=1, source_target_pairs={{0,1},{1,0},{2,3},{3,2},{4,5},{5,4},{6,7},{7,6},{8,9},{9,8},{10,11... | collective-permute-start | bytes 1572872 | tf_op jit(solution)/shard_map/ppermute | solution.py:24
  67.0 41.9 %collective-permute-start.17 = (f32[8,128,128]{2,1,0:T(8,128)}, f32[8,128,128]{2,1,0:T(8,128)}, u32[]{:S(2)}, u32[]{:S(2)}) collective-permute-start(f32[8,128,128]{2,1,0:T(8,128)} %gather_fusion.6), channel_id=1, source_target_pairs={{0,4},{1,5},{2,6},{3,7},{4,0},{5,1},{6,2},{7,3},{8,12},{9,13},{10,... | collective-permute-start | bytes 1572872 | tf_op jit(solution)/shard_map/ppermute | solution.py:24
  81.3 38.9 %collective-permute-start.18 = (f32[8,128,128]{2,1,0:T(8,128)}, f32[8,128,128]{2,1,0:T(8,128)}, u32[]{:S(2)}, u32[]{:S(2)}) collective-permute-start(f32[8,128,128]{2,1,0:T(8,128)} %gather_fusion.7), channel_id=1, source_target_pairs={{0,5},{1,4},{2,7},{3,6},{4,1},{5,0},{6,3},{7,2},{8,13},{9,12},{10,... | collective-permute-start | bytes 1572872 | tf_op jit(solution)/shard_map/ppermute | solution.py:24
  82.9 38.5 %collective-permute-start.19 = (f32[8,128,128]{2,1,0:T(8,128)S(1)}, f32[8,128,128]{2,1,0:T(8,128)}, u32[]{:S(2)}, u32[]{:S(2)}) collective-permute-start(f32[8,128,128]{2,1,0:T(8,128)S(1)} %gather_fusion.4), channel_id=1, source_target_pairs={{0,7},{1,0},{2,1},{3,2},{4,3},{5,4},{6,5},{7,6},{8,15},{9,8},{10,9... | collective-permute-start | bytes 1572872 | tf_op jit(solution)/shard_map/ppermute | solution.py:24
  83.0 39.8 %collective-permute-start.21 = (f32[8,128,128]{2,1,0:T(8,128)}, f32[8,128,128]{2,1,0:T(8,128)}, u32[]{:S(2)}, u32[]{:S(2)}) collective-permute-start(f32[8,128,128]{2,1,0:T(8,128)} %gather_fusion.8), channel_id=1, source_target_pairs={{2,3},{6,7},{10,11},{14,15},{18,19},{22,23},{26,27},{30,31}} | collective-permute-start | bytes 1572872 | tf_op jit(solution)/shard_map/ppermute | solution.py:24
  89.4 106.5 %collective-permute-start.6 = (f32[21,128,128]{2,1,0:T(8,128)}, f32[21,128,128]{2,1,0:T(8,128)}, u32[]{:S(2)}, u32[]{:S(2)}) collective-permute-start(f32[21,128,128]{2,1,0:T(8,128)} %slice.41), channel_id=1, source_target_pairs={{0,16},{8,24},{16,0},{24,8},{1,17},{9,25},{17,1},{25,9},{2,18},{10... | collective-permute-start | bytes 4128776 | tf_op jit(solution)/shard_map/ppermute | solution.py:24
  108.9 89.0 %collective-permute-start.7 = (f32[21,128,128]{2,1,0:T(8,128)}, f32[21,128,128]{2,1,0:T(8,128)}, u32[]{:S(2)}, u32[]{:S(2)}) collective-permute-start(f32[21,128,128]{2,1,0:T(8,128)} %slice.42), channel_id=1, source_target_pairs={{0,8},{8,0},{16,24},{24,16},{1,9},{9,1},{17,25},{25,17},{2,10},{10... | collective-permute-start | bytes 4128776 | tf_op jit(solution)/shard_map/ppermute | solution.py:24
  122.8 40.3 %collective-permute-start.8 = (f32[8,128,128]{2,1,0:T(8,128)}, f32[8,128,128]{2,1,0:T(8,128)}, u32[]{:S(2)}, u32[]{:S(2)}) collective-permute-start(f32[8,128,128]{2,1,0:T(8,128)} %gather_fusion), channel_id=1, source_target_pairs={{0,6},{1,7},{2,4},{3,5},{4,2},{5,3},{6,0},{7,1},{8,14},{9,15},{10,... | collective-permute-start | bytes 1572872 | tf_op jit(solution)/shard_map/ppermute | solution.py:24
  134.4 55.5 %collective-permute-start.9 = (f32[8,128,128]{2,1,0:T(8,128)}, f32[8,128,128]{2,1,0:T(8,128)}, u32[]{:S(2)}, u32[]{:S(2)}) collective-permute-start(f32[8,128,128]{2,1,0:T(8,128)} %gather_fusion.1), channel_id=1, source_target_pairs={{0,7},{1,6},{2,5},{3,4},{4,3},{5,2},{6,1},{7,0},{8,15},{9,14},{10,... | collective-permute-start | bytes 1572872 | tf_op jit(solution)/shard_map/ppermute | solution.py:24
  138.2 52.8 %collective-permute-start.12 = (f32[8,128,128]{2,1,0:T(8,128)}, f32[8,128,128]{2,1,0:T(8,128)S(1)}, u32[]{:S(2)}, u32[]{:S(2)}) collective-permute-start(f32[8,128,128]{2,1,0:T(8,128)} %copy-done.4), channel_id=1, source_target_pairs={{0,7},{1,0},{2,1},{3,2},{4,3},{5,4},{6,5},{7,6},{8,15},{9,8},{10,9... | collective-permute-start | bytes 1572872 | tf_op jit(solution)/shard_map/ppermute | solution.py:24
  163.1 30.6 %collective-permute-start.15 = (f32[8,128,128]{2,1,0:T(8,128)}, f32[8,128,128]{2,1,0:T(8,128)}, u32[]{:S(2)}, u32[]{:S(2)}) collective-permute-start(f32[8,128,128]{2,1,0:T(8,128)} %collective-permute-done.14.refs_3_.refs_4_), channel_id=1, source_target_pairs={{0,7},{1,0},{2,1},{3,2},{4,3},{5,4},{6,5},{7,6},{8,15},{9,8},{10,9... | collective-permute-start | bytes 1572872 | tf_op jit(solution)/shard_map/ppermute | solution.py:24
  189.9 69.0 %collective-permute-start.20 = (f32[8,128,128]{2,1,0:T(8,128)}, f32[8,128,128]{2,1,0:T(8,128)}, u32[]{:S(2)}, u32[]{:S(2)}) collective-permute-start(f32[8,128,128]{2,1,0:T(8,128)} %collective-permute-done.16.refs_1_.refs_2_), channel_id=1, source_target_pairs={{0,7},{1,0},{2,1},{3,2},{4,3},{5,4},{6,5},{7,6},{8,15},{9,8},{10,9... | collective-permute-start | bytes 1572872 | tf_op jit(solution)/shard_map/ppermute | solution.py:24
  191.0 67.9 %collective-permute-start.22 = (f32[8,128,128]{2,1,0:T(8,128)}, f32[8,128,128]{2,1,0:T(8,128)}, u32[]{:S(2)}, u32[]{:S(2)}) collective-permute-start(f32[8,128,128]{2,1,0:T(8,128)} %collective-permute-done.17.refs_4_.refs_5_), channel_id=1, source_target_pairs={{1,0},{2,1},{3,2},{5,4},{6,5},{7,6},{9,8},{10,9},{11,10},{13,12},{... | collective-permute-start | bytes 1572872 | tf_op jit(solution)/shard_map/ppermute | solution.py:24
  193.7 65.2 %collective-permute-start.24 = (f32[8,128,128]{2,1,0:T(8,128)}, f32[8,128,128]{2,1,0:T(8,128)}, u32[]{:S(2)}, u32[]{:S(2)}) collective-permute-start(f32[8,128,128]{2,1,0:T(8,128)} %collective-permute-done.18.refs_5_.refs_6_), channel_id=1, source_target_pairs={{1,0},{2,1},{3,2},{5,4},{6,5},{7,6},{9,8},{10,9},{11,10},{13,12},{... | collective-permute-start | bytes 1572872 | tf_op jit(solution)/shard_map/ppermute | solution.py:24
  195.9 84.4 %collective-permute-start.10 = (f32[8,128,128]{2,1,0:T(8,128)}, f32[8,128,128]{2,1,0:T(8,128)}, u32[]{:S(2)}, u32[]{:S(2)}) collective-permute-start(f32[8,128,128]{2,1,0:T(8,128)} %collective-permute-done.8.refs_1_), channel_id=1, source_target_pairs={{1,0},{2,1},{3,2},{5,4},{6,5},{7,6},{9,8},{10,9},{11,10},{13,12},{... | collective-permute-start | bytes 1572872 | tf_op jit(solution)/shard_map/ppermute | solution.py:24
  198.0 82.3 %collective-permute-start.13 = (f32[8,128,128]{2,1,0:T(8,128)}, f32[8,128,128]{2,1,0:T(8,128)}, u32[]{:S(2)}, u32[]{:S(2)}) collective-permute-start(f32[8,128,128]{2,1,0:T(8,128)} %collective-permute-done.9.refs_2_), channel_id=1, source_target_pairs={{1,0},{2,1},{3,2},{5,4},{6,5},{7,6},{9,8},{10,9},{11,10},{13,12},{... | collective-permute-start | bytes 1572872 | tf_op jit(solution)/shard_map/ppermute | solution.py:24
  290.9 34.1 %collective-permute-start.33 = (f32[4,128,128]{2,1,0:T(8,128)S(1)}, f32[4,128,128]{2,1,0:T(8,128)S(1)}, u32[]{:S(2)}, u32[]{:S(2)}) collective-permute-start(f32[4,128,128]{2,1,0:T(8,128)S(1)} %get-tuple-element.38), channel_id=1, source_target_pairs={{0,1},{1,0},{2,3},{3,2},{4,5},{5,4},{6,7},{7,6},{8,9},{9,8},{10,11... | collective-permute-start | bytes 786440 | tf_op jit(solution)/shard_map/ppermute | solution.py:24
  325.0 27.4 %collective-permute-start.38 = (f32[4,128,128]{2,1,0:T(8,128)S(1)}, f32[4,128,128]{2,1,0:T(8,128)S(1)}, u32[]{:S(2)}, u32[]{:S(2)}) collective-permute-start(f32[4,128,128]{2,1,0:T(8,128)S(1)} %get-tuple-element.43), channel_id=1, source_target_pairs={{0,6},{1,7},{2,4},{3,5},{4,2},{5,3},{6,0},{7,1},{8,14},{9,15},{10,... | collective-permute-start | bytes 786440 | tf_op jit(solution)/shard_map/ppermute | solution.py:24
  325.0 40.1 %collective-permute-start.39 = (f32[4,128,128]{2,1,0:T(8,128)S(1)}, f32[4,128,128]{2,1,0:T(8,128)S(1)}, u32[]{:S(2)}, u32[]{:S(2)}) collective-permute-start(f32[4,128,128]{2,1,0:T(8,128)S(1)} %get-tuple-element.44), channel_id=1, source_target_pairs={{0,7},{1,6},{2,5},{3,4},{4,3},{5,2},{6,1},{7,0},{8,15},{9,14},{10,... | collective-permute-start | bytes 786440 | tf_op jit(solution)/shard_map/ppermute | solution.py:24
  329.3 35.8 %collective-permute-start.26 = (f32[4,128,128]{2,1,0:T(8,128)S(1)}, f32[4,128,128]{2,1,0:T(8,128)S(1)}, u32[]{:S(2)}, u32[]{:S(2)}) collective-permute-start(f32[4,128,128]{2,1,0:T(8,128)S(1)} %get-tuple-element.30), channel_id=1, source_target_pairs={{0,1},{1,0},{2,3},{3,2},{4,5},{5,4},{6,7},{7,6},{8,9},{9,8},{10,11... | collective-permute-start | bytes 786440 | tf_op jit(solution)/shard_map/ppermute | solution.py:24
  329.4 35.8 %collective-permute-start.27 = (f32[4,128,128]{2,1,0:T(8,128)S(1)}, f32[4,128,128]{2,1,0:T(8,128)S(1)}, u32[]{:S(2)}, u32[]{:S(2)}) collective-permute-start(f32[4,128,128]{2,1,0:T(8,128)S(1)} %get-tuple-element.31), channel_id=1, source_target_pairs={{0,2},{1,3},{2,0},{3,1},{4,6},{5,7},{6,4},{7,5},{8,10},{9,11},{10,... | collective-permute-start | bytes 786440 | tf_op jit(solution)/shard_map/ppermute | solution.py:24
  331.4 34.4 %collective-permute-start.28 = (f32[4,128,128]{2,1,0:T(8,128)S(1)}, f32[4,128,128]{2,1,0:T(8,128)S(1)}, u32[]{:S(2)}, u32[]{:S(2)}) collective-permute-start(f32[4,128,128]{2,1,0:T(8,128)S(1)} %get-tuple-element.32), channel_id=1, source_target_pairs={{0,3},{1,2},{2,1},{3,0},{4,7},{5,6},{6,5},{7,4},{8,11},{9,10},{10,... | collective-permute-start | bytes 786440 | tf_op jit(solution)/shard_map/ppermute | solution.py:24
  352.4 32.4 %collective-permute-start.29 = (f32[4,128,128]{2,1,0:T(8,128)S(1)}, f32[4,128,128]{2,1,0:T(8,128)S(1)}, u32[]{:S(2)}, u32[]{:S(2)}) collective-permute-start(f32[4,128,128]{2,1,0:T(8,128)S(1)} %get-tuple-element.33), channel_id=1, source_target_pairs={{0,4},{1,5},{2,6},{3,7},{4,0},{5,1},{6,2},{7,3},{8,12},{9,13},{10,... | collective-permute-start | bytes 786440 | tf_op jit(solution)/shard_map/ppermute | solution.py:24
  365.1 25.4 %collective-permute-start.30 = (f32[4,128,128]{2,1,0:T(8,128)S(1)}, f32[4,128,128]{2,1,0:T(8,128)S(1)}, u32[]{:S(2)}, u32[]{:S(2)}) collective-permute-start(f32[4,128,128]{2,1,0:T(8,128)S(1)} %get-tuple-element.34), channel_id=1, source_target_pairs={{0,5},{1,4},{2,7},{3,6},{4,1},{5,0},{6,3},{7,2},{8,13},{9,12},{10,... | collective-permute-start | bytes 786440 | tf_op jit(solution)/shard_map/ppermute | solution.py:24
  365.1 32.3 %collective-permute-start.31 = (f32[4,128,128]{2,1,0:T(8,128)S(1)}, f32[4,128,128]{2,1,0:T(8,128)S(1)}, u32[]{:S(2)}, u32[]{:S(2)}) collective-permute-start(f32[4,128,128]{2,1,0:T(8,128)S(1)} %get-tuple-element.35), channel_id=1, source_target_pairs={{0,6},{1,7},{2,4},{3,5},{4,2},{5,3},{6,0},{7,1},{8,14},{9,15},{10,... | collective-permute-start | bytes 786440 | tf_op jit(solution)/shard_map/ppermute | solution.py:24
  365.2 38.4 %collective-permute-start.32 = (f32[4,128,128]{2,1,0:T(8,128)S(1)}, f32[4,128,128]{2,1,0:T(8,128)S(1)}, u32[]{:S(2)}, u32[]{:S(2)}) collective-permute-start(f32[4,128,128]{2,1,0:T(8,128)S(1)} %get-tuple-element.36), channel_id=1, source_target_pairs={{0,7},{1,6},{2,5},{3,4},{4,3},{5,2},{6,1},{7,0},{8,15},{9,14},{10,... | collective-permute-start | bytes 786440 | tf_op jit(solution)/shard_map/ppermute | solution.py:24
  (39 other events, 950.7 us)

commit v3 on v2

--- a/solution.py
+++ b/solution.py
@@ -37,7 +37,7 @@
     return direct + [mask for mask in range(rows) if mask not in direct]
 
 
-def plan_body(sizes, place_ref, triple_ref, left_ref, left_next_ref, table_ref, code_ref, slot_ref, bound_ref,
+def plan_body(sizes, place_ref, triple_ref, left_ref, left_next_ref, table_ref, code_ref, bound_ref,
               block_ref, left_at, right_at, out_at, raw_code, raw_key, count_ref):
     rows, cols, own, per_left, per_right, panel, pairs = sizes
     row, col = place_ref[0], place_ref[1]
@@ -90,13 +90,13 @@
             block_ref[stop * 2 * panel + index] = jnp.where(there, rank * own + block, 0)
         return 0
 
-    lax.fori_loop(0, 2 * panel, tables, 0)
+    lax.fori_loop(0, 2 * panel, tables, 0, unroll=2)
 
     def clear(index, _):
         count_ref[index] = 0
         return 0
 
-    lax.fori_loop(0, 3 * slots + 1, clear, 0)
+    lax.fori_loop(0, 3 * slots + 8, clear, 0, unroll=8)
     total = jnp.int32(0)
     for stop in range(2):
         for image in range(2):
@@ -113,7 +113,7 @@
                     chapter = (code >> RELAY) & 1 if stop == 0 else 1
                     chapter = jnp.where(((code >> LATE) & 1) == 1, 2, chapter)
                     key = jnp.where(live, spot + chapter * slots, 3 * slots)
-                    raw_code[found] = code & ((1 << LATE) - 1)
+                    raw_code[found] = (code & ((1 << LATE) - 1)) + (spot << LATE)
                     raw_key[found] = key
                     count_ref[key] = count_ref[key] + 1
                     found = found + live.astype(jnp.int32)
@@ -122,35 +122,23 @@
             total = lax.fori_loop(0, pairs // READ, read, total)
 
     def fill(index, _):
-        code_ref[index] = 0
+        code_ref[index] = slots << LATE
         return 0
 
     lax.fori_loop(0, code_ref.shape[0], fill, 0, unroll=16)
 
-    def idle(index, _):
-        slot_ref[index] = slots
-        return 0
-
-    lax.fori_loop(0, slot_ref.shape[0], idle, 0, unroll=16)
-
-    def prefix(key, group):
-        groups = (count_ref[key] + GROUP - 1) // GROUP
-
-        def label(index, _):
-            slot_ref[index] = lax.rem(key, slots)
-            return 0
-
-        lax.fori_loop(group, group + groups, label, 0)
-        count_ref[key] = group * GROUP
-        return group + groups
+    def prefix(key, start):
+        count = count_ref[key]
+        count_ref[key] = start
+        return start + (count + GROUP - 1) // GROUP * GROUP
 
     done = jnp.int32(0)
     bound_ref[0] = 0
     cuts = (0, slots, 2 * slots, 2 * slots + slots // 2, 3 * slots)
     for part, (low, high) in enumerate(zip(cuts[:-1], cuts[1:])):
-        done = lax.fori_loop(low, high, prefix, done)
-        done = (done + UNROLL - 1) // UNROLL * UNROLL
-        bound_ref[part + 1] = done // UNROLL
+        done = lax.fori_loop(low, high, prefix, done, unroll=8)
+        done = (done + GROUP * UNROLL - 1) // (GROUP * UNROLL) * (GROUP * UNROLL)
+        bound_ref[part + 1] = done // (GROUP * UNROLL)
 
     def place(index, _):
         key = raw_key[index]
@@ -165,18 +153,17 @@
 def make_plan(place, triples, left_place, left_next, table, sizes):
     _, cols, _, per_left, _, panel, pairs = sizes
     slots = cols * per_left
-    groups = 4 * pairs // GROUP + 3 * slots + 4 * UNROLL
-    groups = (groups + 31) // 32 * 32
+    room = 4 * pairs + 3 * slots * (GROUP - 1) + 4 * GROUP * UNROLL
+    room = (room + 127) // 128 * 128
     return pl.pallas_call(
         functools.partial(plan_body, sizes),
         out_shape=(
-            jax.ShapeDtypeStruct((groups * GROUP,), jnp.int32),
-            jax.ShapeDtypeStruct((groups,), jnp.int32),
+            jax.ShapeDtypeStruct((room,), jnp.int32),
             jax.ShapeDtypeStruct((5,), jnp.int32),
             jax.ShapeDtypeStruct((4 * panel,), jnp.int32),
         ),
         in_specs=[SMEM] * 5,
-        out_specs=(SMEM,) * 4,
+        out_specs=(SMEM,) * 3,
         scratch_shapes=[
             pltpu.SMEM((4 * (panel + 1),), jnp.int32),
             pltpu.SMEM((4 * (panel + 1),), jnp.int32),
@@ -193,6 +180,77 @@
 def halves(value):
     high = value.astype(jnp.bfloat16)
     return high, (value - high.astype(jnp.float32)).astype(jnp.bfloat16)
+
+
+def take_body(masks, place_ref, list_ref, blocks_ref, *refs):
+    outs, (held, in_sems, out_sems) = refs[: len(masks)], refs[len(masks) :]
+    col = place_ref[1]
+    cols, per_left = list_ref.shape
+    for bucket, mask in enumerate(masks):
+        peer = jnp.where(col < cols // 2, cols // 2, 0) if mask is None else col ^ mask
+        for within in range(per_left):
+            block = jnp.maximum(list_ref[peer, within], 0)
+            pltpu.make_async_copy(blocks_ref.at[block], held.at[bucket, within], in_sems.at[bucket]).start()
+    stores = []
+    for bucket in range(len(masks)):
+        pltpu.make_async_copy(held.at[bucket], held.at[bucket], in_sems.at[bucket]).wait()
+        stores.append(pltpu.make_async_copy(held.at[bucket], outs[bucket], out_sems.at[bucket]))
+        stores[-1].start()
+    for store in stores:
+        store.wait()
+
+
+def take(masks, place, left_list, left_own):
+    per_left, size = left_list.shape[1], left_own.shape[-1]
+    return pl.pallas_call(
+        functools.partial(take_body, masks),
+        out_shape=[jax.ShapeDtypeStruct((per_left, size, size), jnp.float32)] * len(masks),
+        in_specs=[SMEM] * 2 + [HBM],
+        out_specs=[HBM] * len(masks),
+        scratch_shapes=[
+            pltpu.VMEM((len(masks), per_left, size, size), jnp.float32),
+            pltpu.SemaphoreType.DMA((len(masks),)),
+            pltpu.SemaphoreType.DMA((len(masks),)),
+        ],
+        compiler_params=pltpu.CompilerParams(vmem_limit_bytes=48 * 1024 * 1024),
+        name="take",
+    )(place, left_list, left_own)
+
+
+def part_body(starts, *refs):
+    count = len(starts)
+    sources, outs, (held, in_sems, out_sems) = refs[:count], refs[count : 2 * count], refs[2 * count :]
+    fetches, stores = [], []
+    for index, start in enumerate(starts):
+        length = outs[index].shape[0]
+        target = held.at[index, pl.ds(0, length)]
+        fetches.append(pltpu.make_async_copy(sources[index].at[pl.ds(start, length)], target, in_sems.at[index]))
+        stores.append(pltpu.make_async_copy(target, outs[index], out_sems.at[index]))
+    for fetch in fetches:
+        fetch.start()
+    for fetch, store in zip(fetches, stores):
+        fetch.wait()
+        store.start()
+    for store in stores:
+        store.wait()
+
+
+def parted(wanted):
+    size = wanted[0][0].shape[-1]
+    longest = max(stop - start for _, start, stop in wanted)
+    return pl.pallas_call(
+        functools.partial(part_body, [start for _, start, _ in wanted]),
+        out_shape=[jax.ShapeDtypeStruct((stop - start, size, size), jnp.float32) for _, start, stop in wanted],
+        in_specs=[HBM] * len(wanted),
+        out_specs=[HBM] * len(wanted),
+        scratch_shapes=[
+            pltpu.VMEM((len(wanted), longest, size, size), jnp.float32),
+            pltpu.SemaphoreType.DMA((len(wanted),)),
+            pltpu.SemaphoreType.DMA((len(wanted),)),
+        ],
+        compiler_params=pltpu.CompilerParams(vmem_limit_bytes=48 * 1024 * 1024),
+        name="parted",
+    )(*[array for array, _, _ in wanted])
 
 
 DEPTH = 8
@@ -257,7 +315,7 @@
     )(*[piece for piece, _ in pieces])
 
 
-def multiply_body(mode, part, kinds, sizes, place_ref, code_ref, slot_ref, bound_ref, block_ref, right_ref, *refs):
+def multiply_body(mode, part, kinds, sizes, place_ref, code_ref, bound_ref, block_ref, right_ref, *refs):
     _, cols, _, per_left, _, _, _ = sizes
     slots = cols * per_left
     half = per_left // 2
@@ -328,20 +386,22 @@
         carried.wait()
 
     def multiply(step, _):
+        made = []
         for lane in range(UNROLL):
-            group = step * UNROLL + lane
-            spot = jnp.minimum(slot_ref[group] - first, spots)
+            start = (step * UNROLL + lane) * GROUP
+            codes = [code_ref[start + index] for index in range(GROUP)]
             parts_left, parts_right = [], []
-            for index in range(GROUP):
-                code = code_ref[group * GROUP + index]
-                parts_left.append(lefts[code // SHIFT])
-                block = rights[lax.rem(code, SHIFT)]
+            for code in codes:
+                parts_left.append(lefts[(code & ((1 << LATE) - 1)) // SHIFT])
+                block = rights[code & (SHIFT - 1)]
                 parts_right += [block, block]
             product = jnp.dot(
                 jnp.concatenate(parts_left, axis=1),
                 jnp.concatenate(parts_right, axis=0),
                 preferred_element_type=jnp.float32,
             )
+            made.append((jnp.minimum((codes[0] >> LATE) - first, spots), product))
+        for spot, product in made:
             total[spot] += product[:, 0:size] + product[:, size : 2 * size]
         return 0
 
@@ -377,7 +437,7 @@
     return pl.pallas_call(
         functools.partial(multiply_body, mode, part, [len(entry) - 1 for entry in lefts], sizes),
         out_shape=out_shape,
-        in_specs=[SMEM] * 5 + [HBM] * (len(rights) + len(arrays)),
+        in_specs=[SMEM] * 4 + [HBM] * (len(rights) + len(arrays)),
         out_specs=out_specs,
         scratch_shapes=[
             pltpu.VMEM((len(lefts) * per_left + 1, size, 2 * size), jnp.bfloat16),
@@ -394,39 +454,49 @@
     )(place, *plan, *rights, *arrays)
 
 
-def collect_body(sizes, place_ref, list_ref, *refs):
+def collect_body(part, sizes, place_ref, list_ref, *refs):
     _, cols, _, per_left, _, _, _ = sizes
     half = per_left // 2
-    sources, out_ref, whole, sem, out_sem = refs[: 2 * cols], *refs[2 * cols :]
-    for part in range(2):
-        for bucket in range(cols):
-            for within in range(half):
-                block = list_ref[place_ref[1] ^ bucket, part * half + within]
-
-                @pl.when(block >= 0)
-                def _():
-                    pltpu.make_async_copy(sources[part * cols + bucket].at[within], whole.at[block], sem).start()
-
-    pltpu.make_async_copy(out_ref, whole, sem).wait()
-    result = pltpu.make_async_copy(whole, out_ref, out_sem)
-    result.start()
-    result.wait()
-
-
-def collected(sizes, place, left_list, backs):
-    own, size = sizes[2], backs[0].shape[-1]
+    sources, (out_ref, held, in_sems, out_sems) = refs[:cols], refs[-4:]
+    slots = [(bucket, within) for bucket in range(cols) for within in range(half)]
+
+    def each(action):
+        for index, (bucket, within) in enumerate(slots):
+            block = list_ref[place_ref[1] ^ bucket, part * half + within]
+
+            @pl.when(block >= 0)
+            def _():
+                action(
+                    pltpu.make_async_copy(sources[bucket].at[within], held.at[index], in_sems.at[index]),
+                    pltpu.make_async_copy(held.at[index], out_ref.at[block], out_sems.at[index]),
+                )
+
+    def forward(fetch, store):
+        fetch.wait()
+        store.start()
+
+    each(lambda fetch, store: fetch.start())
+    each(forward)
+    each(lambda fetch, store: store.wait())
+
+
+def collected(part, sizes, place, left_list, backs, before):
+    _, cols, own, per_left, _, _, _ = sizes
+    size = backs[0].shape[-1]
+    slots = cols * per_left // 2
+    held = [] if before is None else [before]
     return pl.pallas_call(
-        functools.partial(collect_body, sizes),
+        functools.partial(collect_body, part, sizes),
         out_shape=jax.ShapeDtypeStruct((own, size, size), jnp.float32),
-        in_specs=[SMEM] * 2 + [HBM] * len(backs),
+        in_specs=[SMEM] * 2 + [HBM] * (len(backs) + len(held)),
         out_specs=HBM,
+        input_output_aliases={2 + len(backs): 0} if held else {},
         scratch_shapes=[
-            pltpu.VMEM((own, size, size), jnp.float32),
-            pltpu.SemaphoreType.DMA,
-            pltpu.SemaphoreType.DMA,
+            pltpu.VMEM((slots, size, size), jnp.float32),
+            pltpu.SemaphoreType.DMA((slots,)),
+            pltpu.SemaphoreType.DMA((slots,)),
         ],
-        name="collect",
-    )(place, left_list, *backs)
+    )(place, left_list, *backs, *held)
 
 
 def send_order(cols):
@@ -462,22 +532,23 @@
     whole, low, high = {0: right_own}, {}, {}
     for mask in masks:
         whole[mask] = moved(right_own, "row", lambda source: source ^ mask)
-        low[mask], high[mask] = whole[mask][:cut], whole[mask][cut:]
-    for key in range(rows):
-        if key not in whole:
-            top, bottom = 1 << (key.bit_length() - 1), key & -key
-            low[key] = moved(low[key ^ top], "row", lambda source: source ^ top)
-            high[key] = moved(high[key ^ bottom], "row", lambda source: source ^ bottom)
-
-    def bucket_for(peer):
-        return left_own[jnp.clip(left_list[peer], 0, own - 1)]
-
+    relays = [(key, 1 << (key.bit_length() - 1), key & -key) for key in right_order(rows)[len(whole) :]]
+    lows = sorted({key ^ top for key, top, _ in relays} & set(masks))
+    highs = sorted({key ^ bottom for key, _, bottom in relays} & set(masks))
+    parts = parted([(whole[mask], 0, cut) for mask in lows] + [(whole[mask], cut, own) for mask in highs])
+    low.update(zip(lows, parts[: len(lows)]))
+    high.update(zip(highs, parts[len(lows) :]))
+    for key, top, bottom in relays:
+        low[key] = moved(low[key ^ top], "row", lambda source: source ^ top)
+        high[key] = moved(high[key ^ bottom], "row", lambda source: source ^ bottom)
+
+    order = send_order(cols)
+    taken = list(take(order[:2], place, left_list, left_own))
+    taken += list(take(order[2:] + [0, None], place, left_list, left_own))
     here = {}
-    for mask in send_order(cols):
-        bucket = bucket_for(col ^ mask)
-        here[mask] = moved(bucket, "col", lambda source: source ^ mask)
-    here[0] = bucket_for(col)
-    extra = {0: bucket_for(jnp.where(col < middle, middle, 0))}
+    for index, mask in enumerate(order):
+        here[mask] = moved(taken[index], "col", lambda source: source ^ mask)
+    here[0], extra = taken[-2], {0: taken[-1]}
     for mask in range(1, middle):
         extra[mask] = moved(
             extra[0], "col", lambda source: source ^ mask, [(middle - 1) ^ mask, (cols - 1) ^ mask]
@@ -503,14 +574,17 @@
     late += [(there[mask], there[mask - middle]) for mask in range(3 * quarter, cols)]
     before = multiplied(0, 0, sizes, place, plan, rights, first)
     before = multiplied(1, 0, sizes, place, plan, rights, second, before)
+    result = None
     backs = []
     for part in range(2):
         product = multiplied(2, part, sizes, place, plan, rights, late, before)
         returned = {0: product[0]}
         for mask in list(range(middle, cols)) + list(range(1, middle)):
             returned[mask] = moved(product[mask], "col", lambda source: source ^ mask)
-        backs += [returned[mask] for mask in range(cols)]
-    return collected(sizes, place, left_list, backs)[None, None]
+        backs.append([returned[mask] for mask in range(cols)])
+    for part in range(2):
+        result = collected(part, sizes, place, left_list, backs[part], result)
+    return result[None, None]
 
 
 def solution(mesh):

time: 409 us -> 365 us (0.89)
  waiting for transfers between devices: 200 us -> 164 us
  local copies, waits for them, and re-layouts: 26.4 us -> 7.58 us
  starting transfers between devices: 82.5 us -> 92.1 us
    ppermute x40, waiting for transfers between devices: 200 us -> 164 us  [moved(): lax.ppermute(value, axis, [(source, target(source)) for source in places])]
    gather x9 -> x0, local copies, waits for them, and re-layouts: 11.8 us -> none  [bucket_for(): return left_own[jnp.clip(left_list[peer], 0, own - 1)]]
    pallas_call x1 -> x5, Pallas kernels: 4.07 us -> 14.7 us  [the longest x2 6.58 us: collected(): pl.pallas_call(functools.partial(collect_body, part, sizes), out_shape=ja...]
    ppermute x40, starting transfers between devices: 82.5 us -> 92.1 us  [moved(): lax.ppermute(value, axis, [(source, target(source)) for source in places])]
    slice x2 -> x0, local copies, waits for them, and re-layouts: 5.14 us -> none  [local(): low[mask], high[mask] = (whole[mask][:cut], whole[mask][cut:])]
    pallas_call x4, Pallas kernels: 50 us -> 45.3 us  [multiplied(): pl.pallas_call(functools.partial(multiply_body, mode, part, [len(entry) -...]
    pallas_call x1, Pallas kernels: 33.4 us -> 29 us  [make_plan(): pl.pallas_call(functools.partial(plan_body, sizes), out_shape=(jax.ShapeD...]
  transfers between devices with their start and end apart: 40 -> 40, of which waited for: 15 -> 16; matrix products, arithmetic and copies ran while one was open for 5% -> 0% of each run, Pallas kernels for 20% -> 24%
where the time goes in v3:
time: 365 us; the launch traced here: 364 us
  waiting for transfers between devices  164 us (45%)
  Pallas kernels  98.5 us (27%)
  starting transfers between devices  92.1 us (25%)
  local copies, waits for them, and re-layouts  7.58 us (2%)
    ppermute x40, waiting for transfers between devices, moved(): lax.ppermute(value, axis, [(source, target(source)) for source in places])  164 us
    ppermute x40, starting transfers between devices, moved(): lax.ppermute(value, axis, [(source, target(source)) for source in places])  92.1 us
    pallas_call x4, Pallas kernels, multiplied(): pl.pallas_call(functools.partial(multiply_body, mode, part, [len(entry) -...  45.3 us
    pallas_call x1, Pallas kernels, make_plan(): pl.pallas_call(functools.partial(plan_body, sizes), out_shape=(jax.ShapeD...  29 us
    pallas_call x2, Pallas kernels, split(): pl.pallas_call(functools.partial(split_body, [base for _, base in pieces]...  9.47 us
  transfers between devices with their start and end apart: 40, of which 16 were waited for; matrix products, arithmetic and copies ran while one was open for 0% of the time, Pallas kernels for 24%

profile of v3, /device:TPU:11, one launch (start us, length us, event | category | flops | bytes accessed | tf_op | source)
XLA Modules:
  0.0 364.0 jit_solution(8980262381697531499)
XLA Ops:
  4.1 3.1 take.3
  11.8 22.2 %collective-permute-done.left_next_ref = s32[2,32]{1,0:T(2,128)S(1)} collective-permute-done((s32[2,32]{1,0:T(2,128)S(1)}, s32[2,32]{1,0:T(2,128)S(1)}, u32[]{:S(2)}, u32[]{:S(2)}) %collective-permute-start) | collective-permute-done | bytes 288 | tf_op jit(solution)/shard_map/ppermute | solution.py:24
  35.2 26.7 %collective-permute-done.1 = s32[128]{0:T(128)S(1)} collective-permute-done((s32[128]{0:T(128)S(1)}, s32[128]{0:T(128)S(1)}, u32[]{:S(2)}, u32[]{:S(2)}) %collective-permute-start.1) | collective-permute-done | bytes 544 | tf_op jit(solution)/shard_map/ppermute | solution.py:24
  64.6 3.3 take.2
  69.2 3.6 collective-permute-start.9
  79.6 25.8 %collective-permute-done.8.refs_1_ = f32[8,128,128]{2,1,0:T(8,128)S(1)} collective-permute-done((f32[8,128,128]{2,1,0:T(8,128)S(1)}, f32[8,128,128]{2,1,0:T(8,128)S(1)}, u32[]{:S(2)}, u32[]{:S(2)}) %collective-permute-start.8) | collective-permute-done | bytes 524320 | tf_op jit(solution)/shard_map/ppermute | solution.py:24
  107.3 22.0 %collective-permute-done.9.refs_2_ = f32[8,128,128]{2,1,0:T(8,128)} collective-permute-done((f32[8,128,128]{2,1,0:T(8,128)S(1)}, f32[8,128,128]{2,1,0:T(8,128)}, u32[]{:S(2)}, u32[]{:S(2)}) %collective-permute-start.9) | collective-permute-done | bytes 524320 | tf_op jit(solution)/shard_map/ppermute | solution.py:24
  129.8 5.0 %collective-permute-start.19 = (f32[8,128,128]{2,1,0:T(8,128)S(1)}, f32[8,128,128]{2,1,0:T(8,128)S(1)}, u32[]{:S(2)}, u32[]{:S(2)}) collective-permute-start(f32[8,128,128]{2,1,0:T(8,128)S(1)} %get-tuple-element.44.refs_0_.refs_1_), channel_id=1, source_target_pairs={{0,7},{1,0},{2,1},{3,2},{4,3},{5,4},{6,5},{7,6},{8,15},{9,8},{10,9... | collective-permute-start | bytes 1572872 | tf_op jit(solution)/shard_map/ppermute | solution.py:24
  136.1 4.5 %collective-permute-done.18.refs_5_.refs_6_ = f32[8,128,128]{2,1,0:T(8,128)} collective-permute-done((f32[8,128,128]{2,1,0:T(8,128)S(1)}, f32[8,128,128]{2,1,0:T(8,128)}, u32[]{:S(2)}, u32[]{:S(2)}) %collective-permute-start.18) | collective-permute-done | bytes 524320 | tf_op jit(solution)/shard_map/ppermute | solution.py:24
  147.1 4.1 %collective-permute-done.23.refs_14_ = f32[8,128,128]{2,1,0:T(8,128)S(1)} collective-permute-done((f32[8,128,128]{2,1,0:T(8,128)S(1)}, f32[8,128,128]{2,1,0:T(8,128)S(1)}, u32[]{:S(2)}, u32[]{:S(2)}) %collective-permute-start.23) | collective-permute-done | bytes 524320 | tf_op jit(solution)/shard_map/ppermute | solution.py:24
  154.7 3.5 collective-permute-done.12.refs_9_.refs_4_
  160.1 3.1 collective-permute-start.20
  163.2 3.9 %collective-permute-start.24 = (f32[8,128,128]{2,1,0:T(8,128)}, f32[8,128,128]{2,1,0:T(8,128)}, u32[]{:S(2)}, u32[]{:S(2)}) collective-permute-start(f32[8,128,128]{2,1,0:T(8,128)} %collective-permute-done.18.refs_5_.refs_6_), channel_id=1, source_target_pairs={{1,0},{2,1},{3,2},{5,4},{6,5},{7,6},{9,8},{10,9},{11,10},{13,12},{... | collective-permute-start | bytes 1572872 | tf_op jit(solution)/shard_map/ppermute | solution.py:24
  168.4 29.0 %plan.1 = (s32[2176]{0:T(1024)}, s32[5]{0:T(128)}, s32[128]{0:T(128)}) custom-call(s32[2]{0:T(128)} %copy-done.13, s32[1536]{0:T(1024)} %add.26.triple_ref, s32[2,32]{1,0:T(2,128)} %bitcast.28, s32[2,32]{1,0:T(2,128)} %copy-done.41, s32[4,128]{1,0:T(4,128)} %pad_add_fusion.table_ref), custom_call_target="tpu_custom_call" | custom-call | flops 40000000 | bytes 60000000 | tf_op jit(solution)/shard_map/plan/pallas_call | solution.py:158
  197.5 6.7 %split.2.right_ref = bf16[126,128,256]{2,1,0:T(8,128)(2,1)} custom-call(f32[42,128,128]{2,1,0:T(8,128)} %bitcast.24, f32[42,128,128]{2,1,0:T(8,128)} %copy-done.1, f32[42,128,128]{2,1,0:T(8,128)} %collective-permute-done.5.refs_2_.refs_1_), custom_call_target="tpu_custom_call" | custom-call | bytes 16515072 | tf_op jit(solution)/shard_map/split/pallas_call | solution.py:302
  204.2 10.5 %shard_map.73.refs_17_ = f32[64,128,128]{2,1,0:T(8,128)} custom-call(s32[2]{0:T(128)S(1)} %copy-done.14, s32[2176]{0:T(1024)S(1)} %copy-done.10, s32[5]{0:T(128)S(1)} %copy-done.15, s32[128]{0:T(128)S(1)} %copy-done.16, bf16[126,128,256]{2,1,0:T(8,128)(2,1)} %split.2.right_ref, f32[8,128,128]{2,1,0:T(8,128)S(1)} %copy-done.3, ...), custom_call_target="tpu_custom_call" | custom-call | bytes 16777216 | tf_op jit(solution)/shard_map/pallas_call | solution.py:437
  214.7 2.8 split.3.refs_0_
  219.6 17.1 %shard_map.74.refs_7_ = f32[64,128,128]{2,1,0:T(8,128)} custom-call(s32[2]{0:T(128)S(1)} %copy-done.14, s32[2176]{0:T(1024)S(1)} %copy-done.10, s32[5]{0:T(128)S(1)} %copy-done.15, s32[128]{0:T(128)S(1)} %copy-done.16, bf16[126,128,256]{2,1,0:T(8,128)(2,1)} %split.2.right_ref, bf16[42,128,256]{2,1,0:T(8,128)(2,1)} %split.3.refs_0_, ...), custom_call_target="tpu_custom_call" | custom-call | bytes 16777216 | tf_op jit(solution)/shard_map/pallas_call | solution.py:437
  236.7 8.5 %shard_map.76 = (f32[4,128,128]{2,1,0:T(8,128)S(1)}, f32[4,128,128]{2,1,0:T(8,128)S(1)}, f32[4,128,128]{2,1,0:T(8,128)S(1)}, f32[4,128,128]{2,1,0:T(8,128)S(1)},...) custom-call(s32[2]{0:T(128)S(1)} %copy-done.14, ...), custom_call_target="tpu_custom_call" | custom-call | bytes 16777216 | tf_op jit(solution)/shard_map/pallas_call | solution.py:437
  245.9 20.5 %collective-permute-start.33 = (f32[4,128,128]{2,1,0:T(8,128)S(1)}, f32[4,128,128]{2,1,0:T(8,128)S(1)}, u32[]{:S(2)}, u32[]{:S(2)}) collective-permute-start(f32[4,128,128]{2,1,0:T(8,128)S(1)} %get-tuple-element.58), channel_id=1, source_target_pairs={{0,1},{1,0},{2,3},{3,2},{4,5},{5,4},{6,7},{7,6},{8,9},{9,8},{10,11... | collective-permute-start | bytes 786440 | tf_op jit(solution)/shard_map/ppermute | solution.py:24
  270.8 9.3 %shard_map.75 = (f32[4,128,128]{2,1,0:T(8,128)S(1)}, f32[4,128,128]{2,1,0:T(8,128)S(1)}, f32[4,128,128]{2,1,0:T(8,128)S(1)}, f32[4,128,128]{2,1,0:T(8,128)}, f32...) custom-call(s32[2]{0:T(128)S(1)} %copy-done.14, ...), custom_call_target="tpu_custom_call" | custom-call | bytes 16777216 | tf_op jit(solution)/shard_map/pallas_call | solution.py:437
  280.2 3.4 collective-permute-start.39
  283.6 15.1 %collective-permute-start.27 = (f32[4,128,128]{2,1,0:T(8,128)S(1)}, f32[4,128,128]{2,1,0:T(8,128)S(1)}, u32[]{:S(2)}, u32[]{:S(2)}) collective-permute-start(f32[4,128,128]{2,1,0:T(8,128)S(1)} %get-tuple-element.51), channel_id=1, source_target_pairs={{0,2},{1,3},{2,0},{3,1},{4,6},{5,7},{6,4},{7,5},{8,10},{9,11},{10,... | collective-permute-start | bytes 786440 | tf_op jit(solution)/shard_map/ppermute | solution.py:24
  298.8 6.0 %collective-permute-start.28 = (f32[4,128,128]{2,1,0:T(8,128)}, f32[4,128,128]{2,1,0:T(8,128)S(1)}, u32[]{:S(2)}, u32[]{:S(2)}) collective-permute-start(f32[4,128,128]{2,1,0:T(8,128)} %get-tuple-element.52), channel_id=1, source_target_pairs={{0,3},{1,2},{2,1},{3,0},{4,7},{5,6},{6,5},{7,4},{8,11},{9,10},{10,... | collective-permute-start | bytes 786440 | tf_op jit(solution)/shard_map/ppermute | solution.py:24
  304.8 4.1 %collective-permute-done.38.refs_6_ = f32[4,128,128]{2,1,0:T(8,128)S(1)} collective-permute-done((f32[4,128,128]{2,1,0:T(8,128)S(1)}, f32[4,128,128]{2,1,0:T(8,128)S(1)}, u32[]{:S(2)}, u32[]{:S(2)}) %collective-permute-start.38) | collective-permute-done | bytes 262176 | tf_op jit(solution)/shard_map/ppermute | solution.py:24
  308.9 12.6 %collective-permute-done.39.refs_7_ = f32[4,128,128]{2,1,0:T(8,128)S(1)} collective-permute-done((f32[4,128,128]{2,1,0:T(8,128)S(1)}, f32[4,128,128]{2,1,0:T(8,128)S(1)}, u32[]{:S(2)}, u32[]{:S(2)}) %collective-permute-start.39) | collective-permute-done | bytes 262176 | tf_op jit(solution)/shard_map/ppermute | solution.py:24
  322.3 3.3 shard_map.77.refs_8_
  325.6 15.8 %collective-permute-done.29.refs_4_ = f32[4,128,128]{2,1,0:T(8,128)S(1)} collective-permute-done((f32[4,128,128]{2,1,0:T(8,128)}, f32[4,128,128]{2,1,0:T(8,128)S(1)}, u32[]{:S(2)}, u32[]{:S(2)}) %collective-permute-start.29) | collective-permute-done | bytes 262176 | tf_op jit(solution)/shard_map/ppermute | solution.py:24
  341.4 5.6 %collective-permute-done.30.refs_5_ = f32[4,128,128]{2,1,0:T(8,128)S(1)} collective-permute-done((f32[4,128,128]{2,1,0:T(8,128)}, f32[4,128,128]{2,1,0:T(8,128)S(1)}, u32[]{:S(2)}, u32[]{:S(2)}) %collective-permute-start.30) | collective-permute-done | bytes 262176 | tf_op jit(solution)/shard_map/ppermute | solution.py:24
  347.0 6.8 %collective-permute-done.31.refs_6_ = f32[4,128,128]{2,1,0:T(8,128)S(1)} collective-permute-done((f32[4,128,128]{2,1,0:T(8,128)S(1)}, f32[4,128,128]{2,1,0:T(8,128)S(1)}, u32[]{:S(2)}, u32[]{:S(2)}) %collective-permute-start.31) | collective-permute-done | bytes 262176 | tf_op jit(solution)/shard_map/ppermute | solution.py:24
  353.8 6.2 %collective-permute-done.32.refs_7_ = f32[4,128,128]{2,1,0:T(8,128)S(1)} collective-permute-done((f32[4,128,128]{2,1,0:T(8,128)S(1)}, f32[4,128,128]{2,1,0:T(8,128)S(1)}, u32[]{:S(2)}, u32[]{:S(2)}) %collective-permute-start.32) | collective-permute-done | bytes 262176 | tf_op jit(solution)/shard_map/ppermute | solution.py:24
  360.7 3.3 shard_map.78
  (153 shorter events, 46.0 us)
Async XLA Ops:
  0.0 75.3 %collective-permute-start.5 = (f32[42,128,128]{2,1,0:T(8,128)}, f32[42,128,128]{2,1,0:T(8,128)}, u32[]{:S(2)}, u32[]{:S(2)}) collective-permute-start(f32[42,128,128]{2,1,0:T(8,128)} %bitcast.22), channel_id=1, source_target_pairs={{0,16},{8,24},{16,0},{24,8},{1,17},{9,25},{17,1},{25,9},{2,18},{10... | collective-permute-start | bytes 8257544 | tf_op jit(solution)/shard_map/ppermute | solution.py:24
  1.3 74.2 %collective-permute-start.4 = (f32[42,128,128]{2,1,0:T(8,128)}, f32[42,128,128]{2,1,0:T(8,128)S(1)}, u32[]{:S(2)}, u32[]{:S(2)}) collective-permute-start(f32[42,128,128]{2,1,0:T(8,128)} %bitcast.23), channel_id=1, source_target_pairs={{0,8},{8,0},{16,24},{24,16},{1,9},{9,1},{17,25},{25,17},{2,10},{10... | collective-permute-start | bytes 8257544 | tf_op jit(solution)/shard_map/ppermute | solution.py:24
  7.2 62.0 %collective-permute-start.11 = (f32[8,128,128]{2,1,0:T(8,128)}, f32[8,128,128]{2,1,0:T(8,128)}, u32[]{:S(2)}, u32[]{:S(2)}) collective-permute-start(f32[8,128,128]{2,1,0:T(8,128)} %get-tuple-element.42), channel_id=1, source_target_pairs={{0,2},{1,3},{2,0},{3,1},{4,6},{5,7},{6,4},{7,5},{8,10},{9,11},{10,... | collective-permute-start | bytes 1572872 | tf_op jit(solution)/shard_map/ppermute | solution.py:24
  7.4 65.4 %collective-permute-start.17 = (f32[8,128,128]{2,1,0:T(8,128)}, f32[8,128,128]{2,1,0:T(8,128)}, u32[]{:S(2)}, u32[]{:S(2)}) collective-permute-start(f32[8,128,128]{2,1,0:T(8,128)} %get-tuple-element.46), channel_id=1, source_target_pairs={{0,4},{1,5},{2,6},{3,7},{4,0},{5,1},{6,2},{7,3},{8,12},{9,13},{10,... | collective-permute-start | bytes 1572872 | tf_op jit(solution)/shard_map/ppermute | solution.py:24
  9.7 24.3 %collective-permute-start = (s32[2,32]{1,0:T(2,128)S(1)}, s32[2,32]{1,0:T(2,128)S(1)}, u32[]{:S(2)}, u32[]{:S(2)}) collective-permute-start(s32[2,32]{1,0:T(2,128)S(1)} %bitcast.29), channel_id=1, source_target_pairs={{0,7},{1,0},{2,1},{3,2},{4,3},{5,4},{6,5},{7,6},{8,15},{9,8},{10,9... | collective-permute-start | bytes 776 | tf_op jit(solution)/shard_map/ppermute | solution.py:24
  34.0 27.9 %collective-permute-start.1 = (s32[128]{0:T(128)S(1)}, s32[128]{0:T(128)S(1)}, u32[]{:S(2)}, u32[]{:S(2)}) collective-permute-start(s32[128]{0:T(128)S(1)} %pad_add_fusion.2), channel_id=1, source_target_pairs={{0,8},{8,0},{16,24},{24,16},{1,9},{9,1},{17,25},{25,17},{2,10},{10... | collective-permute-start | bytes 1544 | tf_op jit(solution)/shard_map/ppermute | solution.py:24
  68.0 37.4 %collective-permute-start.8 = (f32[8,128,128]{2,1,0:T(8,128)S(1)}, f32[8,128,128]{2,1,0:T(8,128)S(1)}, u32[]{:S(2)}, u32[]{:S(2)}) collective-permute-start(f32[8,128,128]{2,1,0:T(8,128)S(1)} %get-tuple-element.40), channel_id=1, source_target_pairs={{0,6},{1,7},{2,4},{3,5},{4,2},{5,3},{6,0},{7,1},{8,14},{9,15},{10,... | collective-permute-start | bytes 1572872 | tf_op jit(solution)/shard_map/ppermute | solution.py:24
  69.2 60.1 %collective-permute-start.9 = (f32[8,128,128]{2,1,0:T(8,128)S(1)}, f32[8,128,128]{2,1,0:T(8,128)}, u32[]{:S(2)}, u32[]{:S(2)}) collective-permute-start(f32[8,128,128]{2,1,0:T(8,128)S(1)} %get-tuple-element.41), channel_id=1, source_target_pairs={{0,7},{1,6},{2,5},{3,4},{4,3},{5,2},{6,1},{7,0},{8,15},{9,14},{10,... | collective-permute-start | bytes 1572872 | tf_op jit(solution)/shard_map/ppermute | solution.py:24
  72.8 57.0 %collective-permute-start.14 = (f32[8,128,128]{2,1,0:T(8,128)S(1)}, f32[8,128,128]{2,1,0:T(8,128)}, u32[]{:S(2)}, u32[]{:S(2)}) collective-permute-start(f32[8,128,128]{2,1,0:T(8,128)S(1)} %get-tuple-element.43), channel_id=1, source_target_pairs={{0,3},{1,2},{2,1},{3,0},{4,7},{5,6},{6,5},{7,4},{8,11},{9,10},{10,... | collective-permute-start | bytes 1572872 | tf_op jit(solution)/shard_map/ppermute | solution.py:24
  75.4 59.4 %collective-permute-start.16 = (f32[8,128,128]{2,1,0:T(8,128)S(1)}, f32[8,128,128]{2,1,0:T(8,128)}, u32[]{:S(2)}, u32[]{:S(2)}) collective-permute-start(f32[8,128,128]{2,1,0:T(8,128)S(1)} %get-tuple-element.45), channel_id=1, source_target_pairs={{0,1},{1,0},{2,3},{3,2},{4,5},{5,4},{6,7},{7,6},{8,9},{9,8},{10,11... | collective-permute-start | bytes 1572872 | tf_op jit(solution)/shard_map/ppermute | solution.py:24
  75.5 65.1 %collective-permute-start.18 = (f32[8,128,128]{2,1,0:T(8,128)S(1)}, f32[8,128,128]{2,1,0:T(8,128)}, u32[]{:S(2)}, u32[]{:S(2)}) collective-permute-start(f32[8,128,128]{2,1,0:T(8,128)S(1)} %get-tuple-element.47), channel_id=1, source_target_pairs={{0,5},{1,4},{2,7},{3,6},{4,1},{5,0},{6,3},{7,2},{8,13},{9,12},{10,... | collective-permute-start | bytes 1572872 | tf_op jit(solution)/shard_map/ppermute | solution.py:24
  105.4 54.7 %collective-permute-start.6 = (f32[21,128,128]{2,1,0:T(8,128)S(1)}, f32[21,128,128]{2,1,0:T(8,128)S(1)}, u32[]{:S(2)}, u32[]{:S(2)}) collective-permute-start(f32[21,128,128]{2,1,0:T(8,128)S(1)} %get-tuple-element.38), channel_id=1, source_target_pairs={{0,16},{8,24},{16,0},{24,8},{1,17},{9,25},{17,1},{25,9},{2,18},{10... | collective-permute-start | bytes 4128776 | tf_op jit(solution)/shard_map/ppermute | solution.py:24
  129.3 33.8 %collective-permute-start.7 = (f32[21,128,128]{2,1,0:T(8,128)S(1)}, f32[21,128,128]{2,1,0:T(8,128)S(1)}, u32[]{:S(2)}, u32[]{:S(2)}) collective-permute-start(f32[21,128,128]{2,1,0:T(8,128)S(1)} %get-tuple-element.39), channel_id=1, source_target_pairs={{0,8},{8,0},{16,24},{24,16},{1,9},{9,1},{17,25},{25,17},{2,10},{10... | collective-permute-start | bytes 4128776 | tf_op jit(solution)/shard_map/ppermute | solution.py:24
  129.8 14.0 %collective-permute-start.19 = (f32[8,128,128]{2,1,0:T(8,128)S(1)}, f32[8,128,128]{2,1,0:T(8,128)S(1)}, u32[]{:S(2)}, u32[]{:S(2)}) collective-permute-start(f32[8,128,128]{2,1,0:T(8,128)S(1)} %get-tuple-element.44.refs_0_.refs_1_), channel_id=1, source_target_pairs={{0,7},{1,0},{2,1},{3,2},{4,3},{5,4},{6,5},{7,6},{8,15},{9,8},{10,9... | collective-permute-start | bytes 1572872 | tf_op jit(solution)/shard_map/ppermute | solution.py:24
  152.5 84.1 %collective-permute-start.10 = (f32[8,128,128]{2,1,0:T(8,128)S(1)}, f32[8,128,128]{2,1,0:T(8,128)S(1)}, u32[]{:S(2)}, u32[]{:S(2)}) collective-permute-start(f32[8,128,128]{2,1,0:T(8,128)S(1)} %collective-permute-done.8.refs_1_), channel_id=1, source_target_pairs={{1,0},{2,1},{3,2},{5,4},{6,5},{7,6},{9,8},{10,9},{11,10},{13,12},{... | collective-permute-start | bytes 1572872 | tf_op jit(solution)/shard_map/ppermute | solution.py:24
  158.2 78.5 %collective-permute-start.13 = (f32[8,128,128]{2,1,0:T(8,128)}, f32[8,128,128]{2,1,0:T(8,128)S(1)}, u32[]{:S(2)}, u32[]{:S(2)}) collective-permute-start(f32[8,128,128]{2,1,0:T(8,128)} %collective-permute-done.9.refs_2_), channel_id=1, source_target_pairs={{1,0},{2,1},{3,2},{5,4},{6,5},{7,6},{9,8},{10,9},{11,10},{13,12},{... | collective-permute-start | bytes 1572872 | tf_op jit(solution)/shard_map/ppermute | solution.py:24
  160.0 57.5 %collective-permute-start.15 = (f32[8,128,128]{2,1,0:T(8,128)}, f32[8,128,128]{2,1,0:T(8,128)S(1)}, u32[]{:S(2)}, u32[]{:S(2)}) collective-permute-start(f32[8,128,128]{2,1,0:T(8,128)} %collective-permute-done.14.refs_3_.refs_4_), channel_id=1, source_target_pairs={{0,7},{1,0},{2,1},{3,2},{4,3},{5,4},{6,5},{7,6},{8,15},{9,8},{10,9... | collective-permute-start | bytes 1572872 | tf_op jit(solution)/shard_map/ppermute | solution.py:24
  160.1 57.4 %collective-permute-start.20 = (f32[8,128,128]{2,1,0:T(8,128)}, f32[8,128,128]{2,1,0:T(8,128)}, u32[]{:S(2)}, u32[]{:S(2)}) collective-permute-start(f32[8,128,128]{2,1,0:T(8,128)} %collective-permute-done.16.refs_1_.refs_2_), channel_id=1, source_target_pairs={{0,7},{1,0},{2,1},{3,2},{4,3},{5,4},{6,5},{7,6},{8,15},{9,8},{10,9... | collective-permute-start | bytes 1572872 | tf_op jit(solution)/shard_map/ppermute | solution.py:24
  163.2 54.3 %collective-permute-start.24 = (f32[8,128,128]{2,1,0:T(8,128)}, f32[8,128,128]{2,1,0:T(8,128)}, u32[]{:S(2)}, u32[]{:S(2)}) collective-permute-start(f32[8,128,128]{2,1,0:T(8,128)} %collective-permute-done.18.refs_5_.refs_6_), channel_id=1, source_target_pairs={{1,0},{2,1},{3,2},{5,4},{6,5},{7,6},{9,8},{10,9},{11,10},{13,12},{... | collective-permute-start | bytes 1572872 | tf_op jit(solution)/shard_map/ppermute | solution.py:24
  245.9 34.2 %collective-permute-start.33 = (f32[4,128,128]{2,1,0:T(8,128)S(1)}, f32[4,128,128]{2,1,0:T(8,128)S(1)}, u32[]{:S(2)}, u32[]{:S(2)}) collective-permute-start(f32[4,128,128]{2,1,0:T(8,128)S(1)} %get-tuple-element.58), channel_id=1, source_target_pairs={{0,1},{1,0},{2,3},{3,2},{4,5},{5,4},{6,7},{7,6},{8,9},{9,8},{10,11... | collective-permute-start | bytes 786440 | tf_op jit(solution)/shard_map/ppermute | solution.py:24
  266.4 17.2 %collective-permute-start.35 = (f32[4,128,128]{2,1,0:T(8,128)S(1)}, f32[4,128,128]{2,1,0:T(8,128)S(1)}, u32[]{:S(2)}, u32[]{:S(2)}) collective-permute-start(f32[4,128,128]{2,1,0:T(8,128)S(1)} %get-tuple-element.60), channel_id=1, source_target_pairs={{0,3},{1,2},{2,1},{3,0},{4,7},{5,6},{6,5},{7,4},{8,11},{9,10},{10,... | collective-permute-start | bytes 786440 | tf_op jit(solution)/shard_map/ppermute | solution.py:24
  268.0 15.6 %collective-permute-start.36 = (f32[4,128,128]{2,1,0:T(8,128)S(1)}, f32[4,128,128]{2,1,0:T(8,128)S(1)}, u32[]{:S(2)}, u32[]{:S(2)}) collective-permute-start(f32[4,128,128]{2,1,0:T(8,128)S(1)} %get-tuple-element.61), channel_id=1, source_target_pairs={{0,4},{1,5},{2,6},{3,7},{4,0},{5,1},{6,2},{7,3},{8,12},{9,13},{10,... | collective-permute-start | bytes 786440 | tf_op jit(solution)/shard_map/ppermute | solution.py:24
  268.1 30.7 %collective-permute-start.37 = (f32[4,128,128]{2,1,0:T(8,128)S(1)}, f32[4,128,128]{2,1,0:T(8,128)S(1)}, u32[]{:S(2)}, u32[]{:S(2)}) collective-permute-start(f32[4,128,128]{2,1,0:T(8,128)S(1)} %get-tuple-element.62), channel_id=1, source_target_pairs={{0,5},{1,4},{2,7},{3,6},{4,1},{5,0},{6,3},{7,2},{8,13},{9,12},{10,... | collective-permute-start | bytes 786440 | tf_op jit(solution)/shard_map/ppermute | solution.py:24
  280.1 28.7 %collective-permute-start.38 = (f32[4,128,128]{2,1,0:T(8,128)S(1)}, f32[4,128,128]{2,1,0:T(8,128)S(1)}, u32[]{:S(2)}, u32[]{:S(2)}) collective-permute-start(f32[4,128,128]{2,1,0:T(8,128)S(1)} %get-tuple-element.63), channel_id=1, source_target_pairs={{0,6},{1,7},{2,4},{3,5},{4,2},{5,3},{6,0},{7,1},{8,14},{9,15},{10,... | collective-permute-start | bytes 786440 | tf_op jit(solution)/shard_map/ppermute | solution.py:24
  280.2 41.3 %collective-permute-start.39 = (f32[4,128,128]{2,1,0:T(8,128)S(1)}, f32[4,128,128]{2,1,0:T(8,128)S(1)}, u32[]{:S(2)}, u32[]{:S(2)}) collective-permute-start(f32[4,128,128]{2,1,0:T(8,128)S(1)} %get-tuple-element.64), channel_id=1, source_target_pairs={{0,7},{1,6},{2,5},{3,4},{4,3},{5,2},{6,1},{7,0},{8,15},{9,14},{10,... | collective-permute-start | bytes 786440 | tf_op jit(solution)/shard_map/ppermute | solution.py:24
  283.6 37.9 %collective-permute-start.26 = (f32[4,128,128]{2,1,0:T(8,128)S(1)}, f32[4,128,128]{2,1,0:T(8,128)S(1)}, u32[]{:S(2)}, u32[]{:S(2)}) collective-permute-start(f32[4,128,128]{2,1,0:T(8,128)S(1)} %get-tuple-element.50), channel_id=1, source_target_pairs={{0,1},{1,0},{2,3},{3,2},{4,5},{5,4},{6,7},{7,6},{8,9},{9,8},{10,11... | collective-permute-start | bytes 786440 | tf_op jit(solution)/shard_map/ppermute | solution.py:24
  283.6 38.0 %collective-permute-start.27 = (f32[4,128,128]{2,1,0:T(8,128)S(1)}, f32[4,128,128]{2,1,0:T(8,128)S(1)}, u32[]{:S(2)}, u32[]{:S(2)}) collective-permute-start(f32[4,128,128]{2,1,0:T(8,128)S(1)} %get-tuple-element.51), channel_id=1, source_target_pairs={{0,2},{1,3},{2,0},{3,1},{4,6},{5,7},{6,4},{7,5},{8,10},{9,11},{10,... | collective-permute-start | bytes 786440 | tf_op jit(solution)/shard_map/ppermute | solution.py:24
  298.8 26.8 %collective-permute-start.28 = (f32[4,128,128]{2,1,0:T(8,128)}, f32[4,128,128]{2,1,0:T(8,128)S(1)}, u32[]{:S(2)}, u32[]{:S(2)}) collective-permute-start(f32[4,128,128]{2,1,0:T(8,128)} %get-tuple-element.52), channel_id=1, source_target_pairs={{0,3},{1,2},{2,1},{3,0},{4,7},{5,6},{6,5},{7,4},{8,11},{9,10},{10,... | collective-permute-start | bytes 786440 | tf_op jit(solution)/shard_map/ppermute | solution.py:24
  308.9 32.5 %collective-permute-start.29 = (f32[4,128,128]{2,1,0:T(8,128)}, f32[4,128,128]{2,1,0:T(8,128)S(1)}, u32[]{:S(2)}, u32[]{:S(2)}) collective-permute-start(f32[4,128,128]{2,1,0:T(8,128)} %get-tuple-element.53), channel_id=1, source_target_pairs={{0,4},{1,5},{2,6},{3,7},{4,0},{5,1},{6,2},{7,3},{8,12},{9,13},{10,... | collective-permute-start | bytes 786440 | tf_op jit(solution)/shard_map/ppermute | solution.py:24
  321.5 25.5 %collective-permute-start.30 = (f32[4,128,128]{2,1,0:T(8,128)}, f32[4,128,128]{2,1,0:T(8,128)S(1)}, u32[]{:S(2)}, u32[]{:S(2)}) collective-permute-start(f32[4,128,128]{2,1,0:T(8,128)} %get-tuple-element.54), channel_id=1, source_target_pairs={{0,5},{1,4},{2,7},{3,6},{4,1},{5,0},{6,3},{7,2},{8,13},{9,12},{10,... | collective-permute-start | bytes 786440 | tf_op jit(solution)/shard_map/ppermute | solution.py:24
  321.5 32.3 %collective-permute-start.31 = (f32[4,128,128]{2,1,0:T(8,128)S(1)}, f32[4,128,128]{2,1,0:T(8,128)S(1)}, u32[]{:S(2)}, u32[]{:S(2)}) collective-permute-start(f32[4,128,128]{2,1,0:T(8,128)S(1)} %get-tuple-element.55), channel_id=1, source_target_pairs={{0,6},{1,7},{2,4},{3,5},{4,2},{5,3},{6,0},{7,1},{8,14},{9,15},{10,... | collective-permute-start | bytes 786440 | tf_op jit(solution)/shard_map/ppermute | solution.py:24
  321.6 38.4 %collective-permute-start.32 = (f32[4,128,128]{2,1,0:T(8,128)S(1)}, f32[4,128,128]{2,1,0:T(8,128)S(1)}, u32[]{:S(2)}, u32[]{:S(2)}) collective-permute-start(f32[4,128,128]{2,1,0:T(8,128)S(1)} %get-tuple-element.56), channel_id=1, source_target_pairs={{0,7},{1,6},{2,5},{3,4},{4,3},{5,2},{6,1},{7,0},{8,15},{9,14},{10,... | collective-permute-start | bytes 786440 | tf_op jit(solution)/shard_map/ppermute | solution.py:24
  (50 other events, 1047.1 us)

commit v4 on v3

--- a/solution.py
+++ b/solution.py
@@ -9,7 +9,7 @@
 
 
 GROUP = 4
-UNROLL = 4
+UNROLL = 8
 SHIFT = 1024
 READ = 8
 ABSENT = -(1 << 24)
@@ -212,7 +212,7 @@
             pltpu.SemaphoreType.DMA((len(masks),)),
             pltpu.SemaphoreType.DMA((len(masks),)),
         ],
-        compiler_params=pltpu.CompilerParams(vmem_limit_bytes=48 * 1024 * 1024),
+        compiler_params=pltpu.CompilerParams(vmem_limit_bytes=62 * 1024 * 1024),
         name="take",
     )(place, left_list, left_own)
 
@@ -248,7 +248,7 @@
             pltpu.SemaphoreType.DMA((len(wanted),)),
             pltpu.SemaphoreType.DMA((len(wanted),)),
         ],
-        compiler_params=pltpu.CompilerParams(vmem_limit_bytes=48 * 1024 * 1024),
+        compiler_params=pltpu.CompilerParams(vmem_limit_bytes=62 * 1024 * 1024),
         name="parted",
     )(*[array for array, _, _ in wanted])
 
@@ -450,7 +450,7 @@
             pltpu.SemaphoreType.DMA((cols,)),
         ],
         cost_estimate=pl.CostEstimate(flops=0, bytes_accessed=4 * slots * size * size * 4, transcendentals=0),
-        compiler_params=pltpu.CompilerParams(vmem_limit_bytes=48 * 1024 * 1024),
+        compiler_params=pltpu.CompilerParams(vmem_limit_bytes=(48 if late else 62) * 1024 * 1024),
     )(place, *plan, *rights, *arrays)
 
 

time: 365 us -> 363 us (level)
  transfers between devices with their start and end apart: 40 -> 40, of which waited for: 16 -> 16; matrix products, arithmetic and copies ran while one was open for 0% -> 1% of each run, Pallas kernels for 24% -> 24%
where the time goes in v4:
time: 363 us; the launch traced here: 362 us
  waiting for transfers between devices  166 us (46%)
  Pallas kernels  99.4 us (27%)
  starting transfers between devices  90.4 us (25%)
  local copies, waits for them, and re-layouts  4.13 us (1%)
    ppermute x40, waiting for transfers between devices, moved(): lax.ppermute(value, axis, [(source, target(source)) for source in places])  166 us
    ppermute x40, starting transfers between devices, moved(): lax.ppermute(value, axis, [(source, target(source)) for source in places])  90.4 us
    pallas_call x4, Pallas kernels, multiplied(): pl.pallas_call(functools.partial(multiply_body, mode, part, [len(entry) -...  43.1 us
    pallas_call x1, Pallas kernels, make_plan(): pl.pallas_call(functools.partial(plan_body, sizes), out_shape=(jax.ShapeD...  29.1 us
    pallas_call x2, Pallas kernels, split(): pl.pallas_call(functools.partial(split_body, [base for _, base in pieces]...  9.34 us
    pallas_call x2, Pallas kernels, take(): pl.pallas_call(functools.partial(take_body, masks), out_shape=[jax.ShapeD...  8.33 us
  transfers between devices with their start and end apart: 40, of which 16 were waited for; matrix products, arithmetic and copies ran while one was open for 1% of the time, Pallas kernels for 24%

profile of v4, /device:TPU:11, one launch (start us, length us, event | category | flops | bytes accessed | tf_op | source)
XLA Modules:
  0.0 362.0 jit_solution(5636361515160049865)
XLA Ops:
  2.1 3.0 take.3
  9.8 22.2 %collective-permute-done.left_next_ref = s32[2,32]{1,0:T(2,128)S(1)} collective-permute-done((s32[2,32]{1,0:T(2,128)S(1)}, s32[2,32]{1,0:T(2,128)S(1)}, u32[]{:S(2)}, u32[]{:S(2)}) %collective-permute-start) | collective-permute-done | bytes 288 | tf_op jit(solution)/shard_map/ppermute | solution.py:24
  33.2 28.7 %collective-permute-done.1 = s32[128]{0:T(128)S(1)} collective-permute-done((s32[128]{0:T(128)S(1)}, s32[128]{0:T(128)S(1)}, u32[]{:S(2)}, u32[]{:S(2)}) %collective-permute-start.1) | collective-permute-done | bytes 544 | tf_op jit(solution)/shard_map/ppermute | solution.py:24
  64.6 5.3 %take.2 = (f32[8,128,128]{2,1,0:T(8,128)}, f32[8,128,128]{2,1,0:T(8,128)}, f32[8,128,128]{2,1,0:T(8,128)}, f32[8,128,128]{2,1,0:T(8,128)}, f32[8,128,128]{2,1,0:...) custom-call(s32[2]{0:T(128)} %pad_add_fusion.1.place_ref, s32[8,8]{1,0:T(8,128)} %bitcast.22, ...), custom_call_target="tpu_custom_call" | custom-call | tf_op jit(solution)/shard_map/take/pallas_call | solution.py:205
  71.1 3.5 collective-permute-start.9
  79.7 2.9 parted.1
  82.6 25.5 %collective-permute-done.8.refs_1_ = f32[8,128,128]{2,1,0:T(8,128)S(1)} collective-permute-done((f32[8,128,128]{2,1,0:T(8,128)}, f32[8,128,128]{2,1,0:T(8,128)S(1)}, u32[]{:S(2)}, u32[]{:S(2)}) %collective-permute-start.8) | collective-permute-done | bytes 524320 | tf_op jit(solution)/shard_map/ppermute | solution.py:24
  109.9 21.8 %collective-permute-done.9.refs_2_ = f32[8,128,128]{2,1,0:T(8,128)} collective-permute-done((f32[8,128,128]{2,1,0:T(8,128)}, f32[8,128,128]{2,1,0:T(8,128)}, u32[]{:S(2)}, u32[]{:S(2)}) %collective-permute-start.9) | collective-permute-done | bytes 524320 | tf_op jit(solution)/shard_map/ppermute | solution.py:24
  132.0 4.8 %collective-permute-start.19 = (f32[8,128,128]{2,1,0:T(8,128)}, f32[8,128,128]{2,1,0:T(8,128)S(1)}, u32[]{:S(2)}, u32[]{:S(2)}) collective-permute-start(f32[8,128,128]{2,1,0:T(8,128)} %get-tuple-element.44.refs_0_.refs_1_), channel_id=1, source_target_pairs={{0,7},{1,0},{2,1},{3,2},{4,3},{5,4},{6,5},{7,6},{8,15},{9,8},{10,9... | collective-permute-start | bytes 1572872 | tf_op jit(solution)/shard_map/ppermute | solution.py:24
  138.1 4.9 %collective-permute-done.18.refs_5_.refs_6_ = f32[8,128,128]{2,1,0:T(8,128)} collective-permute-done((f32[8,128,128]{2,1,0:T(8,128)}, f32[8,128,128]{2,1,0:T(8,128)}, u32[]{:S(2)}, u32[]{:S(2)}) %collective-permute-start.18) | collective-permute-done | bytes 524320 | tf_op jit(solution)/shard_map/ppermute | solution.py:24
  148.5 5.0 %collective-permute-done.23.refs_14_ = f32[8,128,128]{2,1,0:T(8,128)S(1)} collective-permute-done((f32[8,128,128]{2,1,0:T(8,128)}, f32[8,128,128]{2,1,0:T(8,128)S(1)}, u32[]{:S(2)}, u32[]{:S(2)}) %collective-permute-start.23) | collective-permute-done | bytes 524320 | tf_op jit(solution)/shard_map/ppermute | solution.py:24
  154.8 3.0 collective-permute-start.10
  164.9 2.8 collective-permute-start.24
  168.9 29.1 %plan.1 = (s32[2304]{0:T(1024)}, s32[5]{0:T(128)}, s32[128]{0:T(128)}) custom-call(s32[2]{0:T(128)} %pad_add_fusion.1.place_ref, s32[1536]{0:T(1024)} %add.26.triple_ref, s32[2,32]{1,0:T(2,128)} %bitcast.28, s32[2,32]{1,0:T(2,128)} %copy-done.32, s32[4,128]{1,0:T(4,128)} %pad_add_fusion.table_ref), custom_call_target="tpu_custom_call" | custom-call | flops 40000000 | bytes 60000000 | tf_op jit(solution)/shard_map/plan/pallas_call | solution.py:158
  198.0 6.5 %split.2.right_ref = bf16[126,128,256]{2,1,0:T(8,128)(2,1)} custom-call(f32[42,128,128]{2,1,0:T(8,128)} %bitcast.20, f32[42,128,128]{2,1,0:T(8,128)} %collective-permute-done.4.refs_1_.refs_0_, f32[42,128,128]{2,1,0:T(8,128)} %collective-permute-done.5.refs_2_.refs_1_), custom_call_target="tpu_custom_call" | custom-call | bytes 16515072 | tf_op jit(solution)/shard_map/split/pallas_call | solution.py:302
  204.6 10.4 %shard_map.73.refs_17_ = f32[64,128,128]{2,1,0:T(8,128)} custom-call(s32[2]{0:T(128)} %pad_add_fusion.1.place_ref, s32[2304]{0:T(1024)} %get-tuple-element.35.code_ref, s32[5]{0:T(128)} %get-tuple-element.36.bound_ref, s32[128]{0:T(128)} %get-tuple-element.37.block_ref, bf16[126,128,256]{2,1,0:T(8,128)(2,1)} %split.2.right_ref, ...), custom_call_target="tpu_custom_call" | custom-call | bytes 16777216 | tf_op jit(solution)/shard_map/pallas_call | solution.py:437
  215.0 2.8 split.3.refs_0_
  218.7 15.8 %shard_map.74.refs_7_ = f32[64,128,128]{2,1,0:T(8,128)} custom-call(s32[2]{0:T(128)} %pad_add_fusion.1.place_ref, s32[2304]{0:T(1024)} %get-tuple-element.35.code_ref, s32[5]{0:T(128)} %get-tuple-element.36.bound_ref, s32[128]{0:T(128)} %get-tuple-element.37.block_ref, bf16[126,128,256]{2,1,0:T(8,128)(2,1)} %split.2.right_ref, ...), custom_call_target="tpu_custom_call" | custom-call | bytes 16777216 | tf_op jit(solution)/shard_map/pallas_call | solution.py:437
  235.7 8.4 %shard_map.76 = (f32[4,128,128]{2,1,0:T(8,128)S(1)}, f32[4,128,128]{2,1,0:T(8,128)S(1)}, f32[4,128,128]{2,1,0:T(8,128)S(1)}, f32[4,128,128]{2,1,0:T(8,128)S(1)},...) custom-call(s32[2]{0:T(128)S(1)} %copy-done.7, ...), custom_call_target="tpu_custom_call" | custom-call | bytes 16777216 | tf_op jit(solution)/shard_map/pallas_call | solution.py:437
  244.8 20.2 %collective-permute-start.33 = (f32[4,128,128]{2,1,0:T(8,128)S(1)}, f32[4,128,128]{2,1,0:T(8,128)S(1)}, u32[]{:S(2)}, u32[]{:S(2)}) collective-permute-start(f32[4,128,128]{2,1,0:T(8,128)S(1)} %get-tuple-element.58), channel_id=1, source_target_pairs={{0,1},{1,0},{2,3},{3,2},{4,5},{5,4},{6,7},{7,6},{8,9},{9,8},{10,11... | collective-permute-start | bytes 786440 | tf_op jit(solution)/shard_map/ppermute | solution.py:24
  269.4 8.5 %shard_map.75 = (f32[4,128,128]{2,1,0:T(8,128)S(1)}, f32[4,128,128]{2,1,0:T(8,128)S(1)}, f32[4,128,128]{2,1,0:T(8,128)S(1)}, f32[4,128,128]{2,1,0:T(8,128)S(1)},...) custom-call(s32[2]{0:T(128)S(1)} %copy-done.7, ...), custom_call_target="tpu_custom_call" | custom-call | bytes 16777216 | tf_op jit(solution)/shard_map/pallas_call | solution.py:437
  278.7 3.6 collective-permute-start.39
  282.3 15.1 %collective-permute-start.27 = (f32[4,128,128]{2,1,0:T(8,128)S(1)}, f32[4,128,128]{2,1,0:T(8,128)S(1)}, u32[]{:S(2)}, u32[]{:S(2)}) collective-permute-start(f32[4,128,128]{2,1,0:T(8,128)S(1)} %get-tuple-element.51), channel_id=1, source_target_pairs={{0,2},{1,3},{2,0},{3,1},{4,6},{5,7},{6,4},{7,5},{8,10},{9,11},{10,... | collective-permute-start | bytes 786440 | tf_op jit(solution)/shard_map/ppermute | solution.py:24
  297.4 6.0 %collective-permute-start.28 = (f32[4,128,128]{2,1,0:T(8,128)S(1)}, f32[4,128,128]{2,1,0:T(8,128)S(1)}, u32[]{:S(2)}, u32[]{:S(2)}) collective-permute-start(f32[4,128,128]{2,1,0:T(8,128)S(1)} %get-tuple-element.52), channel_id=1, source_target_pairs={{0,3},{1,2},{2,1},{3,0},{4,7},{5,6},{6,5},{7,4},{8,11},{9,10},{10,... | collective-permute-start | bytes 786440 | tf_op jit(solution)/shard_map/ppermute | solution.py:24
  303.4 4.1 %collective-permute-done.38.refs_6_ = f32[4,128,128]{2,1,0:T(8,128)S(1)} collective-permute-done((f32[4,128,128]{2,1,0:T(8,128)S(1)}, f32[4,128,128]{2,1,0:T(8,128)S(1)}, u32[]{:S(2)}, u32[]{:S(2)}) %collective-permute-start.38) | collective-permute-done | bytes 262176 | tf_op jit(solution)/shard_map/ppermute | solution.py:24
  307.5 12.6 %collective-permute-done.39.refs_7_ = f32[4,128,128]{2,1,0:T(8,128)S(1)} collective-permute-done((f32[4,128,128]{2,1,0:T(8,128)S(1)}, f32[4,128,128]{2,1,0:T(8,128)S(1)}, u32[]{:S(2)}, u32[]{:S(2)}) %collective-permute-start.39) | collective-permute-done | bytes 262176 | tf_op jit(solution)/shard_map/ppermute | solution.py:24
  320.9 3.3 shard_map.77.refs_8_
  324.2 15.7 %collective-permute-done.29.refs_4_ = f32[4,128,128]{2,1,0:T(8,128)S(1)} collective-permute-done((f32[4,128,128]{2,1,0:T(8,128)S(1)}, f32[4,128,128]{2,1,0:T(8,128)S(1)}, u32[]{:S(2)}, u32[]{:S(2)}) %collective-permute-start.29) | collective-permute-done | bytes 262176 | tf_op jit(solution)/shard_map/ppermute | solution.py:24
  339.9 5.6 %collective-permute-done.30.refs_5_ = f32[4,128,128]{2,1,0:T(8,128)} collective-permute-done((f32[4,128,128]{2,1,0:T(8,128)S(1)}, f32[4,128,128]{2,1,0:T(8,128)}, u32[]{:S(2)}, u32[]{:S(2)}) %collective-permute-start.30) | collective-permute-done | bytes 262176 | tf_op jit(solution)/shard_map/ppermute | solution.py:24
  345.5 7.0 %collective-permute-done.31.refs_6_ = f32[4,128,128]{2,1,0:T(8,128)} collective-permute-done((f32[4,128,128]{2,1,0:T(8,128)S(1)}, f32[4,128,128]{2,1,0:T(8,128)}, u32[]{:S(2)}, u32[]{:S(2)}) %collective-permute-start.31) | collective-permute-done | bytes 262176 | tf_op jit(solution)/shard_map/ppermute | solution.py:24
  352.5 6.2 %collective-permute-done.32.refs_7_ = f32[4,128,128]{2,1,0:T(8,128)} collective-permute-done((f32[4,128,128]{2,1,0:T(8,128)S(1)}, f32[4,128,128]{2,1,0:T(8,128)}, u32[]{:S(2)}, u32[]{:S(2)}) %collective-permute-start.32) | collective-permute-done | bytes 262176 | tf_op jit(solution)/shard_map/ppermute | solution.py:24
  358.7 3.3 shard_map.78
  (135 shorter events, 43.9 us)
Async XLA Ops:
  0.0 77.2 %collective-permute-start.5 = (f32[42,128,128]{2,1,0:T(8,128)}, f32[42,128,128]{2,1,0:T(8,128)}, u32[]{:S(2)}, u32[]{:S(2)}) collective-permute-start(f32[42,128,128]{2,1,0:T(8,128)} %bitcast.18), channel_id=1, source_target_pairs={{0,16},{8,24},{16,0},{24,8},{1,17},{9,25},{17,1},{25,9},{2,18},{10... | collective-permute-start | bytes 8257544 | tf_op jit(solution)/shard_map/ppermute | solution.py:24
  1.3 76.1 %collective-permute-start.4 = (f32[42,128,128]{2,1,0:T(8,128)}, f32[42,128,128]{2,1,0:T(8,128)}, u32[]{:S(2)}, u32[]{:S(2)}) collective-permute-start(f32[42,128,128]{2,1,0:T(8,128)} %bitcast.19), channel_id=1, source_target_pairs={{0,8},{8,0},{16,24},{24,16},{1,9},{9,1},{17,25},{25,17},{2,10},{10... | collective-permute-start | bytes 8257544 | tf_op jit(solution)/shard_map/ppermute | solution.py:24
  5.2 65.9 %collective-permute-start.11 = (f32[8,128,128]{2,1,0:T(8,128)}, f32[8,128,128]{2,1,0:T(8,128)S(1)}, u32[]{:S(2)}, u32[]{:S(2)}) collective-permute-start(f32[8,128,128]{2,1,0:T(8,128)} %get-tuple-element.42), channel_id=1, source_target_pairs={{0,2},{1,3},{2,0},{3,1},{4,6},{5,7},{6,4},{7,5},{8,10},{9,11},{10,... | collective-permute-start | bytes 1572872 | tf_op jit(solution)/shard_map/ppermute | solution.py:24
  5.5 69.1 %collective-permute-start.17 = (f32[8,128,128]{2,1,0:T(8,128)}, f32[8,128,128]{2,1,0:T(8,128)S(1)}, u32[]{:S(2)}, u32[]{:S(2)}) collective-permute-start(f32[8,128,128]{2,1,0:T(8,128)} %get-tuple-element.46), channel_id=1, source_target_pairs={{0,4},{1,5},{2,6},{3,7},{4,0},{5,1},{6,2},{7,3},{8,12},{9,13},{10,... | collective-permute-start | bytes 1572872 | tf_op jit(solution)/shard_map/ppermute | solution.py:24
  7.8 24.2 %collective-permute-start = (s32[2,32]{1,0:T(2,128)S(1)}, s32[2,32]{1,0:T(2,128)S(1)}, u32[]{:S(2)}, u32[]{:S(2)}) collective-permute-start(s32[2,32]{1,0:T(2,128)S(1)} %bitcast.29), channel_id=1, source_target_pairs={{0,7},{1,0},{2,1},{3,2},{4,3},{5,4},{6,5},{7,6},{8,15},{9,8},{10,9... | collective-permute-start | bytes 776 | tf_op jit(solution)/shard_map/ppermute | solution.py:24
  32.0 29.9 %collective-permute-start.1 = (s32[128]{0:T(128)S(1)}, s32[128]{0:T(128)S(1)}, u32[]{:S(2)}, u32[]{:S(2)}) collective-permute-start(s32[128]{0:T(128)S(1)} %pad_add_fusion.2), channel_id=1, source_target_pairs={{0,8},{8,0},{16,24},{24,16},{1,9},{9,1},{17,25},{25,17},{2,10},{10... | collective-permute-start | bytes 1544 | tf_op jit(solution)/shard_map/ppermute | solution.py:24
  69.9 38.2 %collective-permute-start.8 = (f32[8,128,128]{2,1,0:T(8,128)}, f32[8,128,128]{2,1,0:T(8,128)S(1)}, u32[]{:S(2)}, u32[]{:S(2)}) collective-permute-start(f32[8,128,128]{2,1,0:T(8,128)} %get-tuple-element.40), channel_id=1, source_target_pairs={{0,6},{1,7},{2,4},{3,5},{4,2},{5,3},{6,0},{7,1},{8,14},{9,15},{10,... | collective-permute-start | bytes 1572872 | tf_op jit(solution)/shard_map/ppermute | solution.py:24
  71.1 60.6 %collective-permute-start.9 = (f32[8,128,128]{2,1,0:T(8,128)}, f32[8,128,128]{2,1,0:T(8,128)}, u32[]{:S(2)}, u32[]{:S(2)}) collective-permute-start(f32[8,128,128]{2,1,0:T(8,128)} %get-tuple-element.41), channel_id=1, source_target_pairs={{0,7},{1,6},{2,5},{3,4},{4,3},{5,2},{6,1},{7,0},{8,15},{9,14},{10,... | collective-permute-start | bytes 1572872 | tf_op jit(solution)/shard_map/ppermute | solution.py:24
  74.6 57.4 %collective-permute-start.14 = (f32[8,128,128]{2,1,0:T(8,128)}, f32[8,128,128]{2,1,0:T(8,128)}, u32[]{:S(2)}, u32[]{:S(2)}) collective-permute-start(f32[8,128,128]{2,1,0:T(8,128)} %get-tuple-element.43), channel_id=1, source_target_pairs={{0,3},{1,2},{2,1},{3,0},{4,7},{5,6},{6,5},{7,4},{8,11},{9,10},{10,... | collective-permute-start | bytes 1572872 | tf_op jit(solution)/shard_map/ppermute | solution.py:24
  77.2 59.6 %collective-permute-start.16 = (f32[8,128,128]{2,1,0:T(8,128)}, f32[8,128,128]{2,1,0:T(8,128)}, u32[]{:S(2)}, u32[]{:S(2)}) collective-permute-start(f32[8,128,128]{2,1,0:T(8,128)} %get-tuple-element.45), channel_id=1, source_target_pairs={{0,1},{1,0},{2,3},{3,2},{4,5},{5,4},{6,7},{7,6},{8,9},{9,8},{10,11... | collective-permute-start | bytes 1572872 | tf_op jit(solution)/shard_map/ppermute | solution.py:24
  77.4 65.6 %collective-permute-start.18 = (f32[8,128,128]{2,1,0:T(8,128)}, f32[8,128,128]{2,1,0:T(8,128)}, u32[]{:S(2)}, u32[]{:S(2)}) collective-permute-start(f32[8,128,128]{2,1,0:T(8,128)} %get-tuple-element.47), channel_id=1, source_target_pairs={{0,5},{1,4},{2,7},{3,6},{4,1},{5,0},{6,3},{7,2},{8,13},{9,12},{10,... | collective-permute-start | bytes 1572872 | tf_op jit(solution)/shard_map/ppermute | solution.py:24
  108.1 54.7 %collective-permute-start.6 = (f32[21,128,128]{2,1,0:T(8,128)}, f32[21,128,128]{2,1,0:T(8,128)}, u32[]{:S(2)}, u32[]{:S(2)}) collective-permute-start(f32[21,128,128]{2,1,0:T(8,128)} %get-tuple-element.38), channel_id=1, source_target_pairs={{0,16},{8,24},{16,0},{24,8},{1,17},{9,25},{17,1},{25,9},{2,18},{10... | collective-permute-start | bytes 4128776 | tf_op jit(solution)/shard_map/ppermute | solution.py:24
  131.7 33.2 %collective-permute-start.7 = (f32[21,128,128]{2,1,0:T(8,128)}, f32[21,128,128]{2,1,0:T(8,128)}, u32[]{:S(2)}, u32[]{:S(2)}) collective-permute-start(f32[21,128,128]{2,1,0:T(8,128)} %get-tuple-element.39), channel_id=1, source_target_pairs={{0,8},{8,0},{16,24},{24,16},{1,9},{9,1},{17,25},{25,17},{2,10},{10... | collective-permute-start | bytes 4128776 | tf_op jit(solution)/shard_map/ppermute | solution.py:24
  132.0 14.0 %collective-permute-start.19 = (f32[8,128,128]{2,1,0:T(8,128)}, f32[8,128,128]{2,1,0:T(8,128)S(1)}, u32[]{:S(2)}, u32[]{:S(2)}) collective-permute-start(f32[8,128,128]{2,1,0:T(8,128)} %get-tuple-element.44.refs_0_.refs_1_), channel_id=1, source_target_pairs={{0,7},{1,0},{2,1},{3,2},{4,3},{5,4},{6,5},{7,6},{8,15},{9,8},{10,9... | collective-permute-start | bytes 1572872 | tf_op jit(solution)/shard_map/ppermute | solution.py:24
  154.8 79.7 %collective-permute-start.10 = (f32[8,128,128]{2,1,0:T(8,128)S(1)}, f32[8,128,128]{2,1,0:T(8,128)}, u32[]{:S(2)}, u32[]{:S(2)}) collective-permute-start(f32[8,128,128]{2,1,0:T(8,128)S(1)} %collective-permute-done.8.refs_1_), channel_id=1, source_target_pairs={{1,0},{2,1},{3,2},{5,4},{6,5},{7,6},{9,8},{10,9},{11,10},{13,12},{... | collective-permute-start | bytes 1572872 | tf_op jit(solution)/shard_map/ppermute | solution.py:24
  160.2 74.4 %collective-permute-start.13 = (f32[8,128,128]{2,1,0:T(8,128)}, f32[8,128,128]{2,1,0:T(8,128)}, u32[]{:S(2)}, u32[]{:S(2)}) collective-permute-start(f32[8,128,128]{2,1,0:T(8,128)} %collective-permute-done.9.refs_2_), channel_id=1, source_target_pairs={{1,0},{2,1},{3,2},{5,4},{6,5},{7,6},{9,8},{10,9},{11,10},{13,12},{... | collective-permute-start | bytes 1572872 | tf_op jit(solution)/shard_map/ppermute | solution.py:24
  162.7 55.2 %collective-permute-start.15 = (f32[8,128,128]{2,1,0:T(8,128)}, f32[8,128,128]{2,1,0:T(8,128)S(1)}, u32[]{:S(2)}, u32[]{:S(2)}) collective-permute-start(f32[8,128,128]{2,1,0:T(8,128)} %collective-permute-done.14.refs_3_.refs_4_), channel_id=1, source_target_pairs={{0,7},{1,0},{2,1},{3,2},{4,3},{5,4},{6,5},{7,6},{8,15},{9,8},{10,9... | collective-permute-start | bytes 1572872 | tf_op jit(solution)/shard_map/ppermute | solution.py:24
  162.8 55.2 %collective-permute-start.20 = (f32[8,128,128]{2,1,0:T(8,128)}, f32[8,128,128]{2,1,0:T(8,128)}, u32[]{:S(2)}, u32[]{:S(2)}) collective-permute-start(f32[8,128,128]{2,1,0:T(8,128)} %collective-permute-done.16.refs_1_.refs_2_), channel_id=1, source_target_pairs={{0,7},{1,0},{2,1},{3,2},{4,3},{5,4},{6,5},{7,6},{8,15},{9,8},{10,9... | collective-permute-start | bytes 1572872 | tf_op jit(solution)/shard_map/ppermute | solution.py:24
  164.9 53.1 %collective-permute-start.24 = (f32[8,128,128]{2,1,0:T(8,128)}, f32[8,128,128]{2,1,0:T(8,128)}, u32[]{:S(2)}, u32[]{:S(2)}) collective-permute-start(f32[8,128,128]{2,1,0:T(8,128)} %collective-permute-done.18.refs_5_.refs_6_), channel_id=1, source_target_pairs={{1,0},{2,1},{3,2},{5,4},{6,5},{7,6},{9,8},{10,9},{11,10},{13,12},{... | collective-permute-start | bytes 1572872 | tf_op jit(solution)/shard_map/ppermute | solution.py:24
  244.8 33.8 %collective-permute-start.33 = (f32[4,128,128]{2,1,0:T(8,128)S(1)}, f32[4,128,128]{2,1,0:T(8,128)S(1)}, u32[]{:S(2)}, u32[]{:S(2)}) collective-permute-start(f32[4,128,128]{2,1,0:T(8,128)S(1)} %get-tuple-element.58), channel_id=1, source_target_pairs={{0,1},{1,0},{2,3},{3,2},{4,5},{5,4},{6,7},{7,6},{8,9},{9,8},{10,11... | collective-permute-start | bytes 786440 | tf_op jit(solution)/shard_map/ppermute | solution.py:24
  265.0 17.2 %collective-permute-start.35 = (f32[4,128,128]{2,1,0:T(8,128)S(1)}, f32[4,128,128]{2,1,0:T(8,128)S(1)}, u32[]{:S(2)}, u32[]{:S(2)}) collective-permute-start(f32[4,128,128]{2,1,0:T(8,128)S(1)} %get-tuple-element.60), channel_id=1, source_target_pairs={{0,3},{1,2},{2,1},{3,0},{4,7},{5,6},{6,5},{7,4},{8,11},{9,10},{10,... | collective-permute-start | bytes 786440 | tf_op jit(solution)/shard_map/ppermute | solution.py:24
  266.7 15.6 %collective-permute-start.36 = (f32[4,128,128]{2,1,0:T(8,128)S(1)}, f32[4,128,128]{2,1,0:T(8,128)S(1)}, u32[]{:S(2)}, u32[]{:S(2)}) collective-permute-start(f32[4,128,128]{2,1,0:T(8,128)S(1)} %get-tuple-element.61), channel_id=1, source_target_pairs={{0,4},{1,5},{2,6},{3,7},{4,0},{5,1},{6,2},{7,3},{8,12},{9,13},{10,... | collective-permute-start | bytes 786440 | tf_op jit(solution)/shard_map/ppermute | solution.py:24
  266.7 30.7 %collective-permute-start.37 = (f32[4,128,128]{2,1,0:T(8,128)S(1)}, f32[4,128,128]{2,1,0:T(8,128)S(1)}, u32[]{:S(2)}, u32[]{:S(2)}) collective-permute-start(f32[4,128,128]{2,1,0:T(8,128)S(1)} %get-tuple-element.62), channel_id=1, source_target_pairs={{0,5},{1,4},{2,7},{3,6},{4,1},{5,0},{6,3},{7,2},{8,13},{9,12},{10,... | collective-permute-start | bytes 786440 | tf_op jit(solution)/shard_map/ppermute | solution.py:24
  278.6 28.9 %collective-permute-start.38 = (f32[4,128,128]{2,1,0:T(8,128)S(1)}, f32[4,128,128]{2,1,0:T(8,128)S(1)}, u32[]{:S(2)}, u32[]{:S(2)}) collective-permute-start(f32[4,128,128]{2,1,0:T(8,128)S(1)} %get-tuple-element.63), channel_id=1, source_target_pairs={{0,6},{1,7},{2,4},{3,5},{4,2},{5,3},{6,0},{7,1},{8,14},{9,15},{10,... | collective-permute-start | bytes 786440 | tf_op jit(solution)/shard_map/ppermute | solution.py:24
  278.7 41.5 %collective-permute-start.39 = (f32[4,128,128]{2,1,0:T(8,128)S(1)}, f32[4,128,128]{2,1,0:T(8,128)S(1)}, u32[]{:S(2)}, u32[]{:S(2)}) collective-permute-start(f32[4,128,128]{2,1,0:T(8,128)S(1)} %get-tuple-element.64), channel_id=1, source_target_pairs={{0,7},{1,6},{2,5},{3,4},{4,3},{5,2},{6,1},{7,0},{8,15},{9,14},{10,... | collective-permute-start | bytes 786440 | tf_op jit(solution)/shard_map/ppermute | solution.py:24
  282.2 37.9 %collective-permute-start.26 = (f32[4,128,128]{2,1,0:T(8,128)S(1)}, f32[4,128,128]{2,1,0:T(8,128)S(1)}, u32[]{:S(2)}, u32[]{:S(2)}) collective-permute-start(f32[4,128,128]{2,1,0:T(8,128)S(1)} %get-tuple-element.50), channel_id=1, source_target_pairs={{0,1},{1,0},{2,3},{3,2},{4,5},{5,4},{6,7},{7,6},{8,9},{9,8},{10,11... | collective-permute-start | bytes 786440 | tf_op jit(solution)/shard_map/ppermute | solution.py:24
  282.3 38.0 %collective-permute-start.27 = (f32[4,128,128]{2,1,0:T(8,128)S(1)}, f32[4,128,128]{2,1,0:T(8,128)S(1)}, u32[]{:S(2)}, u32[]{:S(2)}) collective-permute-start(f32[4,128,128]{2,1,0:T(8,128)S(1)} %get-tuple-element.51), channel_id=1, source_target_pairs={{0,2},{1,3},{2,0},{3,1},{4,6},{5,7},{6,4},{7,5},{8,10},{9,11},{10,... | collective-permute-start | bytes 786440 | tf_op jit(solution)/shard_map/ppermute | solution.py:24
  297.4 26.8 %collective-permute-start.28 = (f32[4,128,128]{2,1,0:T(8,128)S(1)}, f32[4,128,128]{2,1,0:T(8,128)S(1)}, u32[]{:S(2)}, u32[]{:S(2)}) collective-permute-start(f32[4,128,128]{2,1,0:T(8,128)S(1)} %get-tuple-element.52), channel_id=1, source_target_pairs={{0,3},{1,2},{2,1},{3,0},{4,7},{5,6},{6,5},{7,4},{8,11},{9,10},{10,... | collective-permute-start | bytes 786440 | tf_op jit(solution)/shard_map/ppermute | solution.py:24
  307.5 32.4 %collective-permute-start.29 = (f32[4,128,128]{2,1,0:T(8,128)S(1)}, f32[4,128,128]{2,1,0:T(8,128)S(1)}, u32[]{:S(2)}, u32[]{:S(2)}) collective-permute-start(f32[4,128,128]{2,1,0:T(8,128)S(1)} %get-tuple-element.53), channel_id=1, source_target_pairs={{0,4},{1,5},{2,6},{3,7},{4,0},{5,1},{6,2},{7,3},{8,12},{9,13},{10,... | collective-permute-start | bytes 786440 | tf_op jit(solution)/shard_map/ppermute | solution.py:24
  320.1 25.4 %collective-permute-start.30 = (f32[4,128,128]{2,1,0:T(8,128)S(1)}, f32[4,128,128]{2,1,0:T(8,128)}, u32[]{:S(2)}, u32[]{:S(2)}) collective-permute-start(f32[4,128,128]{2,1,0:T(8,128)S(1)} %get-tuple-element.54), channel_id=1, source_target_pairs={{0,5},{1,4},{2,7},{3,6},{4,1},{5,0},{6,3},{7,2},{8,13},{9,12},{10,... | collective-permute-start | bytes 786440 | tf_op jit(solution)/shard_map/ppermute | solution.py:24
  320.2 32.4 %collective-permute-start.31 = (f32[4,128,128]{2,1,0:T(8,128)S(1)}, f32[4,128,128]{2,1,0:T(8,128)}, u32[]{:S(2)}, u32[]{:S(2)}) collective-permute-start(f32[4,128,128]{2,1,0:T(8,128)S(1)} %get-tuple-element.55), channel_id=1, source_target_pairs={{0,6},{1,7},{2,4},{3,5},{4,2},{5,3},{6,0},{7,1},{8,14},{9,15},{10,... | collective-permute-start | bytes 786440 | tf_op jit(solution)/shard_map/ppermute | solution.py:24
  320.3 38.5 %collective-permute-start.32 = (f32[4,128,128]{2,1,0:T(8,128)S(1)}, f32[4,128,128]{2,1,0:T(8,128)}, u32[]{:S(2)}, u32[]{:S(2)}) collective-permute-start(f32[4,128,128]{2,1,0:T(8,128)S(1)} %get-tuple-element.56), channel_id=1, source_target_pairs={{0,7},{1,6},{2,5},{3,4},{4,3},{5,2},{6,1},{7,0},{8,15},{9,14},{10,... | collective-permute-start | bytes 786440 | tf_op jit(solution)/shard_map/ppermute | solution.py:24
  (41 other events, 950.7 us)
